TPU v7x, 32 devices: a whole 2x2x4 slice. The times are simulated.
32 devices in a mesh: dp: 8 (over y, x, core), tensor: 4 (over z).
Axes of the slice: x: 2, y: 2, z: 4, core: 2. Of those that a mesh axis runs over, the one named last changes fastest.
Arguments:
- layer_in: bfloat16 [64, 128, 1024], P('dp', 'tensor'), may hold values from -6 to 6
- cotangent: bfloat16 [64, 128, 1024], P('dp', 'tensor'), may hold values from -8 to 8
- row_counts: int32 [16], replicated, may hold values from 1 to 8, 64 in all
- tail_tokens: int32 [16], replicated, may hold values from 1 to 128
- row_order: int32 [64], replicated, may hold values from 0 to 63, each once
- gain_one: bfloat16 [1024], P('dp'), may hold values from 0.099609375 to 1.8984375
- w_in: bfloat16 [1024, 3, 1024], P('dp', None, 'tensor'), may hold values from -0.1875 to 0.1875
- kernel: bfloat16 [3, 1024], P(None, 'dp'), may hold values from -3.5 to 3.5
- w_out: bfloat16 [1024, 1024], P('tensor', 'dp'), may hold values from -0.1875 to 0.1875
- gain_two: bfloat16 [1024], P('dp'), may hold values from 0.099609375 to 1.8984375
- w_gu: bfloat16 [1024, 2, 4608], P('dp', None, 'tensor'), may hold values from -0.1875 to 0.1875
- w_down: bfloat16 [4608, 1024], P('tensor', 'dp'), may hold values from -0.125 to 0.125
Outputs:
- layer_out: bfloat16 [64, 128, 1024], P('dp', 'tensor')
- grad_in: bfloat16 [64, 128, 1024], P('dp', 'tensor')
- grad_gain_one: float32 [1024], P('dp')
- grad_w_in: float32 [1024, 3, 1024], P('dp', None, 'tensor')
- grad_kernel: float32 [3, 1024], P(None, 'dp')
- grad_w_out: float32 [1024, 1024], P('tensor', 'dp')
- grad_gain_two: float32 [1024], P('dp')
- grad_w_gu: float32 [1024, 2, 4608], P('dp', None, 'tensor')
- grad_w_down: float32 [4608, 1024], P('tensor', 'dp')
Inputs may be any that keep to these rules, and one draw needn't show every extreme that they name: row_counts sum to 64; the longest sequence has exactly 8 rows. `row_order`: each given-order row stands in exactly one dealt slot.
All inputs are finite; a program needn't handle non-finite values.
Results may differ from a plain program's by a relative error of at most 0.025.
Values may be sent and summed in bfloat16 or wider, within the bound.
No kernel may reach another device: no remote copies, remote signals or barrier semaphores. Data moves between devices by JAX's collectives and lax.ppermute only.
A program may use at most 128 MiB of HBM per device.

v0:
```python
import jax
import jax.numpy as jnp
from jax import lax
from jax.sharding import PartitionSpec as P

EPS = 1e-05


def gather_rows(value):
    return lax.all_gather(value, "tensor", axis=1, tiled=True)


def reduce_rows(value):
    return lax.psum_scatter(
        value.astype(jnp.bfloat16), "tensor", scatter_dimension=1, tiled=True
    ).astype(jnp.float32)


def mixer_weights(w_in, w_out, kernel, gain_one):
    return (
        lax.all_gather(w_in, "dp", axis=0, tiled=True),
        lax.all_gather(w_out, "dp", axis=1, tiled=True),
        lax.all_gather(kernel, "dp", axis=1, tiled=True),
        lax.all_gather(gain_one, "dp", axis=0, tiled=True),
    )


def ffn_weights(w_gu, w_down, gain_two):
    return (
        lax.all_gather(w_gu, "dp", axis=0, tiled=True),
        lax.all_gather(w_down, "dp", axis=1, tiled=True),
        lax.all_gather(gain_two, "dp", axis=0, tiled=True),
    )


def norm_scale(value):
    return lax.rsqrt(jnp.mean(value * value, axis=2, keepdims=True) + EPS)


def norm_back(d_normed, value, scale, gain):
    weighted = d_normed * gain
    d_value = scale * weighted - value * (scale * scale * scale) * jnp.mean(
        weighted * value, axis=2, keepdims=True
    )
    d_gain = jnp.sum(d_normed * value * scale, axis=(0, 1))
    return (d_value, d_gain)


def body(
    layer_in,
    cotangent,
    row_counts,
    tail_tokens,
    row_order,
    gain_one,
    w_in,
    kernel,
    w_out,
    gain_two,
    w_gu,
    w_down,
):
    row_count, own_len, feature_dim = layer_in.shape
    tensor_rank = lax.axis_index("tensor")
    row_len = own_len * lax.axis_size("tensor")
    channels = w_in.shape[2]
    total_rows = row_order.shape[0]
    reach = kernel.shape[0] - 1
    given = lax.dynamic_slice_in_dim(row_order, lax.axis_index("dp") * row_count, row_count)
    starts = jnp.cumsum(row_counts) - row_counts
    ends = starts + row_counts - 1
    is_first = jnp.any(starts[None, :] == given[:, None], axis=1)
    at_end = ends[None, :] == given[:, None]
    row_valid = jnp.where(
        jnp.any(at_end, axis=1),
        jnp.sum(jnp.where(at_end, tail_tokens[None, :], 0), axis=1),
        row_len,
    )
    positions = tensor_rank * own_len + jnp.arange(own_len, dtype=jnp.int32)
    valid = (positions[None, :] < row_valid[:, None]).astype(jnp.float32)
    before_mask = jnp.logical_and(
        row_order[None, :] == (given - 1)[:, None], jnp.logical_not(is_first)[:, None]
    )
    before_low = before_mask.astype(jnp.bfloat16)
    mixer_set = mixer_weights(w_in, w_out, kernel, gain_one)
    w_in_all, w_out_all, kernel_all, gain_one_all = mixer_set
    x_own = layer_in.astype(jnp.float32)
    scale_one = norm_scale(x_own)
    normed_one = gather_rows(
        (x_own * scale_one * gain_one_all.astype(jnp.float32)).astype(jnp.bfloat16)
    )
    projected = jnp.einsum(
        "rtd,dkc->rtkc", normed_one, w_in_all, preferred_element_type=jnp.float32
    )
    b_stream = projected[:, :, 0]
    c_stream = projected[:, :, 1]
    u_stream = projected[:, :, 2]
    mixed_in = (b_stream * u_stream).astype(jnp.bfloat16)
    tails = lax.all_gather(mixed_in[:, row_len - reach :], "dp", axis=0, tiled=True)
    prior = jnp.dot(
        before_low, tails.reshape(total_rows, reach * channels), preferred_element_type=jnp.float32
    )
    prior = prior.reshape(row_count, reach, channels)
    padded = jnp.concatenate([prior, mixed_in.astype(jnp.float32)], axis=1)
    conv_taps = lax.dynamic_slice_in_dim(kernel_all, tensor_rank * channels, channels, 1).astype(
        jnp.float32
    )
    conv_out = jnp.zeros((row_count, row_len, channels), jnp.float32)
    for offset in range(reach + 1):
        conv_out = conv_out + conv_taps[offset] * padded[:, offset : offset + row_len]
    gated = (c_stream * conv_out).astype(jnp.bfloat16)
    mixer_part = jnp.einsum("rtc,ce->rte", gated, w_out_all, preferred_element_type=jnp.float32)
    middle = x_own + reduce_rows(mixer_part)
    ffn_set = ffn_weights(w_gu, w_down, gain_two)
    w_gu_all, w_down_all, gain_two_all = ffn_set
    scale_two = norm_scale(middle)
    normed_two = gather_rows(
        (middle * scale_two * gain_two_all.astype(jnp.float32)).astype(jnp.bfloat16)
    )
    gate_up = jnp.einsum("rtd,dkf->rtkf", normed_two, w_gu_all, preferred_element_type=jnp.float32)
    gate_act = gate_up[:, :, 0]
    up_act = gate_up[:, :, 1]
    sigmoid_gate = jax.nn.sigmoid(gate_act)
    silu_gate = gate_act * sigmoid_gate
    hidden = (silu_gate * up_act).astype(jnp.bfloat16)
    ffn_part = jnp.einsum("rtf,fe->rte", hidden, w_down_all, preferred_element_type=jnp.float32)
    result = middle + reduce_rows(ffn_part)
    layer_out = result.astype(jnp.bfloat16)
    d_result = cotangent.astype(jnp.float32) * valid[:, :, None]
    d_ffn = gather_rows(d_result.astype(jnp.bfloat16))
    ffn_back = ffn_weights(w_gu, w_down, gain_two)
    w_gu_back, w_down_back, gain_two_back = ffn_back
    d_hidden = jnp.einsum("rte,fe->rtf", d_ffn, w_down_back, preferred_element_type=jnp.float32)
    grad_down = jnp.einsum("rtf,rte->fe", hidden, d_ffn, preferred_element_type=jnp.float32)
    d_gate = d_hidden * up_act * sigmoid_gate * (1.0 + gate_act * (1.0 - sigmoid_gate))
    d_up = d_hidden * silu_gate
    d_gate_up = jnp.stack([d_gate, d_up], axis=2).astype(jnp.bfloat16)
    grad_gu = jnp.einsum("rtd,rtkf->dkf", normed_two, d_gate_up, preferred_element_type=jnp.float32)
    d_normed_two = reduce_rows(
        jnp.einsum("rtkf,dkf->rtd", d_gate_up, w_gu_back, preferred_element_type=jnp.float32)
    )
    d_norm_mid, grad_gain_two_term = norm_back(
        d_normed_two, middle, scale_two, gain_two_back.astype(jnp.float32)
    )
    d_middle = d_result + d_norm_mid
    d_mix = gather_rows(d_middle.astype(jnp.bfloat16))
    mixer_back = mixer_weights(w_in, w_out, kernel, gain_one)
    w_in_back, w_out_back, kernel_back, gain_one_back = mixer_back
    back_taps = lax.dynamic_slice_in_dim(kernel_back, tensor_rank * channels, channels, 1).astype(
        jnp.float32
    )
    d_gated = jnp.einsum("rte,ce->rtc", d_mix, w_out_back, preferred_element_type=jnp.float32)
    grad_out = jnp.einsum("rtc,rte->ce", gated, d_mix, preferred_element_type=jnp.float32)
    d_c_stream = d_gated * conv_out
    d_conv = d_gated * c_stream
    d_padded = jnp.zeros((row_count, row_len + reach, channels), jnp.float32)
    tap_grads = []
    for offset in range(reach + 1):
        d_padded = d_padded + jnp.pad(
            back_taps[offset] * d_conv, ((0, 0), (offset, reach - offset), (0, 0))
        )
        tap_grads.append(jnp.sum(d_conv * padded[:, offset : offset + row_len], axis=(0, 1)))
    grad_taps = jnp.stack(tap_grads, axis=0)
    d_prior = d_padded[:, :reach].reshape(row_count, reach * channels)
    spread = jnp.dot(before_mask.astype(jnp.float32).T, d_prior, precision=lax.Precision.HIGHEST)
    back_tails = lax.psum_scatter(spread, "dp", scatter_dimension=0, tiled=True).reshape(
        row_count, reach, channels
    )
    d_mixed = d_padded[:, reach:] + jnp.pad(back_tails, ((0, 0), (row_len - reach, 0), (0, 0)))
    d_proj = jnp.stack([d_mixed * u_stream, d_c_stream, d_mixed * b_stream], axis=2).astype(
        jnp.bfloat16
    )
    grad_in_proj = jnp.einsum(
        "rtd,rtkc->dkc", normed_one, d_proj, preferred_element_type=jnp.float32
    )
    d_normed_one = reduce_rows(
        jnp.einsum("rtkc,dkc->rtd", d_proj, w_in_back, preferred_element_type=jnp.float32)
    )
    d_norm_in, grad_gain_one_term = norm_back(
        d_normed_one, x_own, scale_one, gain_one_back.astype(jnp.float32)
    )
    grad_in = (d_norm_in + d_middle).astype(jnp.bfloat16)
    kernel_term = lax.dynamic_update_slice_in_dim(
        jnp.zeros((reach + 1, feature_dim), jnp.float32), grad_taps, tensor_rank * channels, 1
    )
    grad_w_in, grad_w_out, kernel_part, gain_one_part, grad_w_gu, grad_w_down, gain_two_part = (
        lax.psum_scatter(grad_in_proj, "dp", scatter_dimension=0, tiled=True),
        lax.psum_scatter(grad_out, "dp", scatter_dimension=1, tiled=True),
        lax.psum_scatter(kernel_term, "dp", scatter_dimension=1, tiled=True),
        lax.psum_scatter(grad_gain_one_term, "dp", scatter_dimension=0, tiled=True),
        lax.psum_scatter(grad_gu, "dp", scatter_dimension=0, tiled=True),
        lax.psum_scatter(grad_down, "dp", scatter_dimension=1, tiled=True),
        lax.psum_scatter(grad_gain_two_term, "dp", scatter_dimension=0, tiled=True),
    )
    grad_kernel, grad_gain_one, grad_gain_two = lax.psum(
        (kernel_part, gain_one_part, gain_two_part), "tensor"
    )
    return (
        layer_out,
        grad_in,
        grad_gain_one,
        grad_w_in,
        grad_kernel,
        grad_w_out,
        grad_gain_two,
        grad_w_gu,
        grad_w_down,
    )


def solution(mesh):
    in_specs = (
        P("dp", "tensor", None),
        P("dp", "tensor", None),
        P(),
        P(),
        P(),
        P("dp"),
        P("dp", None, "tensor"),
        P(None, "dp"),
        P("tensor", "dp"),
        P("dp"),
        P("dp", None, "tensor"),
        P("tensor", "dp"),
    )
    out_specs = (
        P("dp", "tensor", None),
        P("dp", "tensor", None),
        P("dp"),
        P("dp", None, "tensor"),
        P(None, "dp"),
        P("tensor", "dp"),
        P("dp"),
        P("dp", None, "tensor"),
        P("tensor", "dp"),
    )
    return jax.shard_map(body, mesh=mesh, in_specs=in_specs, out_specs=out_specs, check_vma=False)
```

profile of v0, /device:TPU:0, one launch (start us, length us, event | category | flops | bytes accessed | tf_op | source)
XLA Modules:
  0.0 825.1 jit_solution(3424187963170859542)
XLA Ops:
  7.3 0.7 all-gather.12.cloned.1.call-update
  8.0 10.4 %all-gather = bf16[8,1,128]{2,1,0:T(2,128)(2,1)S(1)} all-gather(bf16[1,1,128]{2,1,0:T(2,128)(2,1)} %bitcast.184), channel_id=1, replica_groups=mesh['dp'=8,'tensor'=4] {'dp'}, dimensions={0}, use_global_device_ids=true | all-gather | bytes 2304 | tf_op jit(solution)/shard_map/all_gather | solution.py:24
  18.4 1.2 fusion.39
  19.6 2.0 fusion.41
  22.3 8.8 %all_gather.46 = bf16[3,1024]{1,0:T(4,128)(2,1)S(1)} all-gather(bf16[3,128]{1,0:T(4,128)(2,1)S(1)} %copy-done.13), channel_id=1, replica_groups=mesh['dp'=8,'tensor'=4] {'dp'}, dimensions={1}, use_global_device_ids=true | all-gather | bytes 6912 | tf_op jit(solution)/shard_map/all_gather | solution.py:23
  31.1 10.0 %all_gather.48 = bf16[256,1024]{1,0:T(8,128)(2,1)S(1)} all-gather(bf16[256,128]{1,0:T(8,128)(2,1)S(1)} %copy-done.10), channel_id=1, replica_groups=mesh['dp'=8,'tensor'=4] {'dp'}, dimensions={1}, use_global_device_ids=true | all-gather | bytes 589824 | tf_op jit(solution)/shard_map/all_gather | solution.py:22
  41.1 45.7 %all-gather.10.cloned.1.call-done = bf16[8,128,1024]{2,1,0:T(8,128)(2,1)} async-done(((bf16[8,32,1024]{2,1,0:T(8,128)(2,1)}), bf16[8,128,1024]{2,1,0:T(8,128)(2,1)}) %all-gather.10.cloned.1.call-update) | async-done | bytes 2097168 | tf_op jit(solution)/shard_map/all_gather | solution.py:10
  86.8 3.8 fusion.12
  90.9 9.2 %all_gather.47 = bf16[64,2,256]{2,1,0:T(2,128)(2,1)S(1)} all-gather(bf16[8,2,256]{2,1,0:T(2,128)(2,1)S(1)} %slice.61), channel_id=1, replica_groups=mesh['dp'=8,'tensor'=4] {'dp'}, dimensions={0}, use_global_device_ids=true | all-gather | bytes 73728 | tf_op jit(solution)/shard_map/all_gather | solution.py:99
  100.3 1.4 multiply_convert_fusion.7
  101.7 0.8 copy-done.7
  102.5 2.1 convolution_convert_fusion
  104.6 2.0 copy.59
  106.7 8.7 %all-gather.1 = bf16[8,1,128]{2,1,0:T(2,128)(2,1)S(1)} all-gather(bf16[1,1,128]{2,1,0:T(2,128)(2,1)S(1)} %bitcast.185), channel_id=1, replica_groups=mesh['dp'=8,'tensor'=4] {'dp'}, dimensions={0}, use_global_device_ids=true | all-gather | bytes 2304 | tf_op jit(solution)/shard_map/all_gather | solution.py:32
  115.5 30.8 %reduce-scatter.13.cloned.1.call-done = bf16[8,32,1024]{2,1,0:T(8,128)(2,1)} async-done(((bf16[8,128,1024]{2,1,0:T(8,128)(2,1)}), bf16[8,32,1024]{2,1,0:T(8,128)(2,1)}) %reduce-scatter.13.cloned.1.call-update) | async-done | bytes 524304 | tf_op jit(solution)/shard_map/reduce_scatter | solution.py:14
  146.2 1.3 multiply_reduce_fusion.3
  147.5 2.0 multiply_convert_fusion.6
  150.0 1.0 fusion.46
  151.0 0.7 all-gather.18.cloned.1.call-update
  151.7 0.2 reduce-scatter.17.cloned.1.call-start
  151.9 34.7 %all-gather.16.cloned.1.call-done = bf16[1024,2,1152]{2,0,1:T(8,128)(2,1)} async-done(((bf16[128,2,1152]{2,0,1:T(8,128)(2,1)}), bf16[1024,2,1152]{2,0,1:T(8,128)(2,1)}) %all-gather.16.cloned.1.call-update) | async-done | bytes 4718608 | tf_op jit(solution)/shard_map/all_gather | solution.py:30
  186.6 47.7 %all-gather.14.cloned.1.call-done = bf16[8,128,1024]{2,1,0:T(8,128)(2,1)} async-done(((bf16[8,32,1024]{2,1,0:T(8,128)(2,1)}), bf16[8,128,1024]{2,1,0:T(8,128)(2,1)}) %all-gather.14.cloned.1.call-update) | async-done | bytes 2097168 | tf_op jit(solution)/shard_map/all_gather | solution.py:10
  234.3 10.1 %fusion.2 = f32[8,128,2,1152]{3,1,2,0:T(8,128)} fusion(bf16[1024,2,1152]{2,0,1:T(8,128)(2,1)} %all-gather.16.cloned.1.call-done, bf16[8,128,1024]{2,1,0:T(8,128)(2,1)} %all-gather.14.cloned.1.call-done), kind=kOutput, calls=%fused_computation.6 | convolution fusion | flops 4831838208 | bytes 16252928 | tf_op jit(solution)/shard_map/rtd,dkf->rtkf/dot_general | solution.py:120
  244.4 35.8 %all-gather.20.cloned.1.call-done = bf16[8,128,1024]{2,1,0:T(8,128)(2,1)} async-done(((bf16[8,32,1024]{2,1,0:T(8,128)(2,1)}), bf16[8,128,1024]{2,1,0:T(8,128)(2,1)}) %all-gather.20.cloned.1.call-update) | async-done | bytes 2097168 | tf_op jit(solution)/shard_map/all_gather | solution.py:10
  280.2 30.0 %all-gather.18.cloned.1.call-done = bf16[1152,1024]{1,0:T(8,128)(2,1)} async-done(((bf16[1152,128]{1,0:T(8,128)(2,1)}), bf16[1152,1024]{1,0:T(8,128)(2,1)}) %all-gather.18.cloned.1.call-update) | async-done | bytes 2359312 | tf_op jit(solution)/shard_map/all_gather | solution.py:31
  310.2 10.8 %fusion.10 = (bf16[8,128,1,1152]{3,1,0,2:T(8,128)(2,1)S(1)}, bf16[8,128,1,1152]{3,1,0,2:T(8,128)(2,1)S(1)}, bf16[8,128,1152]{2,1,0:T(8,128)(2,1)}) fusion(f32[8,128,2,1152]{3,1,2,0:T(8,128)} %fusion.2, bf16[8,128,1024]{2,1,0:T(8,128)(2,1)} %all-gather.20.cloned.1.call-done, bf16[1152,1024]{1,0:T(8,128)(2,1)} %all-gather.18.cloned.1.call-done), kind=kOutput, calls=%fused_computation.27 | convolution fusion | flops 2433613824 | bytes 20971520 | tf_op jit(solution)/shard_map/rte,fe->rtf/dot_general | solution.py:133
  320.9 1.4 copy-done.18
  322.4 0.7 copy-done.19
  323.1 8.7 %bitcast_convert_fusion.1 = bf16[8,128,1024]{2,1,0:T(8,128)(2,1)} fusion(bf16[1024,2,1152]{2,0,1:T(8,128)(2,1)} %all-gather.16.cloned.1.call-done, bf16[8,128,1,1152]{3,1,0,2:T(8,128)(2,1)S(1)} %get-tuple-element.67, bf16[8,128,1,1152]{3,1,0,2:T(8,128)(2,1)S(1)} %get-tuple-element.66), kind=kOutput, calls=%fused_computation.15 | convolution fusion | flops 4835246080 | bytes 11534336 | tf_op jit(solution)/shard_map/rtkf,dkf->rtd/dot_general | solution.py:140
  331.8 43.7 %reduce-scatter.17.cloned.1.call-done = bf16[8,32,1024]{2,1,0:T(8,128)(2,1)} async-done(((bf16[8,128,1024]{2,1,0:T(8,128)(2,1)}), bf16[8,32,1024]{2,1,0:T(8,128)(2,1)}) %reduce-scatter.17.cloned.1.call-update) | async-done | bytes 524304 | tf_op jit(solution)/shard_map/reduce_scatter | solution.py:14
  375.5 1.4 fusion.38
  377.0 2.3 fusion.54
  379.3 45.0 %all-gather.22.cloned.1.call-done = bf16[8,128,1024]{2,1,0:T(8,128)(2,1)} async-done(((bf16[8,32,1024]{2,1,0:T(8,128)(2,1)}), bf16[8,128,1024]{2,1,0:T(8,128)(2,1)}) %all-gather.22.cloned.1.call-update) | async-done | bytes 2097168 | tf_op jit(solution)/shard_map/all_gather | solution.py:10
  424.3 4.1 multiply_reduce_fusion.2
  428.4 0.3 broadcast_multiply_fusion.2
  428.7 1.0 copy-done.2
  429.7 1.0 fusion.60
  430.8 1.0 copy.72
  431.8 2.4 pad_add_fusion
  434.3 0.3 reduce-scatter.21.cloned.1.call-start
  434.5 28.7 %reduce-scatter.19.cloned.1.call-done = f32[8,512]{1,0:T(8,128)} async-done(((f32[64,512]{1,0:T(8,128)}), f32[8,512]{1,0:T(8,128)}) %reduce-scatter.19.cloned.1.call-update) | async-done | bytes 16400 | tf_op jit(solution)/shard_map/reduce_scatter | solution.py:166
  463.2 0.7 reshape.140
  463.9 2.2 fusion.48
  466.1 4.6 bitcast_convert_fusion
  470.8 6.6 fusion.17
  477.5 10.2 %convolution_bitcast_fusion = f32[1024,2,1152]{2,0,1:T(8,128)} fusion(bf16[8,128,1,1152]{3,1,0,2:T(8,128)(2,1)} %copy-done.19, bf16[8,128,1,1152]{3,1,0,2:T(8,128)(2,1)} %copy-done.18, bf16[8,128,1024]{2,1,0:T(8,128)(2,1)} %all-gather.14.cloned.1.call-done), kind=kOutput, calls=%fused_computation | convolution fusion | flops 4841275392 | bytes 16252928 | tf_op jit(solution)/shard_map/rtd,rtkf->dkf/dot_general | solution.py:138
  487.7 7.1 convolution_bitcast_fusion.1
  494.9 1.0 copy-done.8
  495.9 3.4 convolution_bitcast_fusion.2
  499.3 5.1 fusion.20
  504.5 0.6 copy-done.16
  505.1 0.6 dynamic-slice
  506.4 0.9 copy.73
  507.3 39.5 %reduce-scatter.21.cloned.1.call-done = bf16[8,32,1024]{2,1,0:T(8,128)(2,1)} async-done(((bf16[8,128,1024]{2,1,0:T(8,128)(2,1)}), bf16[8,32,1024]{2,1,0:T(8,128)(2,1)}) %reduce-scatter.21.cloned.1.call-update) | async-done | bytes 524304 | tf_op jit(solution)/shard_map/reduce_scatter | solution.py:14
  546.8 1.4 fusion.45
  548.2 13.5 %all-reduce.6 = (f32[1024]{0:T(1024)S(1)}, f32[1024]{0:T(1024)S(1)}) all-reduce(f32[1024]{0:T(1024)S(1)} %get-tuple-element.50, f32[1024]{0:T(1024)S(1)} %get-tuple-element.47), channel_id=7, replica_groups=mesh['dp'=8,'tensor'=4] {'dp'}, use_global_device_ids=true, to_apply=%region_14.15.clone | all-reduce | flops 2048 | bytes 16384
  561.9 11.3 %all-reduce.7 = (f32[128]{0:T(128)}, f32[3,128]{1,0:T(4,128)}, f32[128]{0:T(128)}) all-reduce(f32[128]{0:T(128)S(1)} %dynamic-slice.1, f32[3,128]{1,0:T(4,128)S(1)} %copy.73, f32[128]{0:T(128)S(1)} %dynamic-slice.3), channel_id=1, replica_groups=mesh['dp'=8,'tensor'=4] {'tensor'}, use_global_device_ids=true, to_apply=%region_15.16 | all-reduce | flops 640 | bytes 5120 | tf_op jit(solution)/shard_map/psum | solution.py:195
  573.2 19.1 %reduce-scatter.15.cloned.1.call-done = bf16[8,32,1024]{2,1,0:T(8,128)(2,1)} async-done(((bf16[8,128,1024]{2,1,0:T(8,128)(2,1)}), bf16[8,32,1024]{2,1,0:T(8,128)(2,1)}) %reduce-scatter.15.cloned.1.call-update) | async-done | bytes 524304 | tf_op jit(solution)/shard_map/reduce_scatter | solution.py:14
  592.3 2.9 fusion.33
  595.2 76.4 %reduce-scatter.27.cloned.1.call-done = f32[128,2,1152]{2,0,1:T(8,128)} async-done(((f32[1024,2,1152]{2,0,1:T(8,128)}), f32[128,2,1152]{2,0,1:T(8,128)}) %reduce-scatter.27.cloned.1.call-update) | async-done | bytes 1179664 | tf_op jit(solution)/shard_map/reduce_scatter | solution.py:191
  671.6 3.2 copy.63
  674.7 54.4 %reduce-scatter.29.cloned.1.call-done = f32[1152,128]{1,0:T(8,128)} async-done(((f32[1152,1024]{1,0:T(8,128)}), f32[1152,128]{1,0:T(8,128)}) %reduce-scatter.29.cloned.1.call-update) | async-done | bytes 589840 | tf_op jit(solution)/shard_map/reduce_scatter | solution.py:192
  729.1 39.6 %reduce-scatter.25.cloned.1.call-done = f32[256,128]{1,0:T(8,128)} async-done(((f32[256,1024]{1,0:T(8,128)}), f32[256,128]{1,0:T(8,128)}) %reduce-scatter.25.cloned.1.call-update) | async-done | bytes 131088 | tf_op jit(solution)/shard_map/reduce_scatter | solution.py:188
  768.7 49.9 %reduce-scatter.23.cloned.1.call-done = f32[128,3,256]{2,0,1:T(8,128)} async-done(((f32[1024,3,256]{2,0,1:T(8,128)}), f32[128,3,256]{2,0,1:T(8,128)}) %reduce-scatter.23.cloned.1.call-update) | async-done | bytes 393232 | tf_op jit(solution)/shard_map/reduce_scatter | solution.py:187
  (95 shorter events, 2.4 us)
Async XLA Ops:
  7.2 14.6 %copy-start.12 = (s32[16]{0:T(128)S(1)}, s32[16]{0:T(128)}, u32[]{:S(2)}) copy-start(s32[16]{0:T(128)} %param.14) | copy-start | bytes 196
  7.2 14.8 %copy-start.11 = (s32[64]{0:T(128)S(1)}, s32[64]{0:T(128)}, u32[]{:S(2)}) copy-start(s32[64]{0:T(128)} %param.16) | copy-start | bytes 772
  7.2 15.1 %copy-start.13 = (bf16[3,128]{1,0:T(4,128)(2,1)S(1)}, bf16[3,128]{1,0:T(4,128)(2,1)}, u32[]{:S(2)}) copy-start(bf16[3,128]{1,0:T(4,128)(2,1)} %param.19) | copy-start | bytes 2308
  7.2 23.9 %copy-start.10 = (bf16[256,128]{1,0:T(8,128)(2,1)S(1)}, bf16[256,128]{1,0:T(8,128)(2,1)}, u32[]{:S(2)}) copy-start(bf16[256,128]{1,0:T(8,128)(2,1)} %param.20) | copy-start | bytes 196612
  7.2 33.9 %all-gather.12.cloned.1.call-start = ((), (), s32[]{:S(2)}) async-start(), calls=%async_computation.11 | async-start | bytes 1769472 | tf_op jit(solution)/shard_map/all_gather | solution.py:21
  8.0 78.8 %all-gather.10.cloned.1.call-start = ((), (), s32[]{:S(2)}) async-start(), calls=%async_computation.10 | async-start | bytes 2621440 | tf_op jit(solution)/shard_map/all_gather | solution.py:10
  21.7 124.5 %reduce-scatter.13.cloned.1.call-start = ((), (), s32[]{:S(2)}) async-start(), calls=%async_computation.12 | async-start | bytes 2621440 | tf_op jit(solution)/shard_map/reduce_scatter | solution.py:14
  90.6 11.0 %copy-start.3 = (f32[8,128,3,256]{3,1,2,0:T(8,128)}, f32[8,128,3,256]{3,1,2,0:T(8,128)S(1)}, u32[]{:S(2)}) copy-start(f32[8,128,3,256]{3,1,2,0:T(8,128)S(1)} %fusion.12) | copy-start | bytes 9437188
  90.8 9.4 %copy-start.9 = (bf16[8,128,256]{2,1,0:T(8,128)(2,1)}, bf16[8,128,256]{2,1,0:T(8,128)(2,1)S(1)}, u32[]{:S(2)}) copy-start(bf16[8,128,256]{2,1,0:T(8,128)(2,1)S(1)} %get-tuple-element.65) | copy-start | bytes 1572868
  101.7 0.8 copy-start.7
  104.5 2.2 copy-start.14
  104.5 41.7 %copy-start = (bf16[8,32,1024]{2,1,0:T(8,128)(2,1)S(1)}, bf16[8,32,1024]{2,1,0:T(8,128)(2,1)}, u32[]{:S(2)}) copy-start(bf16[8,32,1024]{2,1,0:T(8,128)(2,1)} %param.12) | copy-start | bytes 1572868
  104.6 45.1 %copy-start.15 = (s32[16]{0:T(128)S(1)}, s32[16]{0:T(128)}, u32[]{:S(2)}) copy-start(s32[16]{0:T(128)} %param.15) | copy-start | bytes 196
  104.6 45.4 %copy-start.5 = (bf16[8,32,1024]{2,1,0:T(8,128)(2,1)S(1)}, bf16[8,32,1024]{2,1,0:T(8,128)(2,1)}, u32[]{:S(2)}) copy-start(bf16[8,32,1024]{2,1,0:T(8,128)(2,1)} %param.13) | copy-start | bytes 1572868
  104.6 82.0 %all-gather.16.cloned.1.call-start = ((), (), s32[]{:S(2)}) async-start(), calls=%async_computation.14 | async-start | bytes 5308416 | tf_op jit(solution)/shard_map/all_gather | solution.py:30
  106.7 127.6 %all-gather.14.cloned.1.call-start = ((), (), s32[]{:S(2)}) async-start(), calls=%async_computation.13 | async-start | bytes 2621440 | tf_op jit(solution)/shard_map/all_gather | solution.py:10
  149.6 130.6 %all-gather.20.cloned.1.call-start = ((), (), s32[]{:S(2)}) async-start(), calls=%async_computation.17 | async-start | bytes 2621440 | tf_op jit(solution)/shard_map/all_gather | solution.py:10
  150.9 159.2 %all-gather.18.cloned.1.call-start = ((), (), s32[]{:S(2)}) async-start(), calls=%async_computation.15 | async-start | bytes 2654208 | tf_op jit(solution)/shard_map/all_gather | solution.py:31
  151.7 223.8 %reduce-scatter.17.cloned.1.call-start = ((), (), s32[]{:S(2)}) async-start(), calls=%async_computation.18 | async-start | bytes 2621440 | tf_op jit(solution)/shard_map/reduce_scatter | solution.py:14
  320.9 1.5 copy-start.18
  320.9 2.1 copy-start.19
  331.7 43.8 %copy-start.1 = (bf16[8,32,1024]{2,1,0:T(8,128)(2,1)S(1)}, bf16[8,32,1024]{2,1,0:T(8,128)(2,1)}, u32[]{:S(2)}) copy-start(bf16[8,32,1024]{2,1,0:T(8,128)(2,1)} %reduce-scatter.13.cloned.1.call-done) | copy-start | bytes 1572868
  331.8 92.5 %all-gather.22.cloned.1.call-start = ((), (), s32[]{:S(2)}) async-start(), calls=%async_computation.19 | async-start | bytes 2621440 | tf_op jit(solution)/shard_map/all_gather | solution.py:10
  379.3 83.9 %reduce-scatter.19.cloned.1.call-start = ((), (), s32[]{:S(2)}) async-start(), calls=%async_computation.20 | async-start | bytes 147456 | tf_op jit(solution)/shard_map/reduce_scatter | solution.py:166
  428.7 1.0 copy-start.2
  430.7 75.7 %reduce-scatter.31.cloned.1.call-start = ((), (), s32[]{:S(2)}) async-start(), calls=%async_computation.26 | async-start | bytes 589824
  434.2 31.9 %copy-start.17 = (bf16[8,128,1,256]{3,1,0,2:T(8,128)(2,1)S(1)}, bf16[8,128,1,256]{3,1,0,2:T(8,128)(2,1)}, u32[]{:S(2)}) copy-start(bf16[8,128,1,256]{3,1,0,2:T(8,128)(2,1)} %get-tuple-element.73) | copy-start | bytes 1572868
  434.3 112.5 %reduce-scatter.21.cloned.1.call-start = ((), (), s32[]{:S(2)}) async-start(), calls=%async_computation.21 | async-start | bytes 2621440 | tf_op jit(solution)/shard_map/reduce_scatter | solution.py:14
  470.8 121.5 %reduce-scatter.15.cloned.1.call-start = ((), (), s32[]{:S(2)}) async-start(), calls=%async_computation.16 | async-start | bytes 2621440 | tf_op jit(solution)/shard_map/reduce_scatter | solution.py:14
  477.5 194.1 %reduce-scatter.27.cloned.1.call-start = ((), (), s32[]{:S(2)}) async-start(), calls=%async_computation.24 | async-start | bytes 10616832 | tf_op jit(solution)/shard_map/reduce_scatter | solution.py:191
  487.7 241.4 %reduce-scatter.29.cloned.1.call-start = ((), (), s32[]{:S(2)}) async-start(), calls=%async_computation.25 | async-start | bytes 5308416 | tf_op jit(solution)/shard_map/reduce_scatter | solution.py:192
  494.9 1.0 copy-start.8
  494.9 273.8 %reduce-scatter.25.cloned.1.call-start = ((), (), s32[]{:S(2)}) async-start(), calls=%async_computation.23 | async-start | bytes 1179648 | tf_op jit(solution)/shard_map/reduce_scatter | solution.py:188
  499.3 319.3 %reduce-scatter.23.cloned.1.call-start = ((), (), s32[]{:S(2)}) async-start(), calls=%async_computation.22 | async-start | bytes 3538944 | tf_op jit(solution)/shard_map/reduce_scatter | solution.py:187
  504.5 0.7 copy-start.16
  504.5 87.8 %copy-start.4 = (bf16[8,32,1024]{2,1,0:T(8,128)(2,1)S(1)}, bf16[8,32,1024]{2,1,0:T(8,128)(2,1)}, u32[]{:S(2)}) copy-start(bf16[8,32,1024]{2,1,0:T(8,128)(2,1)} %reduce-scatter.17.cloned.1.call-done) | copy-start | bytes 1572868
  504.5 87.8 %copy-start.6 = (bf16[8,32,1024]{2,1,0:T(8,128)(2,1)S(1)}, bf16[8,32,1024]{2,1,0:T(8,128)(2,1)}, u32[]{:S(2)}) copy-start(bf16[8,32,1024]{2,1,0:T(8,128)(2,1)} %param.13) | copy-start | bytes 1572868
Sparse Core Ops, SparseCore 0:
  9.9 28.9 all-gather.11
  41.1 45.6 all-gather.9
  104.7 41.5 reduce-scatter.12
  148.6 37.9 all-gather.15
  188.6 45.6 all-gather.13
  235.7 44.4 all-gather.19
  282.1 28.0 all-gather.17
  331.9 43.5 reduce-scatter.16
  379.4 44.8 all-gather.21
  430.8 32.3 reduce-scatter.18
  466.9 34.0 reduce-scatter.30
  503.2 43.6 reduce-scatter.20
  549.1 43.1 reduce-scatter.14
  595.6 75.8 reduce-scatter.26
  675.4 53.6 reduce-scatter.28
  732.7 35.9 reduce-scatter.24
  772.5 46.0 reduce-scatter.22
where the time goes:
time: 826 us; the launch traced here: 825 us
  waiting for transfers between devices  622 us (75%)
  matrix products  77.7 us (9%)
  blocking collectives  72 us (9%)
  other arithmetic  22.8 us (3%)
  between operations  14.9 us (2%)
  local copies, waits for them, and re-layouts  14.3 us (2%)
    all_gather x4, waiting for transfers between devices, gather_rows(): return lax.all_gather(value, 'tensor', axis=1, tiled=True)  174 us
    reduce_scatter x4, waiting for transfers between devices, reduce_rows(): lax.psum_scatter(value.astype(jnp.bfloat16), 'tensor', scatter_dimension=...  133 us
    reduce_scatter x1, waiting for transfers between devices, body(): lax.psum_scatter(grad_gu, 'dp', scatter_dimension=0, tiled=True)  76.4 us
    reduce_scatter x1, waiting for transfers between devices, body(): lax.psum_scatter(grad_down, 'dp', scatter_dimension=1, tiled=True)  54.4 us
    reduce_scatter x1, waiting for transfers between devices, body(): lax.psum_scatter(grad_in_proj, 'dp', scatter_dimension=0, tiled=True)  49.9 us
    reduce_scatter x1, waiting for transfers between devices, body(): lax.psum_scatter(grad_out, 'dp', scatter_dimension=1, tiled=True)  39.6 us
    all_gather x1, waiting for transfers between devices, ffn_weights(): lax.all_gather(w_gu, 'dp', axis=0, tiled=True)  34.7 us
    all_gather x1, waiting for transfers between devices, ffn_weights(): lax.all_gather(w_down, 'dp', axis=1, tiled=True)  30 us
  transfers between devices with their start and end apart: 17, of which 15 were waited for; matrix products, arithmetic and copies ran while one was open for 9% of the time, Pallas kernels for 0%

commit v1 on v0

v1 whole, which is shorter than its diff:
```python
import functools
import jax
import jax.numpy as jnp
from jax import lax
from jax.experimental import pallas as pl
from jax.experimental.pallas import tpu as pltpu
from jax.sharding import PartitionSpec as P

EPS = 1e-05
INNER = 8
BF = jnp.bfloat16
F32 = jnp.float32


def dp_swap(value, step):
    size = lax.axis_size("dp")
    hop = step * (size // INNER)
    return lax.ppermute(value, "dp", [(i, i ^ hop) for i in range(size)])


def z_shift(value, step):
    size = lax.axis_size("tensor")
    return lax.ppermute(value, "tensor", [(i, (i + step) % size) for i in range(size)])


def outer_groups():
    outer = lax.axis_size("dp") // INNER
    return [[i * outer + o for o in range(outer)] for i in range(INNER)]


def mm(a, b):
    return lax.dot_general(a, b, (((1,), (0,)), ((), ())), preferred_element_type=F32)


def mm_nt(a, b):
    return lax.dot_general(a, b, (((1,), (1,)), ((), ())), preferred_element_type=F32)


def mm_tn(a, b):
    return lax.dot_general(a, b, (((0,), (0,)), ((), ())), preferred_element_type=F32)


def plane_gather(local):
    own = [local] + [dp_swap(local, 2 * kq) for kq in (1, 2, 3)]
    other = [dp_swap(piece, 1) for piece in own]
    return [piece for pair in zip(own, other) for piece in pair]


def place_mixer_kernel(idx_ref, *refs):
    pieces, outs, small_ref = refs[:8], refs[8:12], refs[12]
    held, in_sems, out_sems, small_sems = refs[13:]
    me, z = idx_ref[0], idx_ref[1]
    n_z = outs[0].shape[1] // 256
    rows = outs[0].shape[0] // 8
    loads = [pltpu.make_async_copy(pieces[k], held.at[k], in_sems.at[k]) for k in range(8)]
    for load in loads:
        load.start()
    stores = []
    for k in range(8):
        loads[k].wait()
        at = jnp.bitwise_xor(me, k)
        for s in range(n_z):
            col = lax.rem(z + n_z - s, n_z) * 256
            for st in range(4):
                store = pltpu.make_async_copy(
                    held.at[k, pl.ds((s * 4 + st) * rows, rows)],
                    outs[st].at[
                        pl.ds(pl.multiple_of(at * rows, rows), rows),
                        pl.ds(pl.multiple_of(col, 256), 256),
                    ],
                    out_sems.at[k, s * 4 + st],
                )
                store.start()
                stores.append(store)
        store = pltpu.make_async_copy(
            held.at[k, pl.ds(n_z * 4 * rows, 16)], small_ref.at[at], small_sems.at[k]
        )
        store.start()
        stores.append(store)
    for store in stores:
        store.wait()


def place_mixer(index, pieces, n_z):
    width = n_z * 256
    depth = (pieces[0].shape[0] - 16) // (4 * n_z) * 8
    hbm = pl.BlockSpec(memory_space=pl.ANY)
    return pl.pallas_call(
        place_mixer_kernel,
        out_shape=[jax.ShapeDtypeStruct((depth, width), BF)] * 4
        + [jax.ShapeDtypeStruct((8, 16, 256), BF)],
        in_specs=[pl.BlockSpec(memory_space=pltpu.SMEM)] + [hbm] * 8,
        out_specs=[hbm] * 5,
        scratch_shapes=[
            pltpu.VMEM((8,) + pieces[0].shape, BF),
            pltpu.SemaphoreType.DMA((8,)),
            pltpu.SemaphoreType.DMA((8, 4 * n_z)),
            pltpu.SemaphoreType.DMA((8,)),
        ],
        cost_estimate=pl.CostEstimate(flops=0, bytes_accessed=17_000_000, transcendentals=0),
        name="place_mixer",
    )(index, *pieces)


def place_ffn_kernel(idx_ref, *refs):
    pieces, outs = refs[:8], refs[8:11]
    held, in_sems, out_sems = refs[11:]
    me = idx_ref[0]
    rows = outs[0].shape[0] // 8
    loads = [pltpu.make_async_copy(pieces[k], held.at[k], in_sems.at[k]) for k in range(8)]
    for load in loads:
        load.start()
    stores = []
    for k in range(8):
        loads[k].wait()
        at = jnp.bitwise_xor(me, k)
        for st in range(3):
            store = pltpu.make_async_copy(
                held.at[k, st],
                outs[st].at[pl.ds(pl.multiple_of(at * rows, rows), rows)],
                out_sems.at[k, st],
            )
            store.start()
            stores.append(store)
    for store in stores:
        store.wait()


def place_ffn(index, pieces):
    _, rows, hidden = pieces[0].shape
    hbm = pl.BlockSpec(memory_space=pl.ANY)
    return pl.pallas_call(
        place_ffn_kernel,
        out_shape=[jax.ShapeDtypeStruct((8 * rows, hidden), BF)] * 3,
        in_specs=[pl.BlockSpec(memory_space=pltpu.SMEM)] + [hbm] * 8,
        out_specs=[hbm] * 3,
        scratch_shapes=[
            pltpu.VMEM((8,) + pieces[0].shape, BF),
            pltpu.SemaphoreType.DMA((8,)),
            pltpu.SemaphoreType.DMA((8, 3)),
        ],
        cost_estimate=pl.CostEstimate(flops=0, bytes_accessed=14_000_000, transcendentals=0),
        name="place_ffn",
    )(index, *pieces)


def ffn_kernel(n_ref, d_ref, wg_ref, wu_ref, wd_ref, dn_ref, part_ref, hid_ref, dg_ref, du_ref, acc_n, acc_p):
    j = pl.program_id(0)
    normed, d_out = n_ref[...], d_ref[...]
    wg, wu, wd = wg_ref[...], wu_ref[...], wd_ref[...]
    gate, up = mm(normed, wg), mm(normed, wu)
    sig = jax.nn.sigmoid(gate)
    silu = gate * sig
    hidden = (silu * up).astype(BF)
    d_hidden = mm(d_out, wd)
    d_gate = (d_hidden * up * (sig * (1.0 + gate * (1.0 - sig)))).astype(BF)
    d_up = (d_hidden * silu).astype(BF)
    hid_ref[...] = hidden
    dg_ref[...] = d_gate
    du_ref[...] = d_up
    d_normed = mm_nt(d_gate, wg) + mm_nt(d_up, wu)
    part = mm_nt(hidden, wd)

    @pl.when(j == 0)
    def _():
        acc_n[...] = d_normed
        acc_p[...] = part

    @pl.when(j > 0)
    def _():
        acc_n[...] += d_normed
        acc_p[...] += part

    @pl.when(j == pl.num_programs(0) - 1)
    def _():
        dn_ref[...] = acc_n[...].astype(BF)
        part_ref[...] = acc_p[...].astype(BF)


def ffn_piece(normed, d_out, wg, wu, wd):
    tokens, width = normed.shape
    hidden = wg.shape[1]
    block = 384 if hidden % 384 == 0 else 128
    whole = pl.BlockSpec((tokens, width), lambda j: (0, 0))
    weight = pl.BlockSpec((width, block), lambda j: (0, j))
    act = pl.BlockSpec((tokens, block), lambda j: (0, j))
    return pl.pallas_call(
        ffn_kernel,
        grid=(hidden // block,),
        out_shape=[jax.ShapeDtypeStruct((tokens, width), BF)] * 2
        + [jax.ShapeDtypeStruct((tokens, hidden), BF)] * 3,
        in_specs=[whole, whole, weight, weight, weight],
        out_specs=[whole, whole, act, act, act],
        scratch_shapes=[pltpu.VMEM((tokens, width), F32)] * 2,
        cost_estimate=pl.CostEstimate(
            flops=12 * tokens * width * hidden,
            bytes_accessed=6 * width * hidden + 8 * tokens * width + 6 * tokens * hidden,
            transcendentals=tokens * hidden,
        ),
        name="ffn_piece",
    )(normed, d_out, wg, wu, wd)


def norm_scale(value):
    return lax.rsqrt(jnp.mean(value * value, axis=-1, keepdims=True) + EPS)


def norm_back(d_normed, value, scale, gain):
    weighted = d_normed * gain
    d_value = scale * weighted - value * (scale * scale * scale) * jnp.mean(
        weighted * value, axis=-1, keepdims=True
    )
    return d_value, jnp.sum(d_normed * value * scale, axis=0)


def plane_reduce(blocks, me_in):
    size = blocks.shape[0] // 8
    tail = blocks.shape[1:]
    view = blocks.reshape((4, 2, size) + tail)
    core = lax.rem(me_in, 2)
    quad = me_in // 2
    away = lax.dynamic_index_in_dim(view, 1 - core, 1, keepdims=False)
    home = lax.dynamic_index_in_dim(view, core, 1, keepdims=False)
    half = (home.astype(F32) + dp_swap(away, 1).astype(F32)).astype(BF)
    total = lax.dynamic_index_in_dim(half, quad, 0, keepdims=False).astype(F32)
    for kq in (1, 2, 3):
        piece = lax.dynamic_index_in_dim(half, jnp.bitwise_xor(quad, kq), 0, keepdims=False)
        total = total + dp_swap(piece, 2 * kq).astype(F32)
    return total


def body(
    layer_in,
    cotangent,
    row_counts,
    tail_tokens,
    row_order,
    gain_one,
    w_in,
    kernel,
    w_out,
    gain_two,
    w_gu,
    w_down,
):
    row_count, own_len, width = layer_in.shape
    n_dp, n_z = lax.axis_size("dp"), lax.axis_size("tensor")
    outer = n_dp // INNER
    me, z = lax.axis_index("dp"), lax.axis_index("tensor")
    me_in = me // outer
    row_len = own_len * n_z
    channels = w_in.shape[2]
    reach = kernel.shape[0] - 1
    tokens = row_count * own_len
    block = width // INNER
    index = jnp.stack([me_in, z]).astype(jnp.int32)

    given = lax.dynamic_slice_in_dim(row_order, me * row_count, row_count)
    starts = jnp.cumsum(row_counts) - row_counts
    ends = starts + row_counts - 1
    is_first = jnp.any(starts[None, :] == given[:, None], axis=1)
    at_end = ends[None, :] == given[:, None]
    row_valid = jnp.where(
        jnp.any(at_end, axis=1),
        jnp.sum(jnp.where(at_end, tail_tokens[None, :], 0), axis=1),
        row_len,
    )
    positions = z * own_len + jnp.arange(own_len, dtype=jnp.int32)
    valid = (positions[None, :] < row_valid[:, None]).astype(F32)

    small = jnp.concatenate([gain_one[None], gain_two[None], kernel], axis=0)
    w_in_t = w_in.transpose(1, 0, 2)
    w_out_t = w_out.T[None]
    mixer_own = jnp.concatenate([w_in_t, w_out_t], axis=0)
    ffn_own = jnp.concatenate([w_gu.transpose(1, 0, 2), w_down.T[None]], axis=0)
    if outer > 1:
        groups = outer_groups()
        mixer_own = lax.all_gather(mixer_own, "dp", axis=1, tiled=True, axis_index_groups=groups)
        ffn_own = lax.all_gather(ffn_own, "dp", axis=1, tiled=True, axis_index_groups=groups)
        small = lax.all_gather(small, "dp", axis=1, tiled=True, axis_index_groups=groups)
    n_small = small.shape[0]
    small_rows = jnp.pad(small, ((0, 16 - n_small), (0, 256 - block)))
    mixer_rows = mixer_own.reshape(4 * block, channels)
    shifted = [mixer_rows] + [z_shift(mixer_rows, s) for s in range(1, n_z)]
    mixer_pieces = plane_gather(jnp.concatenate(shifted + [small_rows], axis=0))
    w_b, w_c, w_u, w_o, small_all = place_mixer(index, mixer_pieces, n_z)
    ffn_pieces = plane_gather(ffn_own)
    w_g, w_p, w_d = place_ffn(index, ffn_pieces)
    small_full = small_all[:, :n_small, :block].transpose(1, 0, 2).reshape(n_small, width).astype(F32)
    gain_one_all, gain_two_all, taps = small_full[0], small_full[1], small_full[2:]

    tails = layer_in[:, own_len - reach :]
    before = z_shift(tails, 1)
    spread_in = before[None]
    if outer > 1:
        spread_in = lax.all_gather(before, "dp", axis=0, axis_index_groups=groups)
    every = spread_in[None]
    for step in (1, 2, 4):
        every = jnp.concatenate([every, dp_swap(every, step)], axis=0)
    slots = INNER * outer * row_count
    rel = jnp.bitwise_xor(me_in, jnp.arange(INNER, dtype=jnp.int32))
    slot_rows = row_order.reshape(INNER, outer * row_count)[rel].reshape(slots)
    before_mask = jnp.logical_and(
        slot_rows[None, :] == (given - 1)[:, None], jnp.logical_not(is_first)[:, None]
    )
    before_mask = jnp.logical_and(before_mask, z == 0).astype(BF)
    crossed = mm(before_mask, every.reshape(slots, reach * width)).reshape(row_count, reach, width)
    x_halo = jnp.where(z == 0, crossed, before.astype(F32)).reshape(row_count * reach, width)

    d_result = (cotangent.astype(F32) * valid[:, :, None]).reshape(tokens, width)
    d_ffn = d_result.astype(BF)
    d_ffn_set = [d_ffn] + [z_shift(d_ffn, s) for s in range(1, n_z)]

    x_own = layer_in.reshape(tokens, width).astype(F32)
    scale_one = norm_scale(x_own)
    n_one = (x_own * scale_one * gain_one_all).astype(BF)
    scale_halo = norm_scale(x_halo)
    n_halo = (x_halo * scale_halo * gain_one_all).astype(BF)
    total_ch = channels * n_z
    b_own, c_own, u_own = mm(n_one, w_b), mm(n_one, w_c), mm(n_one, w_u)
    b_halo, u_halo = mm(n_halo, w_b), mm(n_halo, w_u)
    mixed = (b_own * u_own).astype(BF).astype(F32).reshape(row_count, own_len, total_ch)
    mixed_halo = (b_halo * u_halo).astype(BF).astype(F32).reshape(row_count, reach, total_ch)
    padded = jnp.concatenate([mixed_halo, mixed], axis=1)
    conv = jnp.zeros((row_count, own_len, total_ch), F32)
    for k in range(reach + 1):
        conv = conv + taps[k] * padded[:, k : k + own_len]
    conv_flat = conv.reshape(tokens, total_ch)
    gated = (c_own * conv_flat).astype(BF)
    middle = x_own + mm_nt(gated, w_o)
    scale_two = norm_scale(middle)
    n_two = (middle * scale_two * gain_two_all).astype(BF)

    n_two_set = [n_two] + [z_shift(n_two, s) for s in range(1, n_z)]
    runs = [ffn_piece(n_two_set[s], d_ffn_set[s], w_g, w_p, w_d) for s in range(n_z)]
    d_normed_two = runs[0][0].astype(F32)
    for s in range(1, n_z):
        d_normed_two = d_normed_two + z_shift(runs[s][0], n_z - s).astype(F32)
    ffn_sum = runs[0][1].astype(F32)
    for s in range(1, n_z):
        ffn_sum = ffn_sum + z_shift(runs[s][1], n_z - s).astype(F32)
    layer_out = (middle + ffn_sum).astype(BF).reshape(row_count, own_len, width)

    n_two_cat = jnp.concatenate(n_two_set, axis=0)
    d_ffn_cat = jnp.concatenate(d_ffn_set, axis=0)
    hid_cat, dg_cat, du_cat = (jnp.concatenate([run[i] for run in runs], axis=0) for i in (2, 3, 4))
    hidden_units = hid_cat.shape[1]
    ffn_grads = jnp.stack(
        [
            mm_tn(n_two_cat, dg_cat).astype(BF).reshape(INNER, block, hidden_units),
            mm_tn(n_two_cat, du_cat).astype(BF).reshape(INNER, block, hidden_units),
            mm_tn(d_ffn_cat, hid_cat).astype(BF).reshape(INNER, block, hidden_units),
        ],
        axis=1,
    )
    ffn_total = plane_reduce(ffn_grads, me_in)[0]

    d_mid_norm, g_two = norm_back(d_normed_two, middle, scale_two, gain_two_all)
    d_middle = d_result + d_mid_norm
    d_mix = d_middle.astype(BF)
    d_gated = mm(d_mix, w_o)
    d_c = (d_gated * conv_flat).astype(BF)
    d_conv = (d_gated * c_own).reshape(row_count, own_len, total_ch)
    d_padded = jnp.zeros((row_count, own_len + reach, total_ch), F32)
    tap_grads = []
    for k in range(reach + 1):
        d_padded = d_padded + jnp.pad(taps[k] * d_conv, ((0, 0), (k, reach - k), (0, 0)))
        tap_grads.append(jnp.sum(d_conv * padded[:, k : k + own_len], axis=(0, 1)))
    d_mixed = d_padded[:, reach:].reshape(tokens, total_ch)
    d_mixed_halo = d_padded[:, :reach].reshape(row_count * reach, total_ch)
    d_b, d_u = (d_mixed * u_own).astype(BF), (d_mixed * b_own).astype(BF)
    d_b_halo, d_u_halo = (d_mixed_halo * u_halo).astype(BF), (d_mixed_halo * b_halo).astype(BF)
    d_n_one = mm_nt(d_b, w_b) + mm_nt(d_c, w_c) + mm_nt(d_u, w_u)
    d_n_halo = mm_nt(d_b_halo, w_b) + mm_nt(d_u_halo, w_u)
    d_x, g_one = norm_back(d_n_one, x_own, scale_one, gain_one_all)
    d_x_halo, g_one_halo = norm_back(d_n_halo, x_halo, scale_halo, gain_one_all)

    mixer_grads = jnp.stack(
        [
            (mm_tn(n_one, d_b) + mm_tn(n_halo, d_b_halo)).astype(BF),
            mm_tn(n_one, d_c).astype(BF),
            (mm_tn(n_one, d_u) + mm_tn(n_halo, d_u_halo)).astype(BF),
            mm_tn(d_mix, gated).astype(BF),
        ],
        axis=0,
    )
    mixer_grads = mixer_grads.reshape(4, INNER, block, n_z, channels).transpose(1, 3, 0, 2, 4)
    mixer_grads = mixer_grads.reshape(INNER, n_z, 4 * block, channels)
    small_grads = jnp.stack([g_one + g_one_halo, g_two] + tap_grads, axis=0)
    small_grads = small_grads.reshape(n_small, INNER, block).transpose(1, 0, 2).astype(BF)
    small_grads = jnp.pad(small_grads, ((0, 0), (0, 16 - n_small), (0, channels - block)))
    small_grads = jnp.broadcast_to(small_grads[:, None], (INNER, n_z, 16, channels))
    mixer_sum = plane_reduce(jnp.concatenate([mixer_grads, small_grads], axis=2), me_in)[0].astype(BF)
    mixer_total = lax.dynamic_index_in_dim(mixer_sum, z, 0, keepdims=False).astype(F32)
    for s in range(1, n_z):
        piece = lax.dynamic_index_in_dim(mixer_sum, lax.rem(z + s, n_z), 0, keepdims=False)
        mixer_total = mixer_total + z_shift(piece, s).astype(F32)

    back = d_x_halo.reshape(row_count, reach * width).astype(BF)
    spread = lax.dot_general(before_mask, back, (((0,), (0,)), ((), ())), preferred_element_type=F32)
    spread = spread.reshape(INNER, outer * row_count, reach * width)
    for step in (4, 2, 1):
        spread = spread[:step] + dp_swap(spread[step:].astype(BF), step).astype(F32)
    returned = spread[0]
    if outer > 1:
        returned = lax.psum_scatter(
            returned, "dp", scatter_dimension=0, tiled=True, axis_index_groups=groups
        )
    returned = jnp.where(z == 0, returned.astype(BF), back)
    returned = z_shift(returned, n_z - 1).astype(F32).reshape(row_count, reach, width)
    grad_in = (d_x + d_middle).reshape(row_count, own_len, width)
    grad_in = grad_in + jnp.pad(returned, ((0, 0), (own_len - reach, 0), (0, 0)))

    main = mixer_total[: 4 * block].reshape(4, block, channels)
    small_total = mixer_total[4 * block : 4 * block + n_small, :block]
    if outer > 1:
        main = lax.psum_scatter(main, "dp", scatter_dimension=1, tiled=True, axis_index_groups=groups)
        small_total = lax.psum_scatter(
            small_total, "dp", scatter_dimension=1, tiled=True, axis_index_groups=groups
        )
        ffn_total = lax.psum_scatter(
            ffn_total, "dp", scatter_dimension=1, tiled=True, axis_index_groups=groups
        )
    return (
        layer_out,
        grad_in.astype(BF),
        small_total[0],
        main[:3].transpose(1, 0, 2),
        small_total[2:],
        main[3].T,
        small_total[1],
        ffn_total[:2].transpose(1, 0, 2),
        ffn_total[2].T,
    )


def solution(mesh):
    in_specs = (
        P("dp", "tensor", None),
        P("dp", "tensor", None),
        P(),
        P(),
        P(),
        P("dp"),
        P("dp", None, "tensor"),
        P(None, "dp"),
        P("tensor", "dp"),
        P("dp"),
        P("dp", None, "tensor"),
        P("tensor", "dp"),
    )
    out_specs = (
        P("dp", "tensor", None),
        P("dp", "tensor", None),
        P("dp"),
        P("dp", None, "tensor"),
        P(None, "dp"),
        P("tensor", "dp"),
        P("dp"),
        P("dp", None, "tensor"),
        P("tensor", "dp"),
    )
    return jax.shard_map(body, mesh=mesh, in_specs=in_specs, out_specs=out_specs, check_vma=False)
```

time: 826 us -> 580 us (0.70)
  the two profiles are of different devices: /device:TPU:0 before, /device:TPU:9 now
where the time goes in v1:
time: 580 us; the launch traced here: 571 us
  waiting for transfers between devices  302 us (52%)
  local copies, waits for them, and re-layouts  68.8 us (12%)
  starting transfers between devices  58.7 us (10%)
  Pallas kernels  54.5 us (9%)
  matrix products  46.2 us (8%)
  other arithmetic  39.2 us (7%)
    ppermute x20, waiting for transfers between devices, z_shift(): lax.ppermute(value, 'tensor', [(i, (i + step) % size) for i in range(size)])  159 us
    ppermute x28, waiting for transfers between devices, dp_swap(): return lax.ppermute(value, 'dp', [(i, i ^ hop) for i in range(size)])  143 us
    pallas_call x4, Pallas kernels, ffn_piece(): pl.pallas_call(ffn_kernel, grid=(hidden // block,), out_shape=[jax.ShapeD...  39.5 us
    ppermute x28, starting transfers between devices, dp_swap(): return lax.ppermute(value, 'dp', [(i, i ^ hop) for i in range(size)])  35.2 us
    dot_general x9, matrix products, mm_tn(): lax.dot_general(a, b, (((0,), (0,)), ((), ())), preferred_element_type=F32)  29.1 us
    another operation x8, local copies, waits for them, and re-layouts, body(): jnp.stack([(mm_tn(n_one, d_b) + mm_tn(n_halo, d_b_halo)).astype(BF), mm_t...  23.9 us
    ppermute x20, starting transfers between devices, z_shift(): lax.ppermute(value, 'tensor', [(i, (i + step) % size) for i in range(size)])  23.5 us
    unnamed x121, local copies, waits for them, and re-layouts  17.7 us
  transfers between devices with their start and end apart: 48, of which 25 were waited for; matrix products, arithmetic and copies ran while one was open for 18% of the time, Pallas kernels for 8%

profile of v1, /device:TPU:9, one launch (start us, length us, event | category | flops | bytes accessed | tf_op | source)
XLA Modules:
  0.0 571.5 jit_solution(13412087317098535916)
XLA Ops:
  12.8 13.8 %collective-permute-done.10 = bf16[8,2,1024]{2,0,1:T(8,128)(2,1)S(1)} collective-permute-done((bf16[8,2,1024]{2,0,1:T(8,128)(2,1)S(1)}, bf16[8,2,1024]{2,0,1:T(8,128)(2,1)S(1)}, u32[]{:S(2)}, u32[]{:S(2)}) %collective-permute-start.10) | collective-permute-done | bytes 32800 | tf_op jit(solution)/shard_map/ppermute | solution.py:23
  35.6 45.5 %collective-permute-done.13 = bf16[4,1,8,2,1024]{4,2,3,1,0:T(8,128)(2,1)S(1)} collective-permute-done((bf16[4,1,8,2,1024]{4,2,3,1,0:T(8,128)(2,1)S(1)}, bf16[4,1,8,2,1024]{4,2,3,1,0:T(8,128)(2,1)S(1)}, u32[]{:S(2)}, u32[]{:S(2)}) %collective-permute-start.13) | collective-permute-done | bytes 131104 | tf_op jit(solution)/shard_map/ppermute | solution.py:18
  84.3 2.1 collective-permute-start.3
  88.9 12.6 %collective-permute-done.17.refs_4_ = bf16[3,128,1152]{2,1,0:T(8,128)(2,1)S(1)} collective-permute-done((bf16[3,128,1152]{2,1,0:T(8,128)(2,1)}, bf16[3,128,1152]{2,1,0:T(8,128)(2,1)S(1)}, u32[]{:S(2)}, u32[]{:S(2)}) %collective-permute-start.17) | collective-permute-done | bytes 884768 | tf_op jit(solution)/shard_map/ppermute | solution.py:18
  101.5 2.2 collective-permute-start.19
  112.1 9.2 %collective-permute-done.19.refs_6_ = bf16[3,128,1152]{2,1,0:T(8,128)(2,1)} collective-permute-done((bf16[3,128,1152]{2,1,0:T(8,128)(2,1)}, bf16[3,128,1152]{2,1,0:T(8,128)(2,1)}, u32[]{:S(2)}, u32[]{:S(2)}) %collective-permute-start.19) | collective-permute-done | bytes 884768 | tf_op jit(solution)/shard_map/ppermute | solution.py:18
  121.3 3.4 collective-permute-start.14
  124.7 2.2 collective-permute-start.22
  127.7 8.2 %place_mixer.1 = (bf16[1024,1024]{1,0:T(8,128)(2,1)}, bf16[1024,1024]{1,0:T(8,128)(2,1)}, bf16[1024,1024]{1,0:T(8,128)(2,1)}, bf16[1024,1024]{1,0:T(8,128)(2,1)}, bf16[8,16,256]{2,1,0:T(8,128)(2,1)}) custom-call(s32[2]{0:T(128)} %pad_add_fusion.2.idx_ref, bf16[2064,256]{1,0:T(8,128)(2,1)} %copy-done.37, bf16[2064,256]{1,0:T(8,128)(2,1)} %collective-permute-done.3.refs_1_, ...), custom_call_target="tpu_custom_call" | custom-call | bytes 17000000 | tf_op jit(solution)/shard_map/place_mixer/pallas_call | solution.py:88
  137.0 2.0 fusion.99
  143.4 2.0 copy-done.23
  151.4 6.8 %place_ffn.1 = (bf16[1024,1152]{1,0:T(8,128)(2,1)}, bf16[1024,1152]{1,0:T(8,128)(2,1)}, bf16[1024,1152]{1,0:T(8,128)(2,1)}) custom-call(s32[2]{0:T(128)} %pad_add_fusion.2.idx_ref, bf16[3,128,1152]{2,1,0:T(8,128)(2,1)} %pad_maximum_fusion.4.refs_0_, bf16[3,128,1152]{2,1,0:T(8,128)(2,1)} %collective-permute-done.14.refs_1_, ...), custom_call_target="tpu_custom_call" | custom-call | bytes 14000000 | tf_op jit(solution)/shard_map/place_ffn/pallas_call | solution.py:132
  158.2 2.4 collective-permute-start.24
  160.6 9.9 %ffn_piece.4 = (bf16[256,1024]{1,0:T(8,128)(2,1)}, bf16[256,1024]{1,0:T(8,128)(2,1)}, bf16[256,1152]{1,0:T(8,128)(2,1)}, bf16[256,1152]{1,0:T(8,128)(2,1)}, bf16[256,1152]{1,0:T(8,128)(2,1)}) custom-call(bf16[256,1024]{1,0:T(8,128)(2,1)} %multiply_convert_fusion.n_ref, bf16[256,1024]{1,0:T(8,128)(2,1)} %bitcast_convert_fusion.d_ref, ...), custom_call_target="tpu_custom_call" | custom-call | flops 3623878656 | bytes 10944512 | tf_op jit(solution)/shard_map/ffn_piece/pallas_call | solution.py:187
  171.1 9.9 %ffn_piece.5 = (bf16[256,1024]{1,0:T(8,128)(2,1)}, bf16[256,1024]{1,0:T(8,128)(2,1)}, bf16[256,1152]{1,0:T(8,128)(2,1)}, bf16[256,1152]{1,0:T(8,128)(2,1)}, bf16[256,1152]{1,0:T(8,128)(2,1)}) custom-call(bf16[256,1024]{1,0:T(8,128)(2,1)} %collective-permute-done.21.n_ref, bf16[256,1024]{1,0:T(8,128)(2,1)} %collective-permute-done.22.d_ref, ...), custom_call_target="tpu_custom_call" | custom-call | flops 3623878656 | bytes 10944512 | tf_op jit(solution)/shard_map/ffn_piece/pallas_call | solution.py:187
  181.0 36.4 %collective-permute-done.25.d_ref = bf16[256,1024]{1,0:T(8,128)(2,1)} collective-permute-done((bf16[256,1024]{1,0:T(8,128)(2,1)}, bf16[256,1024]{1,0:T(8,128)(2,1)}, u32[]{:S(2)}, u32[]{:S(2)}) %collective-permute-start.25) | collective-permute-done | bytes 524320 | tf_op jit(solution)/shard_map/ppermute | solution.py:23
  217.4 11.2 %collective-permute-done.24.n_ref = bf16[256,1024]{1,0:T(8,128)(2,1)} collective-permute-done((bf16[256,1024]{1,0:T(8,128)(2,1)}, bf16[256,1024]{1,0:T(8,128)(2,1)}, u32[]{:S(2)}, u32[]{:S(2)}) %collective-permute-start.24) | collective-permute-done | bytes 524320 | tf_op jit(solution)/shard_map/ppermute | solution.py:23
  228.6 9.9 %ffn_piece.6 = (bf16[256,1024]{1,0:T(8,128)(2,1)}, bf16[256,1024]{1,0:T(8,128)(2,1)}, bf16[256,1152]{1,0:T(8,128)(2,1)}, bf16[256,1152]{1,0:T(8,128)(2,1)}, bf16[256,1152]{1,0:T(8,128)(2,1)}) custom-call(bf16[256,1024]{1,0:T(8,128)(2,1)} %collective-permute-done.24.n_ref, bf16[256,1024]{1,0:T(8,128)(2,1)} %collective-permute-done.25.d_ref, ...), custom_call_target="tpu_custom_call" | custom-call | flops 3623878656 | bytes 10944512 | tf_op jit(solution)/shard_map/ffn_piece/pallas_call | solution.py:187
  238.5 9.8 %ffn_piece.7 = (bf16[256,1024]{1,0:T(8,128)(2,1)}, bf16[256,1024]{1,0:T(8,128)(2,1)}, bf16[256,1152]{1,0:T(8,128)(2,1)}, bf16[256,1152]{1,0:T(8,128)(2,1)}, bf16[256,1152]{1,0:T(8,128)(2,1)}) custom-call(bf16[256,1024]{1,0:T(8,128)(2,1)} %collective-permute-done.27.n_ref, bf16[256,1024]{1,0:T(8,128)(2,1)} %collective-permute-done.28.d_ref, ...), custom_call_target="tpu_custom_call" | custom-call | flops 3623878656 | bytes 10944512 | tf_op jit(solution)/shard_map/ffn_piece/pallas_call | solution.py:187
  248.3 6.5 %convolution_convert_fusion.2 = bf16[1024,1152]{1,0:T(8,128)(2,1)} fusion(bf16[256,1152]{1,0:T(8,128)(2,1)} %get-tuple-element.56, bf16[256,1152]{1,0:T(8,128)(2,1)} %get-tuple-element.55, bf16[256,1152]{1,0:T(8,128)(2,1)} %get-tuple-element.54, bf16[256,1152]{1,0:T(8,128)(2,1)} %get-tuple-element.53, bf16[256,1024]{1,0:T(8,128)(2,1)} %collective-permute-done.27.n_ref, ...), kind=kOutput, calls=%fused_computation.19 | convolution fusion | flops 2434924544 | bytes 6815744 | tf_op jit(solution)/shard_map/dot_general | solution.py:40
  254.9 4.4 copy.96
  259.3 6.6 %convolution_convert_fusion.1 = bf16[1024,1152]{1,0:T(8,128)(2,1)} fusion(bf16[256,1152]{1,0:T(8,128)(2,1)} %get-tuple-element.60, bf16[256,1152]{1,0:T(8,128)(2,1)} %get-tuple-element.59, bf16[256,1152]{1,0:T(8,128)(2,1)} %get-tuple-element.58, bf16[256,1152]{1,0:T(8,128)(2,1)} %get-tuple-element.57, bf16[256,1024]{1,0:T(8,128)(2,1)} %collective-permute-done.27.n_ref, ...), kind=kOutput, calls=%fused_computation.18 | convolution fusion | flops 2434924544 | bytes 6815744 | tf_op jit(solution)/shard_map/dot_general | solution.py:40
  265.9 4.3 copy.97
  270.2 6.6 %convolution_convert_fusion = bf16[1024,1152]{1,0:T(8,128)(2,1)} fusion(bf16[256,1152]{1,0:T(8,128)(2,1)} %get-tuple-element.64, bf16[256,1152]{1,0:T(8,128)(2,1)} %get-tuple-element.63, bf16[256,1152]{1,0:T(8,128)(2,1)} %get-tuple-element.62, bf16[256,1152]{1,0:T(8,128)(2,1)} %get-tuple-element.61, bf16[256,1024]{1,0:T(8,128)(2,1)} %collective-permute-done.28.d_ref, ...), kind=kOutput, calls=%fused_computation.17 | convolution fusion | flops 2434924544 | bytes 6815744 | tf_op jit(solution)/shard_map/dot_general | solution.py:40
  276.8 4.3 copy.98
  281.1 3.1 collective-permute-start.31
  284.2 2.4 collective-permute-start.32
  287.8 3.9 pad_maximum_fusion.1
  291.7 2.0 collective-permute-done.30
  293.7 2.4 collective-permute-start.29
  296.1 2.2 dynamic-slice_bitcast_fusion
  298.2 19.6 %collective-permute-done.31 = bf16[256,1024]{1,0:T(8,128)(2,1)S(1)} collective-permute-done((bf16[256,1024]{1,0:T(8,128)(2,1)}, bf16[256,1024]{1,0:T(8,128)(2,1)S(1)}, u32[]{:S(2)}, u32[]{:S(2)}) %collective-permute-start.31) | collective-permute-done | bytes 524320 | tf_op jit(solution)/shard_map/ppermute | solution.py:23
  317.9 3.5 collective-permute-start.44
  321.4 30.2 %collective-permute-done.32 = bf16[256,1024]{1,0:T(8,128)(2,1)S(1)} collective-permute-done((bf16[256,1024]{1,0:T(8,128)(2,1)}, bf16[256,1024]{1,0:T(8,128)(2,1)S(1)}, u32[]{:S(2)}, u32[]{:S(2)}) %collective-permute-start.32) | collective-permute-done | bytes 524320 | tf_op jit(solution)/shard_map/ppermute | solution.py:23
  352.1 9.0 %collective-permute-done.23 = bf16[256,1024]{1,0:T(8,128)(2,1)S(1)} collective-permute-done((bf16[256,1024]{1,0:T(8,128)(2,1)}, bf16[256,1024]{1,0:T(8,128)(2,1)S(1)}, u32[]{:S(2)}, u32[]{:S(2)}) %collective-permute-start.23) | collective-permute-done | bytes 524320 | tf_op jit(solution)/shard_map/ppermute | solution.py:23
  362.8 11.1 %collective-permute-done.29 = bf16[256,1024]{1,0:T(8,128)(2,1)S(1)} collective-permute-done((bf16[256,1024]{1,0:T(8,128)(2,1)S(1)}, bf16[256,1024]{1,0:T(8,128)(2,1)S(1)}, u32[]{:S(2)}, u32[]{:S(2)}) %collective-permute-start.29) | collective-permute-done | bytes 524320 | tf_op jit(solution)/shard_map/ppermute | solution.py:23
  381.9 2.1 convolution_convert_fusion.4
  387.1 2.8 fusion.105
  389.9 2.1 convolution_convert_fusion.3
  395.6 2.0 fusion.53
  398.4 3.0 stack.52
  401.4 3.5 copy.91
  404.9 2.8 stack.53
  407.7 3.5 copy.92
  411.9 2.8 stack.54
  414.7 3.5 copy.93
  418.2 2.8 stack.55
  420.9 2.1 copy.94
  423.8 3.0 pad_maximum_fusion
  426.8 2.7 fusion.3
  429.5 2.0 copy-done
  434.6 3.8 collective-permute-done.33
  439.8 1.9 collective-permute-done.34
  441.7 2.1 collective-permute-start.35
  448.3 4.1 fusion.1
  456.2 4.1 fusion
  465.8 6.8 %collective-permute-done.45 = bf16[1,3,128,1152]{2,3,1,0:T(8,128)(2,1)S(1)} collective-permute-done((bf16[1,3,128,1152]{2,3,1,0:T(8,128)(2,1)S(1)}, bf16[1,3,128,1152]{2,3,1,0:T(8,128)(2,1)S(1)}, u32[]{:S(2)}, u32[]{:S(2)}) %collective-permute-start.45) | collective-permute-done | bytes 884768 | tf_op jit(solution)/shard_map/ppermute | solution.py:18
  472.6 2.2 collective-permute-start.40
  474.8 17.8 %collective-permute-done.47 = bf16[1,3,128,1152]{2,3,1,0:T(8,128)(2,1)S(1)} collective-permute-done((bf16[1,3,128,1152]{2,3,1,0:T(8,128)(2,1)S(1)}, bf16[1,3,128,1152]{2,3,1,0:T(8,128)(2,1)S(1)}, u32[]{:S(2)}, u32[]{:S(2)}) %collective-permute-start.47) | collective-permute-done | bytes 884768 | tf_op jit(solution)/shard_map/ppermute | solution.py:18
  494.9 19.9 %collective-permute-done.38 = bf16[1,4,528,256]{3,2,1,0:T(8,128)(2,1)} collective-permute-done((bf16[1,4,528,256]{3,2,1,0:T(8,128)(2,1)}, bf16[1,4,528,256]{3,2,1,0:T(8,128)(2,1)}, u32[]{:S(2)}, u32[]{:S(2)}) %collective-permute-start.38) | collective-permute-done | bytes 1081376 | tf_op jit(solution)/shard_map/ppermute | solution.py:18
  515.7 23.3 %collective-permute-done.40 = bf16[1,4,528,256]{3,2,1,0:T(8,128)(2,1)} collective-permute-done((bf16[1,4,528,256]{3,2,1,0:T(8,128)(2,1)}, bf16[1,4,528,256]{3,2,1,0:T(8,128)(2,1)}, u32[]{:S(2)}, u32[]{:S(2)}) %collective-permute-start.40) | collective-permute-done | bytes 1081376 | tf_op jit(solution)/shard_map/ppermute | solution.py:18
  539.0 2.7 fusion.29
  547.7 16.1 %collective-permute-done.42 = bf16[528,256]{1,0:T(8,128)(2,1)S(1)} collective-permute-done((bf16[528,256]{1,0:T(8,128)(2,1)S(1)}, bf16[528,256]{1,0:T(8,128)(2,1)S(1)}, u32[]{:S(2)}, u32[]{:S(2)}) %collective-permute-start.42) | collective-permute-done | bytes 270368 | tf_op jit(solution)/shard_map/ppermute | solution.py:23
  563.8 4.4 collective-permute-done.43
  (282 shorter events, 98.3 us)
Async XLA Ops:
  2.6 8.6 %copy-start.43 = (s32[16]{0:T(128)S(1)}, s32[16]{0:T(128)}, u32[]{:S(2)}) copy-start(s32[16]{0:T(128)} %param.14) | copy-start | bytes 196
  2.6 8.9 %copy-start.44 = (s32[64]{0:T(128)S(1)}, s32[64]{0:T(128)}, u32[]{:S(2)}) copy-start(s32[64]{0:T(128)} %param.16) | copy-start | bytes 772
  2.6 25.4 %copy-start.50 = (s32[16]{0:T(128)S(1)}, s32[16]{0:T(128)}, u32[]{:S(2)}) copy-start(s32[16]{0:T(128)} %param.15) | copy-start | bytes 196
  2.6 27.6 %collective-permute-start = (bf16[512,256]{1,0:T(8,128)(2,1)S(1)}, bf16[512,256]{1,0:T(8,128)(2,1)}, u32[]{:S(2)}, u32[]{:S(2)}) collective-permute-start(bf16[512,256]{1,0:T(8,128)(2,1)S(1)} %bitcast.223), channel_id=1, source_target_pairs={{0,1},{1,2},{2,3},{3,0},{4,5},{5,6},{6,7},{7,4},{8,9},{9,10},{10,1... | collective-permute-start | bytes 786440 | tf_op jit(solution)/shard_map/ppermute | solution.py:23
  4.0 27.2 %collective-permute-start.1 = (bf16[512,256]{1,0:T(8,128)(2,1)S(1)}, bf16[512,256]{1,0:T(8,128)(2,1)S(1)}, u32[]{:S(2)}, u32[]{:S(2)}) collective-permute-start(bf16[512,256]{1,0:T(8,128)(2,1)S(1)} %bitcast.224), channel_id=1, source_target_pairs={{0,2},{1,3},{2,0},{3,1},{4,6},{5,7},{6,4},{7,5},{8,10},{9,11},{10,... | collective-permute-start | bytes 786440 | tf_op jit(solution)/shard_map/ppermute | solution.py:23
  5.1 26.1 %collective-permute-start.2 = (bf16[512,256]{1,0:T(8,128)(2,1)S(1)}, bf16[512,256]{1,0:T(8,128)(2,1)S(1)}, u32[]{:S(2)}, u32[]{:S(2)}) collective-permute-start(bf16[512,256]{1,0:T(8,128)(2,1)S(1)} %bitcast.225), channel_id=1, source_target_pairs={{0,3},{1,0},{2,1},{3,2},{4,7},{5,4},{6,5},{7,6},{8,11},{9,8},{10,9... | collective-permute-start | bytes 786440 | tf_op jit(solution)/shard_map/ppermute | solution.py:23
  7.4 19.1 %collective-permute-start.10 = (bf16[8,2,1024]{2,0,1:T(8,128)(2,1)S(1)}, bf16[8,2,1024]{2,0,1:T(8,128)(2,1)S(1)}, u32[]{:S(2)}, u32[]{:S(2)}) collective-permute-start(bf16[8,2,1024]{2,0,1:T(8,128)(2,1)S(1)} %copy.101), channel_id=1, source_target_pairs={{0,1},{1,2},{2,3},{3,0},{4,5},{5,6},{6,7},{7,4},{8,9},{9,10},{10,1... | collective-permute-start | bytes 98312 | tf_op jit(solution)/shard_map/ppermute | solution.py:23
  8.9 22.4 %copy-start.47 = (bf16[3,128]{1,0:T(4,128)(2,1)S(1)}, bf16[3,128]{1,0:T(4,128)(2,1)}, u32[]{:S(2)}) copy-start(bf16[3,128]{1,0:T(4,128)(2,1)} %param.19) | copy-start | bytes 2308
  8.9 22.4 %copy-start.48 = (bf16[128]{0:T(256)(128)(2,1)S(1)}, bf16[128]{0:T(256)(128)(2,1)}, u32[]{:S(2)}) copy-start(bf16[128]{0:T(256)(128)(2,1)} %param.21) | copy-start | bytes 772
  8.9 22.4 %copy-start.49 = (bf16[128]{0:T(256)(128)(2,1)S(1)}, bf16[128]{0:T(256)(128)(2,1)}, u32[]{:S(2)}) copy-start(bf16[128]{0:T(256)(128)(2,1)} %param.17) | copy-start | bytes 772
  8.9 26.4 %copy-start.14 = (bf16[8,32,1024]{2,1,0:T(8,128)(2,1)S(1)}, bf16[8,32,1024]{2,1,0:T(8,128)(2,1)}, u32[]{:S(2)}) copy-start(bf16[8,32,1024]{2,1,0:T(8,128)(2,1)} %param.12) | copy-start | bytes 1572868
  10.0 74.3 %collective-permute-start.15 = (bf16[3,128,1152]{2,1,0:T(8,128)(2,1)}, bf16[3,128,1152]{2,1,0:T(8,128)(2,1)}, u32[]{:S(2)}, u32[]{:S(2)}) collective-permute-start(bf16[3,128,1152]{2,1,0:T(8,128)(2,1)} %pad_maximum_fusion.4.refs_0_), channel_id=1, source_target_pairs={{0,8},{4,12},{8,0},{12,4},{16,24},{20,28},{24,16},{28,20},{1,9},{5... | collective-permute-start | bytes 2654216 | tf_op jit(solution)/shard_map/ppermute | solution.py:18
  26.5 2.4 collective-permute-start.11
  28.9 5.1 collective-permute-start.12
  31.3 78.2 %copy-start.37 = (bf16[2064,256]{1,0:T(8,128)(2,1)}, bf16[2064,256]{1,0:T(8,128)(2,1)S(1)}, u32[]{:S(2)}) copy-start(bf16[2064,256]{1,0:T(8,128)(2,1)S(1)} %constant_dynamic-update-slice_fusion.refs_0_) | copy-start | bytes 3170308
  31.3 55.0 %collective-permute-start.4 = (bf16[2064,256]{1,0:T(8,128)(2,1)S(1)}, bf16[2064,256]{1,0:T(8,128)(2,1)}, u32[]{:S(2)}, u32[]{:S(2)}) collective-permute-start(bf16[2064,256]{1,0:T(8,128)(2,1)S(1)} %constant_dynamic-update-slice_fusion.refs_0_), channel_id=1, source_target_pairs={{0,8},{4,12},{8,0},{12,4},{16,24},{20,28},{24,16},{28,20},{1,9},{5... | collective-permute-start | bytes 3170312 | tf_op jit(solution)/shard_map/ppermute | solution.py:18
  31.6 54.8 %collective-permute-start.6 = (bf16[2064,256]{1,0:T(8,128)(2,1)S(1)}, bf16[2064,256]{1,0:T(8,128)(2,1)}, u32[]{:S(2)}, u32[]{:S(2)}) collective-permute-start(bf16[2064,256]{1,0:T(8,128)(2,1)S(1)} %constant_dynamic-update-slice_fusion.refs_0_), channel_id=1, source_target_pairs={{0,16},{4,20},{8,24},{12,28},{16,0},{20,4},{24,8},{28,12},{1,17},{... | collective-permute-start | bytes 3170312 | tf_op jit(solution)/shard_map/ppermute | solution.py:18
  32.9 54.0 %collective-permute-start.8 = (bf16[2064,256]{1,0:T(8,128)(2,1)S(1)}, bf16[2064,256]{1,0:T(8,128)(2,1)}, u32[]{:S(2)}, u32[]{:S(2)}) collective-permute-start(bf16[2064,256]{1,0:T(8,128)(2,1)S(1)} %constant_dynamic-update-slice_fusion.refs_0_), channel_id=1, source_target_pairs={{0,24},{4,28},{8,16},{12,20},{16,8},{20,12},{24,0},{28,4},{1,25},{... | collective-permute-start | bytes 3170312 | tf_op jit(solution)/shard_map/ppermute | solution.py:18
  34.0 49.0 %copy-start.42 = (bf16[2,1,8,2,1024]{4,2,3,1,0:T(8,128)(2,1)}, bf16[2,1,8,2,1024]{4,2,3,1,0:T(8,128)(2,1)S(1)}, u32[]{:S(2)}) copy-start(bf16[2,1,8,2,1024]{4,2,3,1,0:T(8,128)(2,1)S(1)} %collective-permute-done.12) | copy-start | bytes 196612
  34.1 47.0 %collective-permute-start.13 = (bf16[4,1,8,2,1024]{4,2,3,1,0:T(8,128)(2,1)S(1)}, bf16[4,1,8,2,1024]{4,2,3,1,0:T(8,128)(2,1)S(1)}, u32[]{:S(2)}, u32[]{:S(2)}) collective-permute-start(bf16[4,1,8,2,1024]{4,2,3,1,0:T(8,128)(2,1)S(1)} %pad_maximum_fusion.8), channel_id=1, source_target_pairs={{0,16},{4,20},{8,24},{12,28},{16,0},{20,4},{24,8},{28,12},{1,17},{... | collective-permute-start | bytes 393224 | tf_op jit(solution)/shard_map/ppermute | solution.py:18
  81.8 19.7 %collective-permute-start.17 = (bf16[3,128,1152]{2,1,0:T(8,128)(2,1)}, bf16[3,128,1152]{2,1,0:T(8,128)(2,1)S(1)}, u32[]{:S(2)}, u32[]{:S(2)}) collective-permute-start(bf16[3,128,1152]{2,1,0:T(8,128)(2,1)} %pad_maximum_fusion.4.refs_0_), channel_id=1, source_target_pairs={{0,16},{4,20},{8,24},{12,28},{16,0},{20,4},{24,8},{28,12},{1,17},{... | collective-permute-start | bytes 2654216 | tf_op jit(solution)/shard_map/ppermute | solution.py:18
  84.3 51.7 %copy-start.17 = (f32[8,32,1024]{2,1,0:T(8,128)}, f32[8,32,1024]{2,1,0:T(8,128)S(1)}, u32[]{:S(2)}) copy-start(f32[8,32,1024]{2,1,0:T(8,128)S(1)} %convert_multiply_fusion.1) | copy-start | bytes 3145732
  84.3 40.5 %collective-permute-start.3 = (bf16[2064,256]{1,0:T(8,128)(2,1)S(1)}, bf16[2064,256]{1,0:T(8,128)(2,1)}, u32[]{:S(2)}, u32[]{:S(2)}) collective-permute-start(bf16[2064,256]{1,0:T(8,128)(2,1)S(1)} %constant_dynamic-update-slice_fusion.refs_0_), channel_id=1, source_target_pairs={{0,4},{4,0},{8,12},{12,8},{16,20},{20,16},{24,28},{28,24},{1,5},{5... | collective-permute-start | bytes 3170312 | tf_op jit(solution)/shard_map/ppermute | solution.py:18
  86.4 40.6 %collective-permute-start.5 = (bf16[2064,256]{1,0:T(8,128)(2,1)}, bf16[2064,256]{1,0:T(8,128)(2,1)}, u32[]{:S(2)}, u32[]{:S(2)}) collective-permute-start(bf16[2064,256]{1,0:T(8,128)(2,1)} %collective-permute-done.4.refs_2_), channel_id=1, source_target_pairs={{0,4},{4,0},{8,12},{12,8},{16,20},{20,16},{24,28},{28,24},{1,5},{5... | collective-permute-start | bytes 3170312 | tf_op jit(solution)/shard_map/ppermute | solution.py:18
  86.5 40.8 %collective-permute-start.7 = (bf16[2064,256]{1,0:T(8,128)(2,1)}, bf16[2064,256]{1,0:T(8,128)(2,1)}, u32[]{:S(2)}, u32[]{:S(2)}) collective-permute-start(bf16[2064,256]{1,0:T(8,128)(2,1)} %collective-permute-done.6.refs_4_), channel_id=1, source_target_pairs={{0,4},{4,0},{8,12},{12,8},{16,20},{20,16},{24,28},{28,24},{1,5},{5... | collective-permute-start | bytes 3170312 | tf_op jit(solution)/shard_map/ppermute | solution.py:18
  86.9 40.6 %collective-permute-start.9 = (bf16[2064,256]{1,0:T(8,128)(2,1)}, bf16[2064,256]{1,0:T(8,128)(2,1)}, u32[]{:S(2)}, u32[]{:S(2)}) collective-permute-start(bf16[2064,256]{1,0:T(8,128)(2,1)} %collective-permute-done.8.refs_6_), channel_id=1, source_target_pairs={{0,4},{4,0},{8,12},{12,8},{16,20},{20,16},{24,28},{28,24},{1,5},{5... | collective-permute-start | bytes 3170312 | tf_op jit(solution)/shard_map/ppermute | solution.py:18
  101.5 19.8 %collective-permute-start.19 = (bf16[3,128,1152]{2,1,0:T(8,128)(2,1)}, bf16[3,128,1152]{2,1,0:T(8,128)(2,1)}, u32[]{:S(2)}, u32[]{:S(2)}) collective-permute-start(bf16[3,128,1152]{2,1,0:T(8,128)(2,1)} %pad_maximum_fusion.4.refs_0_), channel_id=1, source_target_pairs={{0,24},{4,28},{8,16},{12,20},{16,8},{20,12},{24,0},{28,4},{1,25},{... | collective-permute-start | bytes 2654216 | tf_op jit(solution)/shard_map/ppermute | solution.py:18
  121.3 28.6 %collective-permute-start.14 = (bf16[3,128,1152]{2,1,0:T(8,128)(2,1)}, bf16[3,128,1152]{2,1,0:T(8,128)(2,1)}, u32[]{:S(2)}, u32[]{:S(2)}) collective-permute-start(bf16[3,128,1152]{2,1,0:T(8,128)(2,1)} %pad_maximum_fusion.4.refs_0_), channel_id=1, source_target_pairs={{0,4},{4,0},{8,12},{12,8},{16,20},{20,16},{24,28},{28,24},{1,5},{5... | collective-permute-start | bytes 2654216 | tf_op jit(solution)/shard_map/ppermute | solution.py:18
  124.7 45.7 %collective-permute-start.22 = (bf16[256,1024]{1,0:T(8,128)(2,1)}, bf16[256,1024]{1,0:T(8,128)(2,1)}, u32[]{:S(2)}, u32[]{:S(2)}) collective-permute-start(bf16[256,1024]{1,0:T(8,128)(2,1)} %bitcast_convert_fusion.d_ref), channel_id=1, source_target_pairs={{0,1},{1,2},{2,3},{3,0},{4,5},{5,6},{6,7},{7,4},{8,9},{9,10},{10,1... | collective-permute-start | bytes 1572872 | tf_op jit(solution)/shard_map/ppermute | solution.py:23
  126.9 23.0 %collective-permute-start.16 = (bf16[3,128,1152]{2,1,0:T(8,128)(2,1)}, bf16[3,128,1152]{2,1,0:T(8,128)(2,1)}, u32[]{:S(2)}, u32[]{:S(2)}) collective-permute-start(bf16[3,128,1152]{2,1,0:T(8,128)(2,1)} %collective-permute-done.15.refs_2_), channel_id=1, source_target_pairs={{0,4},{4,0},{8,12},{12,8},{16,20},{20,16},{24,28},{28,24},{1,5},{5... | collective-permute-start | bytes 2654216 | tf_op jit(solution)/shard_map/ppermute | solution.py:18
  127.2 24.0 %collective-permute-start.18 = (bf16[3,128,1152]{2,1,0:T(8,128)(2,1)}, bf16[3,128,1152]{2,1,0:T(8,128)(2,1)}, u32[]{:S(2)}, u32[]{:S(2)}) collective-permute-start(bf16[3,128,1152]{2,1,0:T(8,128)(2,1)} %copy-done.38), channel_id=1, source_target_pairs={{0,4},{4,0},{8,12},{12,8},{16,20},{20,16},{24,28},{28,24},{1,5},{5... | collective-permute-start | bytes 2654216 | tf_op jit(solution)/shard_map/ppermute | solution.py:18
  127.5 24.0 %collective-permute-start.20 = (bf16[3,128,1152]{2,1,0:T(8,128)(2,1)}, bf16[3,128,1152]{2,1,0:T(8,128)(2,1)}, u32[]{:S(2)}, u32[]{:S(2)}) collective-permute-start(bf16[3,128,1152]{2,1,0:T(8,128)(2,1)} %collective-permute-done.19.refs_6_), channel_id=1, source_target_pairs={{0,4},{4,0},{8,12},{12,8},{16,20},{20,16},{24,28},{28,24},{1,5},{5... | collective-permute-start | bytes 2654216 | tf_op jit(solution)/shard_map/ppermute | solution.py:18
  149.9 21.2 %collective-permute-start.21 = (bf16[256,1024]{1,0:T(8,128)(2,1)}, bf16[256,1024]{1,0:T(8,128)(2,1)}, u32[]{:S(2)}, u32[]{:S(2)}) collective-permute-start(bf16[256,1024]{1,0:T(8,128)(2,1)} %multiply_convert_fusion.n_ref), channel_id=1, source_target_pairs={{0,1},{1,2},{2,3},{3,0},{4,5},{5,6},{6,7},{7,4},{8,9},{9,10},{10,1... | collective-permute-start | bytes 1572872 | tf_op jit(solution)/shard_map/ppermute | solution.py:23
  149.9 67.5 %collective-permute-start.25 = (bf16[256,1024]{1,0:T(8,128)(2,1)}, bf16[256,1024]{1,0:T(8,128)(2,1)}, u32[]{:S(2)}, u32[]{:S(2)}) collective-permute-start(bf16[256,1024]{1,0:T(8,128)(2,1)} %bitcast_convert_fusion.d_ref), channel_id=1, source_target_pairs={{0,2},{1,3},{2,0},{3,1},{4,6},{5,7},{6,4},{7,5},{8,10},{9,11},{10,... | collective-permute-start | bytes 1572872 | tf_op jit(solution)/shard_map/ppermute | solution.py:23
  151.2 87.3 %collective-permute-start.28 = (bf16[256,1024]{1,0:T(8,128)(2,1)}, bf16[256,1024]{1,0:T(8,128)(2,1)}, u32[]{:S(2)}, u32[]{:S(2)}) collective-permute-start(bf16[256,1024]{1,0:T(8,128)(2,1)} %bitcast_convert_fusion.d_ref), channel_id=1, source_target_pairs={{0,3},{1,0},{2,1},{3,2},{4,7},{5,4},{6,5},{7,6},{8,11},{9,8},{10,9... | collective-permute-start | bytes 1572872 | tf_op jit(solution)/shard_map/ppermute | solution.py:23
  158.2 70.4 %collective-permute-start.24 = (bf16[256,1024]{1,0:T(8,128)(2,1)}, bf16[256,1024]{1,0:T(8,128)(2,1)}, u32[]{:S(2)}, u32[]{:S(2)}) collective-permute-start(bf16[256,1024]{1,0:T(8,128)(2,1)} %multiply_convert_fusion.n_ref), channel_id=1, source_target_pairs={{0,2},{1,3},{2,0},{3,1},{4,6},{5,7},{6,4},{7,5},{8,10},{9,11},{10,... | collective-permute-start | bytes 1572872 | tf_op jit(solution)/shard_map/ppermute | solution.py:23
  170.4 68.1 %collective-permute-start.27 = (bf16[256,1024]{1,0:T(8,128)(2,1)}, bf16[256,1024]{1,0:T(8,128)(2,1)}, u32[]{:S(2)}, u32[]{:S(2)}) collective-permute-start(bf16[256,1024]{1,0:T(8,128)(2,1)} %multiply_convert_fusion.n_ref), channel_id=1, source_target_pairs={{0,3},{1,0},{2,1},{3,2},{4,7},{5,4},{6,5},{7,6},{8,11},{9,8},{10,9... | collective-permute-start | bytes 1572872 | tf_op jit(solution)/shard_map/ppermute | solution.py:23
  281.1 12.5 %collective-permute-start.30 = (bf16[256,1024]{1,0:T(8,128)(2,1)}, bf16[256,1024]{1,0:T(8,128)(2,1)S(1)}, u32[]{:S(2)}, u32[]{:S(2)}) collective-permute-start(bf16[256,1024]{1,0:T(8,128)(2,1)} %get-tuple-element.50), channel_id=1, source_target_pairs={{0,3},{1,0},{2,1},{3,2},{4,7},{5,4},{6,5},{7,6},{8,11},{9,8},{10,9... | collective-permute-start | bytes 1572872 | tf_op jit(solution)/shard_map/ppermute | solution.py:23
  281.1 36.7 %collective-permute-start.31 = (bf16[256,1024]{1,0:T(8,128)(2,1)}, bf16[256,1024]{1,0:T(8,128)(2,1)S(1)}, u32[]{:S(2)}, u32[]{:S(2)}) collective-permute-start(bf16[256,1024]{1,0:T(8,128)(2,1)} %get-tuple-element.51), channel_id=1, source_target_pairs={{0,2},{1,3},{2,0},{3,1},{4,6},{5,7},{6,4},{7,5},{8,10},{9,11},{10,... | collective-permute-start | bytes 1572872 | tf_op jit(solution)/shard_map/ppermute | solution.py:23
  284.2 67.3 %collective-permute-start.32 = (bf16[256,1024]{1,0:T(8,128)(2,1)}, bf16[256,1024]{1,0:T(8,128)(2,1)S(1)}, u32[]{:S(2)}, u32[]{:S(2)}) collective-permute-start(bf16[256,1024]{1,0:T(8,128)(2,1)} %get-tuple-element.52), channel_id=1, source_target_pairs={{0,1},{1,2},{2,3},{3,0},{4,5},{5,6},{6,7},{7,4},{8,9},{9,10},{10,1... | collective-permute-start | bytes 1572872 | tf_op jit(solution)/shard_map/ppermute | solution.py:23
  286.6 74.5 %collective-permute-start.23 = (bf16[256,1024]{1,0:T(8,128)(2,1)}, bf16[256,1024]{1,0:T(8,128)(2,1)S(1)}, u32[]{:S(2)}, u32[]{:S(2)}) collective-permute-start(bf16[256,1024]{1,0:T(8,128)(2,1)} %get-tuple-element.46), channel_id=1, source_target_pairs={{0,3},{1,0},{2,1},{3,2},{4,7},{5,4},{6,5},{7,6},{8,11},{9,8},{10,9... | collective-permute-start | bytes 1572872 | tf_op jit(solution)/shard_map/ppermute | solution.py:23
  286.6 76.2 %collective-permute-start.26 = (bf16[256,1024]{1,0:T(8,128)(2,1)}, bf16[256,1024]{1,0:T(8,128)(2,1)S(1)}, u32[]{:S(2)}, u32[]{:S(2)}) collective-permute-start(bf16[256,1024]{1,0:T(8,128)(2,1)} %get-tuple-element.47), channel_id=1, source_target_pairs={{0,2},{1,3},{2,0},{3,1},{4,6},{5,7},{6,4},{7,5},{8,10},{9,11},{10,... | collective-permute-start | bytes 1572872 | tf_op jit(solution)/shard_map/ppermute | solution.py:23
  293.7 57.9 %copy-start.11 = (f32[256,1024]{1,0:T(8,128)S(1)}, f32[256,1024]{1,0:T(8,128)}, u32[]{:S(2)}) copy-start(f32[256,1024]{1,0:T(8,128)} %copy-done.10) | copy-start | bytes 3145732
  293.7 57.9 %copy-start.36 = (bf16[256,1024]{1,0:T(8,128)(2,1)S(1)}, bf16[256,1024]{1,0:T(8,128)(2,1)}, u32[]{:S(2)}) copy-start(bf16[256,1024]{1,0:T(8,128)(2,1)} %get-tuple-element.49) | copy-start | bytes 1572868
  293.7 80.3 %collective-permute-start.29 = (bf16[256,1024]{1,0:T(8,128)(2,1)S(1)}, bf16[256,1024]{1,0:T(8,128)(2,1)S(1)}, u32[]{:S(2)}, u32[]{:S(2)}) collective-permute-start(bf16[256,1024]{1,0:T(8,128)(2,1)S(1)} %copy-done.52), channel_id=1, source_target_pairs={{0,1},{1,2},{2,3},{3,0},{4,5},{5,6},{6,7},{7,4},{8,9},{9,10},{10,1... | collective-permute-start | bytes 1572872 | tf_op jit(solution)/shard_map/ppermute | solution.py:23
  298.2 75.7 %copy-start.18 = (f32[8,32,1024]{2,1,0:T(8,128)S(1)}, f32[8,32,1024]{2,1,0:T(8,128)}, u32[]{:S(2)}) copy-start(f32[8,32,1024]{2,1,0:T(8,128)} %copy-done.17) | copy-start | bytes 3145732
  298.2 75.7 %copy-start.39 = (bf16[256,1024]{1,0:T(8,128)(2,1)S(1)}, bf16[256,1024]{1,0:T(8,128)(2,1)}, u32[]{:S(2)}) copy-start(bf16[256,1024]{1,0:T(8,128)(2,1)} %get-tuple-element.45) | copy-start | bytes 1572868
  317.9 130.4 %collective-permute-start.44 = (bf16[4,1,3,128,1152]{3,4,2,1,0:T(8,128)(2,1)}, bf16[4,1,3,128,1152]{3,4,2,1,0:T(8,128)(2,1)}, u32[]{:S(2)}, u32[]{:S(2)}) collective-permute-start(bf16[4,1,3,128,1152]{3,4,2,1,0:T(8,128)(2,1)} %dynamic-slice_bitcast_fusion), channel_id=1, source_target_pairs={{0,4},{4,0},{8,12},{12,8},{16,20},{20,16},{24,28},{28,24},{1,5},{5... | collective-permute-start | bytes 10616840 | tf_op jit(solution)/shard_map/ppermute | solution.py:18
  375.5 14.4 %copy-start.8 = (f32[256,1024]{1,0:T(8,128)}, f32[256,1024]{1,0:T(8,128)S(1)}, u32[]{:S(2)}) copy-start(f32[256,1024]{1,0:T(8,128)S(1)} %get-tuple-element.139) | copy-start | bytes 3145732
  431.5 13.5 %copy-start.9 = (f32[256,1024]{1,0:T(8,128)S(1)}, f32[256,1024]{1,0:T(8,128)}, u32[]{:S(2)}) copy-start(f32[256,1024]{1,0:T(8,128)} %copy-done.8) | copy-start | bytes 3145732
  431.5 24.7 %collective-permute-start.37 = (bf16[4,1,4,528,256]{4,3,2,0,1:T(8,128)(2,1)}, bf16[4,1,4,528,256]{4,3,2,0,1:T(8,128)(2,1)}, u32[]{:S(2)}, u32[]{:S(2)}) collective-permute-start(bf16[4,1,4,528,256]{4,3,2,0,1:T(8,128)(2,1)} %fusion.3), channel_id=1, source_target_pairs={{0,4},{4,0},{8,12},{12,8},{16,20},{20,16},{24,28},{28,24},{1,5},{5... | collective-permute-start | bytes 12976136 | tf_op jit(solution)/shard_map/ppermute | solution.py:18
  433.4 5.1 collective-permute-start.33
  438.5 3.2 collective-permute-start.34
  441.7 2.9 collective-permute-start.35
  444.7 3.6 collective-permute-start.36
  452.6 20.1 %collective-permute-start.45 = (bf16[1,3,128,1152]{2,3,1,0:T(8,128)(2,1)S(1)}, bf16[1,3,128,1152]{2,3,1,0:T(8,128)(2,1)S(1)}, u32[]{:S(2)}, u32[]{:S(2)}) collective-permute-start(bf16[1,3,128,1152]{2,3,1,0:T(8,128)(2,1)S(1)} %get-tuple-element.127), channel_id=1, source_target_pairs={{0,8},{4,12},{8,0},{12,4},{16,24},{20,28},{24,16},{28,20},{1,9},{5... | collective-permute-start | bytes 2654216 | tf_op jit(solution)/shard_map/ppermute | solution.py:18
  453.8 21.0 %collective-permute-start.46 = (bf16[1,3,128,1152]{2,3,1,0:T(8,128)(2,1)S(1)}, bf16[1,3,128,1152]{2,3,1,0:T(8,128)(2,1)S(1)}, u32[]{:S(2)}, u32[]{:S(2)}) collective-permute-start(bf16[1,3,128,1152]{2,3,1,0:T(8,128)(2,1)S(1)} %get-tuple-element.129), channel_id=1, source_target_pairs={{0,16},{4,20},{8,24},{12,28},{16,0},{20,4},{24,8},{28,12},{1,17},{... | collective-permute-start | bytes 2654216 | tf_op jit(solution)/shard_map/ppermute | solution.py:18
  455.1 37.5 %collective-permute-start.47 = (bf16[1,3,128,1152]{2,3,1,0:T(8,128)(2,1)S(1)}, bf16[1,3,128,1152]{2,3,1,0:T(8,128)(2,1)S(1)}, u32[]{:S(2)}, u32[]{:S(2)}) collective-permute-start(bf16[1,3,128,1152]{2,3,1,0:T(8,128)(2,1)S(1)} %get-tuple-element.128), channel_id=1, source_target_pairs={{0,24},{4,28},{8,16},{12,20},{16,8},{20,12},{24,0},{28,4},{1,25},{... | collective-permute-start | bytes 2654216 | tf_op jit(solution)/shard_map/ppermute | solution.py:18
  463.4 51.5 %collective-permute-start.38 = (bf16[1,4,528,256]{3,2,1,0:T(8,128)(2,1)}, bf16[1,4,528,256]{3,2,1,0:T(8,128)(2,1)}, u32[]{:S(2)}, u32[]{:S(2)}) collective-permute-start(bf16[1,4,528,256]{3,2,1,0:T(8,128)(2,1)} %get-tuple-element.124), channel_id=1, source_target_pairs={{0,8},{4,12},{8,0},{12,4},{16,24},{20,28},{24,16},{28,20},{1,9},{5... | collective-permute-start | bytes 3244040 | tf_op jit(solution)/shard_map/ppermute | solution.py:18
  464.5 51.2 %collective-permute-start.39 = (bf16[1,4,528,256]{3,2,1,0:T(8,128)(2,1)}, bf16[1,4,528,256]{3,2,1,0:T(8,128)(2,1)}, u32[]{:S(2)}, u32[]{:S(2)}) collective-permute-start(bf16[1,4,528,256]{3,2,1,0:T(8,128)(2,1)} %get-tuple-element.126), channel_id=1, source_target_pairs={{0,16},{4,20},{8,24},{12,28},{16,0},{20,4},{24,8},{28,12},{1,17},{... | collective-permute-start | bytes 3244040 | tf_op jit(solution)/shard_map/ppermute | solution.py:18
  472.6 66.4 %collective-permute-start.40 = (bf16[1,4,528,256]{3,2,1,0:T(8,128)(2,1)}, bf16[1,4,528,256]{3,2,1,0:T(8,128)(2,1)}, u32[]{:S(2)}, u32[]{:S(2)}) collective-permute-start(bf16[1,4,528,256]{3,2,1,0:T(8,128)(2,1)} %get-tuple-element.125), channel_id=1, source_target_pairs={{0,24},{4,28},{8,16},{12,20},{16,8},{20,12},{24,0},{28,4},{1,25},{... | collective-permute-start | bytes 3244040 | tf_op jit(solution)/shard_map/ppermute | solution.py:18
  541.9 5.9 %collective-permute-start.41 = (bf16[528,256]{1,0:T(8,128)(2,1)S(1)}, bf16[528,256]{1,0:T(8,128)(2,1)S(1)}, u32[]{:S(2)}, u32[]{:S(2)}) collective-permute-start(bf16[528,256]{1,0:T(8,128)(2,1)S(1)} %get-tuple-element.130), channel_id=1, source_target_pairs={{0,1},{1,2},{2,3},{3,0},{4,5},{5,6},{6,7},{7,4},{8,9},{9,10},{10,1... | collective-permute-start | bytes 811016 | tf_op jit(solution)/shard_map/ppermute | solution.py:23
  543.1 20.7 %collective-permute-start.42 = (bf16[528,256]{1,0:T(8,128)(2,1)S(1)}, bf16[528,256]{1,0:T(8,128)(2,1)S(1)}, u32[]{:S(2)}, u32[]{:S(2)}) collective-permute-start(bf16[528,256]{1,0:T(8,128)(2,1)S(1)} %get-tuple-element.132), channel_id=1, source_target_pairs={{0,2},{1,3},{2,0},{3,1},{4,6},{5,7},{6,4},{7,5},{8,10},{9,11},{10,... | collective-permute-start | bytes 811016 | tf_op jit(solution)/shard_map/ppermute | solution.py:23
  543.9 24.3 %collective-permute-start.43 = (bf16[528,256]{1,0:T(8,128)(2,1)S(1)}, bf16[528,256]{1,0:T(8,128)(2,1)S(1)}, u32[]{:S(2)}, u32[]{:S(2)}) collective-permute-start(bf16[528,256]{1,0:T(8,128)(2,1)S(1)} %get-tuple-element.131), channel_id=1, source_target_pairs={{0,3},{1,0},{2,1},{3,2},{4,7},{5,4},{6,5},{7,6},{8,11},{9,8},{10,9... | collective-permute-start | bytes 811016 | tf_op jit(solution)/shard_map/ppermute | solution.py:23
  (38 other events, 126.4 us)

commit v2 on v0

v2 whole, which is shorter than its diff:
```python
import functools
import jax
import jax.numpy as jnp
from jax import lax
from jax.experimental import pallas as pl
from jax.experimental.pallas import tpu as pltpu
from jax.sharding import PartitionSpec as P

EPS = 1e-05
INNER = 8
BF = jnp.bfloat16
F32 = jnp.float32
VMEM_LIMIT = 26 << 20


def dp_swap(value, step):
    size = lax.axis_size("dp")
    hop = step * (size // INNER)
    return lax.ppermute(value, "dp", [(i, i ^ hop) for i in range(size)])


def z_shift(value, step):
    size = lax.axis_size("tensor")
    return lax.ppermute(value, "tensor", [(i, (i + step) % size) for i in range(size)])


def after(value, *events):
    return lax.optimization_barrier((value,) + events)[0]


def mm(a, b):
    return lax.dot_general(a, b, (((1,), (0,)), ((), ())), preferred_element_type=F32)


def mm_nt(a, b):
    return lax.dot_general(a, b, (((1,), (1,)), ((), ())), preferred_element_type=F32)


def mm_tn(a, b):
    return lax.dot_general(a, b, (((0,), (0,)), ((), ())), preferred_element_type=F32)


def shape(*dims, dtype=BF):
    return jax.ShapeDtypeStruct(dims, dtype)


def whole_call(kernel, name, outs, args, scalars=0, hbm=0, scratch=(), flops=0, extra=0):
    specs = [pl.BlockSpec(memory_space=pltpu.SMEM)] * scalars
    specs += [pl.BlockSpec(memory_space=pl.ANY)] * hbm
    specs += [pl.BlockSpec(memory_space=pltpu.VMEM)] * (len(args) - scalars - hbm)
    moved = sum(a.size * a.dtype.itemsize for a in args) + sum(
        o.size * jnp.dtype(o.dtype).itemsize for o in outs
    )
    return pl.pallas_call(
        kernel,
        out_shape=outs,
        in_specs=specs,
        out_specs=[pl.BlockSpec(memory_space=pltpu.VMEM)] * len(outs),
        scratch_shapes=list(scratch),
        compiler_params=pltpu.CompilerParams(vmem_limit_bytes=VMEM_LIMIT),
        cost_estimate=pl.CostEstimate(flops=flops, bytes_accessed=moved, transcendentals=extra),
        name=name,
    )(*args)


def pair_up(own, other):
    return [piece for pair in zip(own, other) for piece in pair]


def plane_gather(local):
    own = [local] + [dp_swap(local, 2 * kq) for kq in (1, 2, 3)]
    return pair_up(own, [dp_swap(piece, 1) for piece in own])


def place_mixer_kernel(with_small, idx_ref, *refs):
    pieces, outs, sems = refs[:8], refs[8:-1], refs[-1]
    me, z = idx_ref[0], idx_ref[1]
    n_z = outs[0].shape[1] // 256
    rows = outs[0].shape[0] // 8
    copies = []
    for k in range(8):
        at = pl.multiple_of(jnp.bitwise_xor(me, k) * rows, rows)
        for s in range(n_z):
            col = pl.multiple_of(lax.rem(z + n_z - s, n_z) * 256, 256)
            for st in range(2):
                copies.append(
                    pltpu.make_async_copy(
                        pieces[k].at[pl.ds((s * 2 + st) * rows, rows)],
                        outs[st].at[pl.ds(at, rows), pl.ds(col, 256)],
                        sems.at[k, s * 2 + st],
                    )
                )
        if with_small:
            copies.append(
                pltpu.make_async_copy(
                    pieces[k].at[pl.ds(2 * n_z * rows, 16), pl.ds(0, rows)],
                    outs[2].at[:, pl.ds(at, rows)],
                    sems.at[k, 2 * n_z],
                )
            )
    for copy in copies:
        copy.start()
    for copy in copies:
        copy.wait()


def place_mixer(index, pieces, width, n_z, with_small):
    outs = [shape(width, n_z * 256)] * 2 + ([shape(16, width)] if with_small else [])
    return whole_call(
        functools.partial(place_mixer_kernel, with_small),
        "place_small" if with_small else "place_mixer",
        outs,
        (index, *pieces),
        scalars=1,
        hbm=8,
        scratch=[pltpu.SemaphoreType.DMA((8, 2 * n_z + 1))],
    )


def place_ffn_kernel(idx_ref, *refs):
    pieces, (gu_ref, down_ref), sems = refs[:8], refs[8:10], refs[10]
    me = idx_ref[0]
    rows = gu_ref.shape[0] // 8
    split = gu_ref.shape[1]
    copies = []
    for k in range(8):
        at = pl.ds(pl.multiple_of(jnp.bitwise_xor(me, k) * rows, rows), rows)
        copies.append(
            pltpu.make_async_copy(pieces[k].at[:, pl.ds(0, split)], gu_ref.at[at], sems.at[k, 0])
        )
        copies.append(
            pltpu.make_async_copy(
                pieces[k].at[:, pl.ds(split, split // 2)], down_ref.at[at], sems.at[k, 1]
            )
        )
    for copy in copies:
        copy.start()
    for copy in copies:
        copy.wait()


def place_ffn(index, pieces):
    rows, columns = pieces[0].shape
    return whole_call(
        place_ffn_kernel,
        "place_ffn",
        [shape(8 * rows, columns // 3 * 2), shape(8 * rows, columns // 3)],
        (index, *pieces),
        scalars=1,
        hbm=8,
        scratch=[pltpu.SemaphoreType.DMA((8, 2))],
    )


def ffn_kernel(n_ref, d_ref, gu_ref, down_ref, dn_ref, part_ref, hid_ref, dgu_ref):
    units = down_ref.shape[1]
    both = mm(n_ref[...], gu_ref[...])
    gate, up = both[:, :units], both[:, units:]
    sig = jax.nn.sigmoid(gate)
    silu = gate * sig
    hidden = (silu * up).astype(BF)
    hid_ref[...] = hidden
    d_hidden = mm(d_ref[...], down_ref[...])
    dgu_ref[:, :units] = (d_hidden * up * (sig * (1.0 + gate * (1.0 - sig)))).astype(BF)
    dgu_ref[:, units:] = (d_hidden * silu).astype(BF)
    dn_ref[...] = mm_nt(dgu_ref[...], gu_ref[...]).astype(BF)
    part_ref[...] = mm_nt(hidden, down_ref[...]).astype(BF)


def ffn_piece(normed, d_out, w_gu, w_down):
    tokens, width = normed.shape
    units = w_down.shape[1]
    return whole_call(
        ffn_kernel,
        "ffn_piece",
        [shape(tokens, width)] * 2 + [shape(tokens, units), shape(tokens, 2 * units)],
        (normed, d_out, w_gu, w_down),
        flops=12 * tokens * width * units,
        extra=tokens * units,
    )


def norm_scale(value):
    return lax.rsqrt(jnp.mean(value * value, axis=-1, keepdims=True) + EPS)


def norm_back(d_normed, value, scale, gain):
    weighted = d_normed * gain
    d_value = scale * weighted - value * (scale * scale * scale) * jnp.mean(
        weighted * value, axis=-1, keepdims=True
    )
    return d_value, jnp.sum(d_normed * value * scale, axis=0, keepdims=True)


def halo_picks(tokens, own_len, halo):
    token = lax.broadcasted_iota(jnp.int32, (tokens, halo), 0)
    slot = lax.broadcasted_iota(jnp.int32, (tokens, halo), 1)
    run, pos = token // own_len, token % own_len
    one = jnp.logical_and(pos == 0, slot == 2 * run + 1)
    two = jnp.logical_and(pos < 2, slot == 2 * run + pos)
    return one.astype(BF), two.astype(BF)


def earlier(mixed, mixed_halo, own_len):
    tokens = mixed.shape[0]
    pick_one, pick_two = halo_picks(tokens, own_len, mixed_halo.shape[0])
    pos = lax.broadcasted_iota(jnp.int32, mixed.shape, 0) % own_len
    one = jnp.where(pos == 0, mm(pick_one, mixed_halo), pltpu.roll(mixed, 1, axis=0))
    two = jnp.where(pos < 2, mm(pick_two, mixed_halo), pltpu.roll(mixed, 2, axis=0))
    return one, two


def mixer_in_kernel(
    own_len, x_ref, xh_ref, small_ref, wb_ref, wu_ref, n_ref, nh_ref, b_ref, u_ref, bh_ref, uh_ref, mix_ref, mixh_ref, conv_ref
):
    gain = small_ref[0:1].astype(F32)
    x, xh = x_ref[...].astype(F32), xh_ref[...].astype(F32)
    n_ref[...] = (x * norm_scale(x) * gain).astype(BF)
    nh_ref[...] = (xh * norm_scale(xh) * gain).astype(BF)
    b_ref[...] = mm(n_ref[...], wb_ref[...])
    u_ref[...] = mm(n_ref[...], wu_ref[...])
    bh_ref[...] = mm(nh_ref[...], wb_ref[...])
    uh_ref[...] = mm(nh_ref[...], wu_ref[...])
    mix_ref[...] = (b_ref[...] * u_ref[...]).astype(BF)
    mixh_ref[...] = (bh_ref[...] * uh_ref[...]).astype(BF)
    mixed = mix_ref[...].astype(F32)
    one, two = earlier(mixed, mixh_ref[...], own_len)
    taps = [small_ref[2 + k : 3 + k].astype(F32) for k in range(3)]
    conv_ref[...] = taps[0] * two + taps[1] * one + taps[2] * mixed


def mixer_in(own_len, x, x_halo, small, w_b, w_u):
    (tokens, width), halo, ch = x.shape, x_halo.shape[0], w_b.shape[1]
    return whole_call(
        functools.partial(mixer_in_kernel, own_len),
        "mixer_in",
        [
            shape(tokens, width),
            shape(halo, width),
            shape(tokens, ch, dtype=F32),
            shape(tokens, ch, dtype=F32),
            shape(halo, ch, dtype=F32),
            shape(halo, ch, dtype=F32),
            shape(tokens, ch),
            shape(halo, ch),
            shape(tokens, ch, dtype=F32),
        ],
        (x, x_halo, small, w_b, w_u),
        flops=4 * tokens * width * ch,
    )


def mixer_out_kernel(x_ref, n_ref, conv_ref, small_ref, wc_ref, wo_ref, c_ref, gated_ref, mid_ref, n2_ref):
    c_ref[...] = mm(n_ref[...], wc_ref[...])
    gated_ref[...] = (c_ref[...] * conv_ref[...]).astype(BF)
    mid = x_ref[...].astype(F32) + mm_nt(gated_ref[...], wo_ref[...])
    mid_ref[...] = mid
    n2_ref[...] = (mid * norm_scale(mid) * small_ref[1:2].astype(F32)).astype(BF)


def mixer_out(x, n_one, conv, small, w_c, w_o):
    (tokens, width), ch = x.shape, w_c.shape[1]
    return whole_call(
        mixer_out_kernel,
        "mixer_out",
        [
            shape(tokens, ch, dtype=F32),
            shape(tokens, ch),
            shape(tokens, width, dtype=F32),
            shape(tokens, width),
        ],
        (x, n_one, conv, small, w_c, w_o),
        flops=4 * tokens * width * ch,
    )


def mixer_back_kernel(own_len, n_parts, *refs):
    parts = refs[:n_parts]
    (mid_ref, dy_ref, x_ref, xh_ref, small_ref, b_ref, u_ref, c_ref, bh_ref, uh_ref, mix_ref, mixh_ref, conv_ref) = refs[
        n_parts : n_parts + 13
    ]
    wb_ref, wu_ref, wc_ref, wo_ref = refs[n_parts + 13 : n_parts + 17]
    dmix_ref, db_ref, du_ref, dc_ref, dbh_ref, duh_ref, gin_ref, dxh_ref, sg_ref = refs[n_parts + 17 :]
    gain_one, gain_two = small_ref[0:1].astype(F32), small_ref[1:2].astype(F32)
    taps = [small_ref[2 + k : 3 + k].astype(F32) for k in range(3)]
    d_n2 = parts[0][...].astype(F32)
    for part in parts[1:]:
        d_n2 = d_n2 + part[...].astype(F32)
    mid = mid_ref[...]
    d_mid, g_two = norm_back(d_n2, mid, norm_scale(mid), gain_two)
    d_mid = d_mid + dy_ref[...].astype(F32)
    dmix_ref[...] = d_mid.astype(BF)
    d_gated = mm(dmix_ref[...], wo_ref[...])
    dc_ref[...] = (d_gated * conv_ref[...]).astype(BF)
    d_conv = d_gated * c_ref[...]
    mixed = mix_ref[...].astype(F32)
    one, two = earlier(mixed, mixh_ref[...], own_len)
    tap_rows = [jnp.sum(d_conv * view, axis=0, keepdims=True) for view in (two, one, mixed)]
    tokens = mixed.shape[0]
    pos = lax.broadcasted_iota(jnp.int32, mixed.shape, 0) % own_len
    d_mixed = taps[2] * d_conv
    d_mixed = d_mixed + taps[1] * jnp.where(pos < own_len - 1, pltpu.roll(d_conv, tokens - 1, axis=0), 0.0)
    d_mixed = d_mixed + taps[0] * jnp.where(pos < own_len - 2, pltpu.roll(d_conv, tokens - 2, axis=0), 0.0)
    db_ref[...] = (d_mixed * u_ref[...]).astype(BF)
    du_ref[...] = (d_mixed * b_ref[...]).astype(BF)
    pick_one, pick_two = halo_picks(tokens, own_len, mixh_ref.shape[0])
    low = d_conv.astype(BF)
    d_halo = taps[1] * mm_tn(pick_one, low) + taps[0] * mm_tn(pick_two, low)
    dbh_ref[...] = (d_halo * uh_ref[...]).astype(BF)
    duh_ref[...] = (d_halo * bh_ref[...]).astype(BF)
    d_n1 = mm_nt(db_ref[...], wb_ref[...]) + mm_nt(du_ref[...], wu_ref[...]) + mm_nt(dc_ref[...], wc_ref[...])
    x, xh = x_ref[...].astype(F32), xh_ref[...].astype(F32)
    d_x, g_one = norm_back(d_n1, x, norm_scale(x), gain_one)
    gin_ref[...] = d_x + d_mid
    d_nh = mm_nt(dbh_ref[...], wb_ref[...]) + mm_nt(duh_ref[...], wu_ref[...])
    d_xh, g_halo = norm_back(d_nh, xh, norm_scale(xh), gain_one)
    dxh_ref[...] = d_xh.astype(BF)
    for row, value in enumerate([g_one + g_halo, g_two] + tap_rows):
        sg_ref[row : row + 1] = value
    sg_ref[5:8] = jnp.zeros((3, sg_ref.shape[1]), F32)


def mixer_back(own_len, parts, saved, weights):
    (tokens, width), ch = parts[0].shape, weights[0].shape[1]
    halo = saved[3].shape[0]
    return whole_call(
        functools.partial(mixer_back_kernel, own_len, len(parts)),
        "mixer_back",
        [shape(tokens, width)]
        + [shape(tokens, ch)] * 3
        + [shape(halo, ch)] * 2
        + [shape(tokens, width, dtype=F32), shape(halo, width), shape(8, width, dtype=F32)],
        (*parts, *saved, *weights),
        flops=8 * tokens * width * ch,
    )


def mixer_grad_kernel(with_halo, idx_ref, *refs):
    n_in = 7 if with_halo else 4
    ins, away_ref, home_ref = refs[:n_in], refs[n_in], refs[n_in + 1]
    me = idx_ref[0]
    quad, core = me // 2, lax.rem(me, 2)
    n_z, ch = away_ref.shape[1], away_ref.shape[3]
    rows = ins[0].shape[1] // 8

    @pl.loop(0, 4)
    def _(kq):
        chip = jnp.bitwise_xor(quad, kq) * 2
        away = pl.multiple_of((chip + 1 - core) * rows, rows)
        home = pl.multiple_of((chip + core) * rows, rows)
        for st in range(2):
            left_ref, right_ref = ins[2 * st], ins[2 * st + 1]
            left = jnp.concatenate([left_ref[:, pl.ds(away, rows)], left_ref[:, pl.ds(home, rows)]], axis=1)
            grad = mm_tn(left, right_ref[...])
            if with_halo:
                nh_ref = ins[4]
                left = jnp.concatenate([nh_ref[:, pl.ds(away, rows)], nh_ref[:, pl.ds(home, rows)]], axis=1)
                grad = grad + mm_tn(left, ins[5][:, st * n_z * ch : (st + 1) * n_z * ch])
            grad = grad.astype(BF)
            for z in range(n_z):
                cols = slice(z * ch, (z + 1) * ch)
                away_ref[kq, z, st * rows : (st + 1) * rows] = grad[:rows, cols]
                home_ref[kq, z, st * rows : (st + 1) * rows] = grad[rows:, cols]
        if with_halo:
            for ref, at in ((away_ref, away), (home_ref, home)):
                values = ins[6][:, pl.ds(at, rows)]
                values = jnp.concatenate([values, jnp.zeros_like(values)], axis=0)
                values = jnp.concatenate([values] + [jnp.zeros_like(values)] * (ch // rows - 1), axis=1)
                for z in range(n_z):
                    ref[kq, z, 2 * rows :] = values.astype(BF)


def mixer_grads(index, ins, n_z, rows, with_halo):
    ch = ins[1].shape[1] // n_z
    extra = 16 if with_halo else 0
    outs = [shape(4, n_z, 2 * rows + extra, ch)] * 2
    return whole_call(
        functools.partial(mixer_grad_kernel, with_halo),
        "grads_in" if with_halo else "grads_out",
        outs,
        (index, *ins),
        scalars=1,
        flops=4 * ins[0].size * ins[1].shape[1],
    )


def ffn_grad_kernel(first, count, idx_ref, n_ref, d_ref, hid_ref, dgu_ref, away_ref, home_ref):
    me = idx_ref[0]
    quad, core = me // 2, lax.rem(me, 2)
    rows = n_ref.shape[1] // 8
    split = dgu_ref.shape[1]

    @pl.loop(0, count)
    def _(i):
        chip = jnp.bitwise_xor(quad, first - i) * 2
        away = pl.multiple_of((chip + 1 - core) * rows, rows)
        home = pl.multiple_of((chip + core) * rows, rows)
        left = jnp.concatenate([n_ref[:, pl.ds(away, rows)], n_ref[:, pl.ds(home, rows)]], axis=1)
        grad = mm_tn(left, dgu_ref[...]).astype(BF)
        away_ref[i, :, :split] = grad[:rows]
        home_ref[i, :, :split] = grad[rows:]
        left = jnp.concatenate([d_ref[:, pl.ds(away, rows)], d_ref[:, pl.ds(home, rows)]], axis=1)
        grad = mm_tn(left, hid_ref[...]).astype(BF)
        away_ref[i, :, split:] = grad[:rows]
        home_ref[i, :, split:] = grad[rows:]


def ffn_grads(index, first, count, n_all, d_all, hid_all, dgu_all):
    rows = n_all.shape[1] // 8
    columns = hid_all.shape[1] + dgu_all.shape[1]
    return whole_call(
        functools.partial(ffn_grad_kernel, first, count),
        "ffn_grads",
        [shape(count, rows, columns)] * 2,
        (index, n_all, d_all, hid_all, dgu_all),
        scalars=1,
        flops=count * 4 * rows * n_all.shape[0] * columns,
    )


def plane_reduce(halves):
    arrived = {kq: dp_swap(halves[kq], 2 * kq) for kq in (3, 1, 2)}
    return halves[0].astype(F32) + arrived[1].astype(F32) + arrived[2].astype(F32) + arrived[3].astype(F32)


def body(
    layer_in,
    cotangent,
    row_counts,
    tail_tokens,
    row_order,
    gain_one,
    w_in,
    kernel,
    w_out,
    gain_two,
    w_gu,
    w_down,
):
    row_count, own_len, width = layer_in.shape
    n_dp, n_z = lax.axis_size("dp"), lax.axis_size("tensor")
    outer = n_dp // INNER
    me, z = lax.axis_index("dp"), lax.axis_index("tensor")
    me_in = me // outer
    row_len = own_len * n_z
    channels = w_in.shape[2]
    reach = kernel.shape[0] - 1
    tokens = row_count * own_len
    block = width // INNER
    units = w_down.shape[0]
    index = jnp.stack([me_in, z]).astype(jnp.int32)

    given = lax.dynamic_slice_in_dim(row_order, me * row_count, row_count)
    starts = jnp.cumsum(row_counts) - row_counts
    ends = starts + row_counts - 1
    is_first = jnp.any(starts[None, :] == given[:, None], axis=1)
    at_end = ends[None, :] == given[:, None]
    row_valid = jnp.where(
        jnp.any(at_end, axis=1),
        jnp.sum(jnp.where(at_end, tail_tokens[None, :], 0), axis=1),
        row_len,
    )
    positions = z * own_len + jnp.arange(own_len, dtype=jnp.int32)
    valid = positions[None, :] < row_valid[:, None]

    small = jnp.concatenate([gain_one[None], gain_two[None], kernel], axis=0)
    w_b, w_c, w_u = (w_in[:, st] for st in range(3))
    mix_bu = jnp.stack([w_b, w_u])
    mix_co = jnp.stack([w_c, w_out.T])
    ffn_own = jnp.concatenate([w_gu[:, 0], w_gu[:, 1], w_down.T], axis=1)
    groups = [[i * outer + o for o in range(outer)] for i in range(INNER)]
    if outer > 1:
        wide = functools.partial(lax.all_gather, axis_name="dp", tiled=True, axis_index_groups=groups)
        mix_bu, mix_co, ffn_own = wide(mix_bu, axis=1), wide(mix_co, axis=1), wide(ffn_own, axis=0)
        small = wide(small, axis=1)
    n_small = small.shape[0]
    small_rows = jnp.pad(small, ((0, 16 - n_small), (0, channels - block)))
    bu_rows, co_rows = (m.reshape(2 * block, channels) for m in (mix_bu, mix_co))

    bu_set = [bu_rows] + [z_shift(bu_rows, s) for s in range(1, n_z)]
    bu_pieces = plane_gather(jnp.concatenate(bu_set + [small_rows], axis=0))
    co_set = [co_rows] + [z_shift(co_rows, s) for s in range(1, n_z)]
    co_pieces = plane_gather(jnp.concatenate(co_set, axis=0))
    w_b, w_u, small_all = place_mixer(index, bu_pieces, width, n_z, True)
    w_c, w_o = place_mixer(index, co_pieces, width, n_z, False)
    w_gu_all, w_down_all = place_ffn(index, plane_gather(ffn_own))

    before = z_shift(layer_in[:, own_len - reach :].reshape(row_count, reach * width), 1)
    every = before[None]
    if outer > 1:
        every = lax.all_gather(before, "dp", axis=0, axis_index_groups=groups)
    every = every[None]
    for step in (1, 2, 4):
        every = jnp.concatenate([every, dp_swap(every, step)], axis=0)
    slots = INNER * outer * row_count
    rel = jnp.bitwise_xor(me_in, jnp.arange(INNER, dtype=jnp.int32))
    slot_rows = row_order.reshape(INNER, outer * row_count)[rel].reshape(slots)
    before_mask = jnp.logical_and(
        slot_rows[None, :] == (given - 1)[:, None], jnp.logical_not(is_first)[:, None]
    )
    before_mask = jnp.logical_and(before_mask, z == 0).astype(BF)
    crossed = mm(before_mask, every.reshape(slots, reach * width))
    x_halo = jnp.where(z == 0, crossed.astype(BF), before).reshape(row_count * reach, width)

    d_ffn = jnp.where(valid[:, :, None], cotangent, jnp.zeros_like(cotangent)).reshape(tokens, width)
    d_ffn_set = [d_ffn] + [z_shift(d_ffn, s) for s in range(1, n_z)]

    x_own = layer_in.reshape(tokens, width)
    n_one, n_halo, b_own, u_own, b_halo, u_halo, mixed, mixed_halo, conv = mixer_in(
        own_len, x_own, x_halo, small_all, w_b, w_u
    )
    c_own, gated, middle, n_two = mixer_out(x_own, n_one, conv, small_all, w_c, w_o)

    n_two_set = [n_two] + [z_shift(n_two, s) for s in range(1, n_z)]
    order = [0, 1, 3, 2] if n_z == 4 else list(range(n_z))
    runs = {s: ffn_piece(n_two_set[s], d_ffn_set[s], w_gu_all, w_down_all) for s in order}
    d_parts = [runs[0][0]] + [z_shift(runs[s][0], n_z - s) for s in order[1:]]

    n_all = jnp.concatenate([n_two_set[s] for s in order], axis=0)
    d_all = jnp.concatenate([d_ffn_set[s] for s in order], axis=0)
    hid_all = jnp.concatenate([runs[s][2] for s in order], axis=0)
    dgu_all = jnp.concatenate([runs[s][3] for s in order], axis=0)
    away, home = ffn_grads(index, 3, 4, n_all, d_all, hid_all, dgu_all)
    other = dp_swap(away, 1)
    halves = [(home[3 - kq].astype(F32) + other[3 - kq].astype(F32)).astype(BF) for kq in range(4)]
    ffn_total = plane_reduce(halves)

    d_mix, d_b, d_u, d_c, d_b_halo, d_u_halo, grad_mid, d_x_halo, small_grads = mixer_back(
        own_len,
        d_parts,
        (middle, d_ffn, x_own, x_halo, small_all, b_own, u_own, c_own, b_halo, u_halo, mixed, mixed_halo, conv),
        (w_b, w_u, w_c, w_o),
    )
    co_away, co_home = mixer_grads(index, (n_one, d_c, d_mix, gated), n_z, block, False)
    d_bu_halo = jnp.concatenate([d_b_halo, d_u_halo], axis=1)
    bu_away, bu_home = mixer_grads(
        index, (n_one, d_b, n_one, d_u, n_halo, d_bu_halo, small_grads), n_z, block, True
    )

    def mixer_reduce(away, home):
        other = dp_swap(away, 1)
        halves = [(home[kq].astype(F32) + other[kq].astype(F32)).astype(BF) for kq in range(4)]
        plane = plane_reduce(halves).astype(BF)
        total = lax.dynamic_index_in_dim(plane, z, 0, keepdims=False).astype(F32)
        for s in range(1, n_z):
            piece = lax.dynamic_index_in_dim(plane, lax.rem(z + s, n_z), 0, keepdims=False)
            total = total + z_shift(piece, s).astype(F32)
        return total

    co_total = mixer_reduce(co_away, co_home)
    bu_total = mixer_reduce(bu_away, bu_home)

    ffn_sum = runs[0][1].astype(F32)
    for s in order[1:]:
        ffn_sum = ffn_sum + z_shift(runs[s][1], n_z - s).astype(F32)
    layer_out = (middle + ffn_sum).astype(BF).reshape(row_count, own_len, width)

    back = d_x_halo.reshape(row_count, reach * width)
    spread = mm_tn(before_mask, back).astype(BF).reshape(INNER, outer * row_count, reach * width)
    for step in (4, 2, 1):
        spread = (spread[:step].astype(F32) + dp_swap(spread[step:], step).astype(F32)).astype(BF)
    returned = spread[0]
    if outer > 1:
        returned = lax.psum_scatter(
            returned, "dp", scatter_dimension=0, tiled=True, axis_index_groups=groups
        )
    returned = z_shift(jnp.where(z == 0, returned, back), n_z - 1)
    returned = returned.astype(F32).reshape(row_count, reach, width)
    grad_in = grad_mid.reshape(row_count, own_len, width)
    grad_in = grad_in + jnp.pad(returned, ((0, 0), (own_len - reach, 0), (0, 0)))

    if outer > 1:
        narrow = functools.partial(
            lax.psum_scatter, axis_name="dp", tiled=True, axis_index_groups=groups
        )
        grad_bu = narrow(bu_total[: 2 * block].reshape(2, block, channels), scatter_dimension=1)
        grad_co = narrow(co_total.reshape(2, block, channels), scatter_dimension=1)
        grad_small = narrow(bu_total[2 * block : 2 * block + n_small, :block], scatter_dimension=1)
        ffn_total = narrow(ffn_total, scatter_dimension=0)
    else:
        grad_bu = bu_total[: 2 * block].reshape(2, block, channels)
        grad_co = co_total.reshape(2, block, channels)
        grad_small = bu_total[2 * block : 2 * block + n_small, :block]
    return (
        layer_out,
        grad_in.astype(BF),
        grad_small[0],
        jnp.stack([grad_bu[0], grad_co[0], grad_bu[1]], axis=1),
        grad_small[2:],
        grad_co[1].T,
        grad_small[1],
        jnp.stack([ffn_total[:, :units], ffn_total[:, units : 2 * units]], axis=1),
        ffn_total[:, 2 * units :].T,
    )


def solution(mesh):
    in_specs = (
        P("dp", "tensor", None),
        P("dp", "tensor", None),
        P(),
        P(),
        P(),
        P("dp"),
        P("dp", None, "tensor"),
        P(None, "dp"),
        P("tensor", "dp"),
        P("dp"),
        P("dp", None, "tensor"),
        P("tensor", "dp"),
    )
    out_specs = (
        P("dp", "tensor", None),
        P("dp", "tensor", None),
        P("dp"),
        P("dp", None, "tensor"),
        P(None, "dp"),
        P("tensor", "dp"),
        P("dp"),
        P("dp", None, "tensor"),
        P("tensor", "dp"),
    )
    return jax.shard_map(body, mesh=mesh, in_specs=in_specs, out_specs=out_specs, check_vma=False)
```

time: 826 us -> 435 us (0.53)
  waiting for transfers between devices: 622 us -> 184 us
  starting transfers between devices: 1.1 us -> 90.1 us
  matrix products: 77.7 us -> 1.45 us
  blocking collectives: 72 us -> 0 us
  Pallas kernels: 0 us -> 55.8 us
  local copies, waits for them, and re-layouts: 14.3 us -> 52.7 us
  other arithmetic: 22.8 us -> 40.2 us
  between operations: 14.9 us -> 1.67 us
    reduce_scatter x9 -> x0, waiting for transfers between devices: 382 us -> none  [the longest x4 133 us: reduce_rows(): lax.psum_scatter(value.astype(jnp.bfloat16), 'tensor', scatter_dimension=...]
    all_gather x7 -> x0, waiting for transfers between devices: 239 us -> none  [the longest x4 174 us: gather_rows(): return lax.all_gather(value, 'tensor', axis=1, tiled=True)]
    ppermute x0 -> x65, waiting for transfers between devices: none -> 184 us  [the longest x26 93 us: z_shift(): lax.ppermute(value, 'tensor', [(i, (i + step) % size) for i in range(size)])]
    ppermute x0 -> x65, starting transfers between devices: none -> 90.1 us  [the longest x26 60.7 us: z_shift(): lax.ppermute(value, 'tensor', [(i, (i + step) % size) for i in range(size)])]
    dot_general x14 -> x2, matrix products: 77.7 us -> 1.45 us  [the longest x1 1.11 us: mm(): lax.dot_general(a, b, (((1,), (0,)), ((), ())), preferred_element_type=F32)]
    pallas_call x0 -> x13, Pallas kernels: none -> 55.8 us  [whole_call(): pl.pallas_call(kernel, out_shape=outs, in_specs=specs, out_specs=[pl.Bloc...]
    all_gather x5 -> x0, blocking collectives: 47.1 us -> none  [the longest x1 10.4 us: mixer_weights(): lax.all_gather(gain_one, 'dp', axis=0, tiled=True)]
    unnamed x48 -> x137, local copies, waits for them, and re-layouts: 13.4 us -> 44.6 us
  transfers between devices with their start and end apart: 17 -> 65, of which waited for: 15 -> 27; matrix products, arithmetic and copies ran while one was open for 9% -> 12% of each run, Pallas kernels for 0% -> 8%
where the time goes in v2:
time: 435 us; the launch traced here: 426 us
  waiting for transfers between devices  184 us (42%)
  starting transfers between devices  90.1 us (21%)
  Pallas kernels  55.8 us (13%)
  local copies, waits for them, and re-layouts  52.7 us (12%)
  other arithmetic  40.2 us (9%)
    ppermute x26, waiting for transfers between devices, z_shift(): lax.ppermute(value, 'tensor', [(i, (i + step) % size) for i in range(size)])  93 us
    ppermute x39, waiting for transfers between devices, dp_swap(): return lax.ppermute(value, 'dp', [(i, i ^ hop) for i in range(size)])  91.1 us
    ppermute x26, starting transfers between devices, z_shift(): lax.ppermute(value, 'tensor', [(i, (i + step) % size) for i in range(size)])  60.7 us
    pallas_call x13, Pallas kernels, whole_call(): pl.pallas_call(kernel, out_shape=outs, in_specs=specs, out_specs=[pl.Bloc...  55.8 us
    unnamed x137, local copies, waits for them, and re-layouts  44.6 us
    ppermute x39, starting transfers between devices, dp_swap(): return lax.ppermute(value, 'dp', [(i, i ^ hop) for i in range(size)])  29.3 us
    concatenate x1, other arithmetic, body(): dgu_all = jnp.concatenate([runs[s][3] for s in order], axis=0)  10.6 us
  transfers between devices with their start and end apart: 65, of which 27 were waited for; matrix products, arithmetic and copies ran while one was open for 12% of the time, Pallas kernels for 8%

profile of v2, /device:TPU:0, one launch (start us, length us, event | category | flops | bytes accessed | tf_op | source)
XLA Modules:
  0.0 425.9 jit_solution(18395827825141738556)
XLA Ops:
  1.7 3.1 collective-permute-start.4
  4.8 2.6 collective-permute-start.5
  15.2 1.8 fusion.54
  17.1 2.5 collective-permute-done
  22.5 2.7 collective-permute-done.2
  25.2 4.3 %collective-permute-start.14 = (bf16[256,256]{1,0:T(8,128)(2,1)S(1)}, bf16[256,256]{1,0:T(8,128)(2,1)S(1)}, u32[]{:S(2)}, u32[]{:S(2)}) collective-permute-start(bf16[256,256]{1,0:T(8,128)(2,1)S(1)} %bitcast.133), channel_id=1, source_target_pairs={{0,1},{1,2},{2,3},{3,0},{4,5},{5,6},{6,7},{7,4},{8,9},{9,10},{10,1... | collective-permute-start | bytes 393224 | tf_op jit(solution)/shard_map/ppermute | solution.py:24
  32.8 6.7 %collective-permute-start.38 = (bf16[256,1024]{1,0:T(8,128)(2,1)S(1)}, bf16[256,1024]{1,0:T(8,128)(2,1)}, u32[]{:S(2)}, u32[]{:S(2)}) collective-permute-start(bf16[256,1024]{1,0:T(8,128)(2,1)S(1)} %bitcast.118), channel_id=1, source_target_pairs={{0,2},{1,3},{2,0},{3,1},{4,6},{5,7},{6,4},{7,5},{8,10},{9,11},{10,... | collective-permute-start | bytes 1572872 | tf_op jit(solution)/shard_map/ppermute | solution.py:24
  43.4 16.5 %collective-permute-done.38.d_ref = bf16[256,1024]{1,0:T(8,128)(2,1)} collective-permute-done((bf16[256,1024]{1,0:T(8,128)(2,1)S(1)}, bf16[256,1024]{1,0:T(8,128)(2,1)}, u32[]{:S(2)}, u32[]{:S(2)}) %collective-permute-start.38) | collective-permute-done | bytes 524320 | tf_op jit(solution)/shard_map/ppermute | solution.py:24
  62.9 3.4 collective-permute-done.20.refs_4_
  66.4 1.7 collective-permute-start.12
  71.6 1.8 copy.46
  73.5 3.8 collective-permute-done.8.refs_2_
  77.3 12.0 %collective-permute-done.10.refs_4_ = bf16[1040,256]{1,0:T(8,128)(2,1)} collective-permute-done((bf16[1040,256]{1,0:T(8,128)(2,1)S(1)}, bf16[1040,256]{1,0:T(8,128)(2,1)}, u32[]{:S(2)}, u32[]{:S(2)}) %collective-permute-start.10) | collective-permute-done | bytes 532512 | tf_op jit(solution)/shard_map/ppermute | solution.py:19
  105.3 2.7 place_mixer.1
  108.1 2.8 place_small.1
  110.9 2.5 mixer_in.1
  116.7 2.2 collective-permute-start.34
  118.9 15.5 %collective-permute-done.27.refs_4_ = bf16[128,3456]{1,0:T(8,128)(2,1)} collective-permute-done((bf16[128,3456]{1,0:T(8,128)(2,1)S(1)}, bf16[128,3456]{1,0:T(8,128)(2,1)}, u32[]{:S(2)}, u32[]{:S(2)}) %collective-permute-start.27) | collective-permute-done | bytes 884768 | tf_op jit(solution)/shard_map/ppermute | solution.py:19
  135.0 5.4 %collective-permute-done.37.n_ref = bf16[256,1024]{1,0:T(8,128)(2,1)S(1)} collective-permute-done((bf16[256,1024]{1,0:T(8,128)(2,1)S(1)}, bf16[256,1024]{1,0:T(8,128)(2,1)S(1)}, u32[]{:S(2)}, u32[]{:S(2)}) %collective-permute-start.37) | collective-permute-done | bytes 524320 | tf_op jit(solution)/shard_map/ppermute | solution.py:24
  140.8 11.6 %collective-permute-start.31 = (bf16[256,1024]{1,0:T(8,128)(2,1)S(1)}, bf16[256,1024]{1,0:T(8,128)(2,1)S(1)}, u32[]{:S(2)}, u32[]{:S(2)}) collective-permute-start(bf16[256,1024]{1,0:T(8,128)(2,1)S(1)} %get-tuple-element.68.n_ref), channel_id=1, source_target_pairs={{0,1},{1,2},{2,3},{3,0},{4,5},{5,6},{6,7},{7,4},{8,9},{9,10},{10,1... | collective-permute-start | bytes 1572872 | tf_op jit(solution)/shard_map/ppermute | solution.py:24
  152.4 2.9 pad_maximum_fusion.3.d_ref
  155.2 10.6 %collective-permute-done.31.n_ref = bf16[256,1024]{1,0:T(8,128)(2,1)S(1)} collective-permute-done((bf16[256,1024]{1,0:T(8,128)(2,1)S(1)}, bf16[256,1024]{1,0:T(8,128)(2,1)S(1)}, u32[]{:S(2)}, u32[]{:S(2)}) %collective-permute-start.31) | collective-permute-done | bytes 524320 | tf_op jit(solution)/shard_map/ppermute | solution.py:24
  167.3 2.4 place_ffn.1
  169.7 2.2 copy-done.34
  171.9 2.3 copy-done.35
  174.3 4.3 %ffn_piece.4 = (bf16[256,1024]{1,0:T(8,128)(2,1)S(1)}, bf16[256,1024]{1,0:T(8,128)(2,1)S(1)}, bf16[256,1152]{1,0:T(8,128)(2,1)S(1)}, bf16[256,2304]{1,0:T(8,128)(2,1)S(1)}) custom-call(bf16[256,1024]{1,0:T(8,128)(2,1)S(1)} %get-tuple-element.68.n_ref, bf16[256,1024]{1,0:T(8,128)(2,1)S(1)} %bitcast.122, bf16[1024,2304]{1,0:T(8,128)(2,1)S(1)} %copy-done.35, ...), custom_call_target="tpu_custom_call" | custom-call | flops 3623878656 | bytes 10944512 | tf_op jit(solution)/shard_map/ffn_piece/pallas_call | solution.py:54
  179.3 2.3 copy-done.36
  181.7 5.3 %ffn_piece.5 = (bf16[256,1024]{1,0:T(8,128)(2,1)S(1)}, bf16[256,1024]{1,0:T(8,128)(2,1)S(1)}, bf16[256,1152]{1,0:T(8,128)(2,1)S(1)}, bf16[256,2304]{1,0:T(8,128)(2,1)S(1)}) custom-call(bf16[256,1024]{1,0:T(8,128)(2,1)S(1)} %collective-permute-done.31.n_ref, bf16[256,1024]{1,0:T(8,128)(2,1)} %collective-permute-done.32.d_ref, ...), custom_call_target="tpu_custom_call" | custom-call | flops 3623878656 | bytes 10944512 | tf_op jit(solution)/shard_map/ffn_piece/pallas_call | solution.py:54
  187.8 1.7 collective-permute-start.40
  189.5 2.3 copy-done.37
  191.9 5.3 %ffn_piece.6 = (bf16[256,1024]{1,0:T(8,128)(2,1)S(1)}, bf16[256,1024]{1,0:T(8,128)(2,1)S(1)}, bf16[256,1152]{1,0:T(8,128)(2,1)S(1)}, bf16[256,2304]{1,0:T(8,128)(2,1)S(1)}) custom-call(bf16[256,1024]{1,0:T(8,128)(2,1)S(1)} %collective-permute-done.34.n_ref, bf16[256,1024]{1,0:T(8,128)(2,1)} %collective-permute-done.35.d_ref, ...), custom_call_target="tpu_custom_call" | custom-call | flops 3623878656 | bytes 10944512 | tf_op jit(solution)/shard_map/ffn_piece/pallas_call | solution.py:54
  198.3 2.3 copy-done.38
  200.6 5.3 %ffn_piece.7 = (bf16[256,1024]{1,0:T(8,128)(2,1)S(1)}, bf16[256,1024]{1,0:T(8,128)(2,1)S(1)}, bf16[256,1152]{1,0:T(8,128)(2,1)S(1)}, bf16[256,2304]{1,0:T(8,128)(2,1)S(1)}) custom-call(bf16[256,1024]{1,0:T(8,128)(2,1)S(1)} %collective-permute-done.37.n_ref, bf16[256,1024]{1,0:T(8,128)(2,1)} %collective-permute-done.38.d_ref, ...), custom_call_target="tpu_custom_call" | custom-call | flops 3623878656 | bytes 10944512 | tf_op jit(solution)/shard_map/ffn_piece/pallas_call | solution.py:54
  207.0 1.6 pad_maximum_fusion.1.hid_ref
  208.7 10.6 %pad_maximum_fusion.dgu_ref = bf16[1024,2304]{1,0:T(8,128)(2,1)} fusion(bf16[256,2304]{1,0:T(8,128)(2,1)S(1)} %get-tuple-element.108, bf16[256,2304]{1,0:T(8,128)(2,1)S(1)} %get-tuple-element.107, bf16[256,2304]{1,0:T(8,128)(2,1)S(1)} %get-tuple-element.106, bf16[256,2304]{1,0:T(8,128)(2,1)S(1)} %get-tuple-element.105), kind=kLoop, calls=%fused_computation.1 | loop fusion | flops 18874368 | bytes 9437184 | tf_op jit(solution)/shard_map/concatenate | solution.py:522
  219.3 16.2 %collective-permute-done.42.refs_3_ = bf16[256,1024]{1,0:T(8,128)(2,1)S(1)} collective-permute-done((bf16[256,1024]{1,0:T(8,128)(2,1)S(1)}, bf16[256,1024]{1,0:T(8,128)(2,1)S(1)}, u32[]{:S(2)}, u32[]{:S(2)}) %collective-permute-start.42) | collective-permute-done | bytes 524320 | tf_op jit(solution)/shard_map/ppermute | solution.py:24
  235.5 5.7 %mixer_back.1 = (bf16[256,1024]{1,0:T(8,128)(2,1)S(1)}, bf16[256,1024]{1,0:T(8,128)(2,1)S(1)}, bf16[256,1024]{1,0:T(8,128)(2,1)S(1)}, bf16[256,1024]{1,0:T(8,128...) custom-call(bf16[256,1024]{1,0:T(8,128)(2,1)S(1)} %get-tuple-element, ...), custom_call_target="tpu_custom_call" | custom-call | flops 2147483648 | bytes 20807680 | tf_op jit(solution)/shard_map/mixer_back/pallas_call | solution.py:54
  245.7 2.5 grads_out.1
  253.3 4.8 %grads_in.1 = (bf16[4,4,272,256]{3,2,1,0:T(8,128)(2,1)}, bf16[4,4,272,256]{3,2,1,0:T(8,128)(2,1)S(1)}) custom-call(s32[2]{0:T(128)S(1)} %pad_add_fusion.idx_ref, bf16[256,1024]{1,0:T(8,128)(2,1)S(1)} %copy-done.25, bf16[256,1024]{1,0:T(8,128)(2,1)S(1)} %copy-done.45, bf16[256,1024]{1,0:T(8,128)(2,1)S(1)} %copy-done.25, bf16[256,1024]{1,0:T(8,128)(2,1)S(1)} %copy-done.47, ...), custom_call_target="tpu_custom_call" | custom-call | flops 1073741824 | bytes 6684680 | tf_op jit(solution)/shard_map/grads_in/pallas_call | solution.py:54
  258.3 2.2 copy-done.6
  260.5 1.6 copy-done.7
  262.1 10.8 %ffn_grads.1 = (bf16[4,128,3456]{2,1,0:T(8,128)(2,1)}, bf16[4,128,3456]{2,1,0:T(8,128)(2,1)S(1)}) custom-call(s32[2]{0:T(128)S(1)} %pad_add_fusion.idx_ref, bf16[1024,1024]{1,0:T(8,128)(2,1)S(1)} %copy-done.7, bf16[1024,1024]{1,0:T(8,128)(2,1)S(1)} %copy-done.6, bf16[1024,1152]{1,0:T(8,128)(2,1)S(1)} %copy-done.4, bf16[1024,2304]{1,0:T(8,128)(2,1)S(1)} %copy-done.1), custom_call_target="tpu_custom_call" | custom-call | flops 7247757312 | bytes 18350088 | tf_op jit(solution)/shard_map/ffn_grads/pallas_call | solution.py:54
  273.8 1.9 fusion.18
  280.0 11.9 %collective-permute-done.57 = bf16[4,256,256]{2,1,0:T(8,128)(2,1)} collective-permute-done((bf16[4,256,256]{2,1,0:T(8,128)(2,1)}, bf16[4,256,256]{2,1,0:T(8,128)(2,1)}, u32[]{:S(2)}, u32[]{:S(2)}) %collective-permute-start.57) | collective-permute-done | bytes 524320 | tf_op jit(solution)/shard_map/ppermute | solution.py:19
  292.0 10.4 %collective-permute-done.56 = bf16[4,256,256]{2,1,0:T(8,128)(2,1)} collective-permute-done((bf16[4,256,256]{2,1,0:T(8,128)(2,1)}, bf16[4,256,256]{2,1,0:T(8,128)(2,1)}, u32[]{:S(2)}, u32[]{:S(2)}) %collective-permute-start.56) | collective-permute-done | bytes 524320 | tf_op jit(solution)/shard_map/ppermute | solution.py:19
  302.6 3.6 collective-permute-start.33
  306.2 2.0 fusion.8
  308.2 20.2 %collective-permute-done.39 = bf16[256,1024]{1,0:T(8,128)(2,1)S(1)} collective-permute-done((bf16[256,1024]{1,0:T(8,128)(2,1)}, bf16[256,1024]{1,0:T(8,128)(2,1)S(1)}, u32[]{:S(2)}, u32[]{:S(2)}) %collective-permute-start.39) | collective-permute-done | bytes 524320 | tf_op jit(solution)/shard_map/ppermute | solution.py:24
  329.6 1.8 fusion.14
  331.4 1.6 collective-permute-start.50
  333.0 6.2 %collective-permute-done.33 = bf16[256,1024]{1,0:T(8,128)(2,1)S(1)} collective-permute-done((bf16[256,1024]{1,0:T(8,128)(2,1)}, bf16[256,1024]{1,0:T(8,128)(2,1)S(1)}, u32[]{:S(2)}, u32[]{:S(2)}) %collective-permute-start.33) | collective-permute-done | bytes 524320 | tf_op jit(solution)/shard_map/ppermute | solution.py:24
  341.9 4.6 %collective-permute-start.59 = (bf16[256,256]{1,0:T(8,128)(2,1)S(1)}, bf16[256,256]{1,0:T(8,128)(2,1)S(1)}, u32[]{:S(2)}, u32[]{:S(2)}) collective-permute-start(bf16[256,256]{1,0:T(8,128)(2,1)S(1)} %get-tuple-element.161), channel_id=1, source_target_pairs={{0,2},{1,3},{2,0},{3,1},{4,6},{5,7},{6,4},{7,5},{8,10},{9,11},{10,... | collective-permute-start | bytes 393224 | tf_op jit(solution)/shard_map/ppermute | solution.py:24
  347.7 4.4 %collective-permute-done.59 = bf16[256,256]{1,0:T(8,128)(2,1)S(1)} collective-permute-done((bf16[256,256]{1,0:T(8,128)(2,1)S(1)}, bf16[256,256]{1,0:T(8,128)(2,1)S(1)}, u32[]{:S(2)}, u32[]{:S(2)}) %collective-permute-start.59) | collective-permute-done | bytes 131104 | tf_op jit(solution)/shard_map/ppermute | solution.py:24
  353.9 5.3 %collective-permute-done.58 = bf16[256,256]{1,0:T(8,128)(2,1)S(1)} collective-permute-done((bf16[256,256]{1,0:T(8,128)(2,1)S(1)}, bf16[256,256]{1,0:T(8,128)(2,1)S(1)}, u32[]{:S(2)}, u32[]{:S(2)}) %collective-permute-start.58) | collective-permute-done | bytes 131104 | tf_op jit(solution)/shard_map/ppermute | solution.py:24
  359.3 1.8 fusion.5
  362.6 11.7 %collective-permute-start.53 = (bf16[272,256]{1,0:T(8,128)(2,1)S(1)}, bf16[272,256]{1,0:T(8,128)(2,1)S(1)}, u32[]{:S(2)}, u32[]{:S(2)}) collective-permute-start(bf16[272,256]{1,0:T(8,128)(2,1)S(1)} %get-tuple-element.157), channel_id=1, source_target_pairs={{0,3},{1,0},{2,1},{3,2},{4,7},{5,4},{6,5},{7,6},{8,11},{9,8},{10,9... | collective-permute-start | bytes 417800 | tf_op jit(solution)/shard_map/ppermute | solution.py:24
  375.5 3.6 fusion.10
  383.4 1.7 copy.48
  385.0 1.7 collective-permute-done.52
  388.5 1.7 pad_maximum_fusion.7
  390.7 12.2 %collective-permute-done.64 = bf16[128,3456]{1,0:T(8,128)(2,1)} collective-permute-done((bf16[128,3456]{1,0:T(8,128)(2,1)}, bf16[128,3456]{1,0:T(8,128)(2,1)}, u32[]{:S(2)}, u32[]{:S(2)}) %collective-permute-start.64) | collective-permute-done | bytes 884768 | tf_op jit(solution)/shard_map/ppermute | solution.py:19
  402.9 17.1 %collective-permute-done.63 = bf16[128,3456]{1,0:T(8,128)(2,1)} collective-permute-done((bf16[128,3456]{1,0:T(8,128)(2,1)}, bf16[128,3456]{1,0:T(8,128)(2,1)}, u32[]{:S(2)}, u32[]{:S(2)}) %collective-permute-start.63) | collective-permute-done | bytes 884768 | tf_op jit(solution)/shard_map/ppermute | solution.py:19
  420.0 2.5 fusion.2
  422.7 1.9 copy.49
  (280 shorter events, 83.6 us)
Async XLA Ops:
  1.7 37.8 %collective-permute-start.4 = (bf16[256,256]{1,0:T(8,128)(2,1)S(1)}, bf16[256,256]{1,0:T(8,128)(2,1)S(1)}, u32[]{:S(2)}, u32[]{:S(2)}) collective-permute-start(bf16[256,256]{1,0:T(8,128)(2,1)S(1)} %bitcast.127), channel_id=1, source_target_pairs={{0,1},{1,2},{2,3},{3,0},{4,5},{5,6},{6,7},{7,4},{8,9},{9,10},{10,1... | collective-permute-start | bytes 393224 | tf_op jit(solution)/shard_map/ppermute | solution.py:24
  4.8 34.8 %collective-permute-start.5 = (bf16[256,256]{1,0:T(8,128)(2,1)S(1)}, bf16[256,256]{1,0:T(8,128)(2,1)S(1)}, u32[]{:S(2)}, u32[]{:S(2)}) collective-permute-start(bf16[256,256]{1,0:T(8,128)(2,1)S(1)} %bitcast.128), channel_id=1, source_target_pairs={{0,2},{1,3},{2,0},{3,1},{4,6},{5,7},{6,4},{7,5},{8,10},{9,11},{10,... | collective-permute-start | bytes 393224 | tf_op jit(solution)/shard_map/ppermute | solution.py:24
  8.5 21.0 %collective-permute-start.16 = (bf16[256,256]{1,0:T(8,128)(2,1)S(1)}, bf16[256,256]{1,0:T(8,128)(2,1)S(1)}, u32[]{:S(2)}, u32[]{:S(2)}) collective-permute-start(bf16[256,256]{1,0:T(8,128)(2,1)S(1)} %bitcast.131), channel_id=1, source_target_pairs={{0,3},{1,0},{2,1},{3,2},{4,7},{5,4},{6,5},{7,6},{8,11},{9,8},{10,9... | collective-permute-start | bytes 393224 | tf_op jit(solution)/shard_map/ppermute | solution.py:24
  9.9 19.7 %collective-permute-start.15 = (bf16[256,256]{1,0:T(8,128)(2,1)S(1)}, bf16[256,256]{1,0:T(8,128)(2,1)S(1)}, u32[]{:S(2)}, u32[]{:S(2)}) collective-permute-start(bf16[256,256]{1,0:T(8,128)(2,1)S(1)} %bitcast.132), channel_id=1, source_target_pairs={{0,2},{1,3},{2,0},{3,1},{4,6},{5,7},{6,4},{7,5},{8,10},{9,11},{10,... | collective-permute-start | bytes 393224 | tf_op jit(solution)/shard_map/ppermute | solution.py:24
  11.0 8.6 %collective-permute-start = (bf16[8,2048]{1,0:T(8,128)(2,1)S(1)}, bf16[8,2048]{1,0:T(8,128)(2,1)S(1)}, u32[]{:S(2)}, u32[]{:S(2)}) collective-permute-start(bf16[8,2048]{1,0:T(8,128)(2,1)S(1)} %bitcast.141), channel_id=1, source_target_pairs={{0,1},{1,2},{2,3},{3,0},{4,5},{5,6},{6,7},{7,4},{8,9},{9,10},{10,1... | collective-permute-start | bytes 98312 | tf_op jit(solution)/shard_map/ppermute | solution.py:24
  20.8 4.3 %collective-permute-start.2 = (bf16[2,1,8,2048]{3,2,1,0:T(8,128)(2,1)S(1)}, bf16[2,1,8,2048]{3,2,1,0:T(8,128)(2,1)S(1)}, u32[]{:S(2)}, u32[]{:S(2)}) collective-permute-start(bf16[2,1,8,2048]{3,2,1,0:T(8,128)(2,1)S(1)} %pad_maximum_fusion.11), channel_id=1, source_target_pairs={{0,8},{4,12},{8,0},{12,4},{16,24},{20,28},{24,16},{28,20},{1,9},{5... | collective-permute-start | bytes 196616 | tf_op jit(solution)/shard_map/ppermute | solution.py:19
  25.2 7.6 %collective-permute-start.14 = (bf16[256,256]{1,0:T(8,128)(2,1)S(1)}, bf16[256,256]{1,0:T(8,128)(2,1)S(1)}, u32[]{:S(2)}, u32[]{:S(2)}) collective-permute-start(bf16[256,256]{1,0:T(8,128)(2,1)S(1)} %bitcast.133), channel_id=1, source_target_pairs={{0,1},{1,2},{2,3},{3,0},{4,5},{5,6},{6,7},{7,4},{8,9},{9,10},{10,1... | collective-permute-start | bytes 393224 | tf_op jit(solution)/shard_map/ppermute | solution.py:24
  29.5 11.7 %collective-permute-start.6 = (bf16[256,256]{1,0:T(8,128)(2,1)S(1)}, bf16[256,256]{1,0:T(8,128)(2,1)S(1)}, u32[]{:S(2)}, u32[]{:S(2)}) collective-permute-start(bf16[256,256]{1,0:T(8,128)(2,1)S(1)} %bitcast.129), channel_id=1, source_target_pairs={{0,3},{1,0},{2,1},{3,2},{4,7},{5,4},{6,5},{7,6},{8,11},{9,8},{10,9... | collective-permute-start | bytes 393224 | tf_op jit(solution)/shard_map/ppermute | solution.py:24
  29.6 13.1 %collective-permute-start.3 = (bf16[4,1,8,2048]{3,2,1,0:T(8,128)(2,1)S(1)}, bf16[4,1,8,2048]{3,2,1,0:T(8,128)(2,1)S(1)}, u32[]{:S(2)}, u32[]{:S(2)}) collective-permute-start(bf16[4,1,8,2048]{3,2,1,0:T(8,128)(2,1)S(1)} %pad_maximum_fusion.8), channel_id=1, source_target_pairs={{0,16},{4,20},{8,24},{12,28},{16,0},{20,4},{24,8},{28,12},{1,17},{... | collective-permute-start | bytes 393224 | tf_op jit(solution)/shard_map/ppermute | solution.py:19
  32.8 27.1 %collective-permute-start.38 = (bf16[256,1024]{1,0:T(8,128)(2,1)S(1)}, bf16[256,1024]{1,0:T(8,128)(2,1)}, u32[]{:S(2)}, u32[]{:S(2)}) collective-permute-start(bf16[256,1024]{1,0:T(8,128)(2,1)S(1)} %bitcast.118), channel_id=1, source_target_pairs={{0,2},{1,3},{2,0},{3,1},{4,6},{5,7},{6,4},{7,5},{8,10},{9,11},{10,... | collective-permute-start | bytes 1572872 | tf_op jit(solution)/shard_map/ppermute | solution.py:24
  39.5 20.3 %collective-permute-start.17 = (bf16[1024,256]{1,0:T(8,128)(2,1)S(1)}, bf16[1024,256]{1,0:T(8,128)(2,1)S(1)}, u32[]{:S(2)}, u32[]{:S(2)}) collective-permute-start(bf16[1024,256]{1,0:T(8,128)(2,1)S(1)} %pad_maximum_fusion.6.refs_0_), channel_id=1, source_target_pairs={{0,4},{4,0},{8,12},{12,8},{16,20},{20,16},{24,28},{28,24},{1,5},{5... | collective-permute-start | bytes 1572872 | tf_op jit(solution)/shard_map/ppermute | solution.py:19
  39.6 21.8 %collective-permute-start.18 = (bf16[1024,256]{1,0:T(8,128)(2,1)S(1)}, bf16[1024,256]{1,0:T(8,128)(2,1)S(1)}, u32[]{:S(2)}, u32[]{:S(2)}) collective-permute-start(bf16[1024,256]{1,0:T(8,128)(2,1)S(1)} %pad_maximum_fusion.6.refs_0_), channel_id=1, source_target_pairs={{0,8},{4,12},{8,0},{12,4},{16,24},{20,28},{24,16},{28,20},{1,9},{5... | collective-permute-start | bytes 1572872 | tf_op jit(solution)/shard_map/ppermute | solution.py:19
  41.2 25.2 %collective-permute-start.20 = (bf16[1024,256]{1,0:T(8,128)(2,1)S(1)}, bf16[1024,256]{1,0:T(8,128)(2,1)S(1)}, u32[]{:S(2)}, u32[]{:S(2)}) collective-permute-start(bf16[1024,256]{1,0:T(8,128)(2,1)S(1)} %pad_maximum_fusion.6.refs_0_), channel_id=1, source_target_pairs={{0,16},{4,20},{8,24},{12,28},{16,0},{20,4},{24,8},{28,12},{1,17},{... | collective-permute-start | bytes 1572872 | tf_op jit(solution)/shard_map/ppermute | solution.py:19
  42.7 25.3 %collective-permute-start.22 = (bf16[1024,256]{1,0:T(8,128)(2,1)S(1)}, bf16[1024,256]{1,0:T(8,128)(2,1)S(1)}, u32[]{:S(2)}, u32[]{:S(2)}) collective-permute-start(bf16[1024,256]{1,0:T(8,128)(2,1)S(1)} %pad_maximum_fusion.6.refs_0_), channel_id=1, source_target_pairs={{0,24},{4,28},{8,16},{12,20},{16,8},{20,12},{24,0},{28,4},{1,25},{... | collective-permute-start | bytes 1572872 | tf_op jit(solution)/shard_map/ppermute | solution.py:19
  59.8 9.8 %collective-permute-start.7 = (bf16[1040,256]{1,0:T(8,128)(2,1)S(1)}, bf16[1040,256]{1,0:T(8,128)(2,1)S(1)}, u32[]{:S(2)}, u32[]{:S(2)}) collective-permute-start(bf16[1040,256]{1,0:T(8,128)(2,1)S(1)} %constant_dynamic-update-slice_fusion.refs_0_), channel_id=1, source_target_pairs={{0,4},{4,0},{8,12},{12,8},{16,20},{20,16},{24,28},{28,24},{1,5},{5... | collective-permute-start | bytes 1597448 | tf_op jit(solution)/shard_map/ppermute | solution.py:19
  59.9 17.4 %collective-permute-start.8 = (bf16[1040,256]{1,0:T(8,128)(2,1)S(1)}, bf16[1040,256]{1,0:T(8,128)(2,1)}, u32[]{:S(2)}, u32[]{:S(2)}) collective-permute-start(bf16[1040,256]{1,0:T(8,128)(2,1)S(1)} %constant_dynamic-update-slice_fusion.refs_0_), channel_id=1, source_target_pairs={{0,8},{4,12},{8,0},{12,4},{16,24},{20,28},{24,16},{28,20},{1,9},{5... | collective-permute-start | bytes 1597448 | tf_op jit(solution)/shard_map/ppermute | solution.py:19
  61.4 27.9 %collective-permute-start.10 = (bf16[1040,256]{1,0:T(8,128)(2,1)S(1)}, bf16[1040,256]{1,0:T(8,128)(2,1)}, u32[]{:S(2)}, u32[]{:S(2)}) collective-permute-start(bf16[1040,256]{1,0:T(8,128)(2,1)S(1)} %constant_dynamic-update-slice_fusion.refs_0_), channel_id=1, source_target_pairs={{0,16},{4,20},{8,24},{12,28},{16,0},{20,4},{24,8},{28,12},{1,17},{... | collective-permute-start | bytes 1597448 | tf_op jit(solution)/shard_map/ppermute | solution.py:19
  66.4 23.0 %collective-permute-start.12 = (bf16[1040,256]{1,0:T(8,128)(2,1)S(1)}, bf16[1040,256]{1,0:T(8,128)(2,1)}, u32[]{:S(2)}, u32[]{:S(2)}) collective-permute-start(bf16[1040,256]{1,0:T(8,128)(2,1)S(1)} %constant_dynamic-update-slice_fusion.refs_0_), channel_id=1, source_target_pairs={{0,24},{4,28},{8,16},{12,20},{16,8},{20,12},{24,0},{28,4},{1,25},{... | collective-permute-start | bytes 1597448 | tf_op jit(solution)/shard_map/ppermute | solution.py:19
  68.8 21.0 %collective-permute-start.19 = (bf16[1024,256]{1,0:T(8,128)(2,1)S(1)}, bf16[1024,256]{1,0:T(8,128)(2,1)}, u32[]{:S(2)}, u32[]{:S(2)}) collective-permute-start(bf16[1024,256]{1,0:T(8,128)(2,1)S(1)} %collective-permute-done.18.refs_2_), channel_id=1, source_target_pairs={{0,4},{4,0},{8,12},{12,8},{16,20},{20,16},{24,28},{28,24},{1,5},{5... | collective-permute-start | bytes 1572872 | tf_op jit(solution)/shard_map/ppermute | solution.py:19
  70.4 20.6 %collective-permute-start.21 = (bf16[1024,256]{1,0:T(8,128)(2,1)S(1)}, bf16[1024,256]{1,0:T(8,128)(2,1)}, u32[]{:S(2)}, u32[]{:S(2)}) collective-permute-start(bf16[1024,256]{1,0:T(8,128)(2,1)S(1)} %collective-permute-done.20.refs_4_), channel_id=1, source_target_pairs={{0,4},{4,0},{8,12},{12,8},{16,20},{20,16},{24,28},{28,24},{1,5},{5... | collective-permute-start | bytes 1572872 | tf_op jit(solution)/shard_map/ppermute | solution.py:19
  77.3 14.3 %collective-permute-start.23 = (bf16[1024,256]{1,0:T(8,128)(2,1)}, bf16[1024,256]{1,0:T(8,128)(2,1)S(1)}, u32[]{:S(2)}, u32[]{:S(2)}) collective-permute-start(bf16[1024,256]{1,0:T(8,128)(2,1)} %copy-done.30), channel_id=1, source_target_pairs={{0,4},{4,0},{8,12},{12,8},{16,20},{20,16},{24,28},{28,24},{1,5},{5... | collective-permute-start | bytes 1572872 | tf_op jit(solution)/shard_map/ppermute | solution.py:19
  89.3 4.3 %collective-permute-start.9 = (bf16[1040,256]{1,0:T(8,128)(2,1)}, bf16[1040,256]{1,0:T(8,128)(2,1)S(1)}, u32[]{:S(2)}, u32[]{:S(2)}) collective-permute-start(bf16[1040,256]{1,0:T(8,128)(2,1)} %collective-permute-done.8.refs_2_), channel_id=1, source_target_pairs={{0,4},{4,0},{8,12},{12,8},{16,20},{20,16},{24,28},{28,24},{1,5},{5... | collective-permute-start | bytes 1597448 | tf_op jit(solution)/shard_map/ppermute | solution.py:19
  89.3 6.0 %collective-permute-start.11 = (bf16[1040,256]{1,0:T(8,128)(2,1)}, bf16[1040,256]{1,0:T(8,128)(2,1)S(1)}, u32[]{:S(2)}, u32[]{:S(2)}) collective-permute-start(bf16[1040,256]{1,0:T(8,128)(2,1)} %collective-permute-done.10.refs_4_), channel_id=1, source_target_pairs={{0,4},{4,0},{8,12},{12,8},{16,20},{20,16},{24,28},{28,24},{1,5},{5... | collective-permute-start | bytes 1597448 | tf_op jit(solution)/shard_map/ppermute | solution.py:19
  89.8 7.7 %collective-permute-start.13 = (bf16[1040,256]{1,0:T(8,128)(2,1)}, bf16[1040,256]{1,0:T(8,128)(2,1)S(1)}, u32[]{:S(2)}, u32[]{:S(2)}) collective-permute-start(bf16[1040,256]{1,0:T(8,128)(2,1)} %collective-permute-done.12.refs_6_), channel_id=1, source_target_pairs={{0,4},{4,0},{8,12},{12,8},{16,20},{20,16},{24,28},{28,24},{1,5},{5... | collective-permute-start | bytes 1597448 | tf_op jit(solution)/shard_map/ppermute | solution.py:19
  91.0 25.7 %collective-permute-start.35 = (bf16[256,1024]{1,0:T(8,128)(2,1)S(1)}, bf16[256,1024]{1,0:T(8,128)(2,1)}, u32[]{:S(2)}, u32[]{:S(2)}) collective-permute-start(bf16[256,1024]{1,0:T(8,128)(2,1)S(1)} %bitcast.119), channel_id=1, source_target_pairs={{0,3},{1,0},{2,1},{3,2},{4,7},{5,4},{6,5},{7,6},{8,11},{9,8},{10,9... | collective-permute-start | bytes 1572872 | tf_op jit(solution)/shard_map/ppermute | solution.py:24
  92.4 26.5 %collective-permute-start.25 = (bf16[128,3456]{1,0:T(8,128)(2,1)S(1)}, bf16[128,3456]{1,0:T(8,128)(2,1)S(1)}, u32[]{:S(2)}, u32[]{:S(2)}) collective-permute-start(bf16[128,3456]{1,0:T(8,128)(2,1)S(1)} %pad_maximum_fusion.5.refs_0_), channel_id=1, source_target_pairs={{0,8},{4,12},{8,0},{12,4},{16,24},{20,28},{24,16},{28,20},{1,9},{5... | collective-permute-start | bytes 2654216 | tf_op jit(solution)/shard_map/ppermute | solution.py:19
  94.4 40.1 %collective-permute-start.27 = (bf16[128,3456]{1,0:T(8,128)(2,1)S(1)}, bf16[128,3456]{1,0:T(8,128)(2,1)}, u32[]{:S(2)}, u32[]{:S(2)}) collective-permute-start(bf16[128,3456]{1,0:T(8,128)(2,1)S(1)} %pad_maximum_fusion.5.refs_0_), channel_id=1, source_target_pairs={{0,16},{4,20},{8,24},{12,28},{16,0},{20,4},{24,8},{28,12},{1,17},{... | collective-permute-start | bytes 2654216 | tf_op jit(solution)/shard_map/ppermute | solution.py:19
  96.1 38.4 %collective-permute-start.29 = (bf16[128,3456]{1,0:T(8,128)(2,1)S(1)}, bf16[128,3456]{1,0:T(8,128)(2,1)}, u32[]{:S(2)}, u32[]{:S(2)}) collective-permute-start(bf16[128,3456]{1,0:T(8,128)(2,1)S(1)} %pad_maximum_fusion.5.refs_0_), channel_id=1, source_target_pairs={{0,24},{4,28},{8,16},{12,20},{16,8},{20,12},{24,0},{28,4},{1,25},{... | collective-permute-start | bytes 2654216 | tf_op jit(solution)/shard_map/ppermute | solution.py:19
  98.4 18.3 %collective-permute-start.32 = (bf16[256,1024]{1,0:T(8,128)(2,1)S(1)}, bf16[256,1024]{1,0:T(8,128)(2,1)}, u32[]{:S(2)}, u32[]{:S(2)}) collective-permute-start(bf16[256,1024]{1,0:T(8,128)(2,1)S(1)} %bitcast.120), channel_id=1, source_target_pairs={{0,1},{1,2},{2,3},{3,0},{4,5},{5,6},{6,7},{7,4},{8,9},{9,10},{10,1... | collective-permute-start | bytes 1572872 | tf_op jit(solution)/shard_map/ppermute | solution.py:24
  116.7 23.7 %collective-permute-start.37 = (bf16[256,1024]{1,0:T(8,128)(2,1)S(1)}, bf16[256,1024]{1,0:T(8,128)(2,1)S(1)}, u32[]{:S(2)}, u32[]{:S(2)}) collective-permute-start(bf16[256,1024]{1,0:T(8,128)(2,1)S(1)} %get-tuple-element.68.n_ref), channel_id=1, source_target_pairs={{0,2},{1,3},{2,0},{3,1},{4,6},{5,7},{6,4},{7,5},{8,10},{9,11},{10,... | collective-permute-start | bytes 1572872 | tf_op jit(solution)/shard_map/ppermute | solution.py:24
  116.7 24.1 %collective-permute-start.34 = (bf16[256,1024]{1,0:T(8,128)(2,1)S(1)}, bf16[256,1024]{1,0:T(8,128)(2,1)S(1)}, u32[]{:S(2)}, u32[]{:S(2)}) collective-permute-start(bf16[256,1024]{1,0:T(8,128)(2,1)S(1)} %get-tuple-element.68.n_ref), channel_id=1, source_target_pairs={{0,3},{1,0},{2,1},{3,2},{4,7},{5,4},{6,5},{7,6},{8,11},{9,8},{10,9... | collective-permute-start | bytes 1572872 | tf_op jit(solution)/shard_map/ppermute | solution.py:24
  118.9 48.4 %collective-permute-start.24 = (bf16[128,3456]{1,0:T(8,128)(2,1)S(1)}, bf16[128,3456]{1,0:T(8,128)(2,1)S(1)}, u32[]{:S(2)}, u32[]{:S(2)}) collective-permute-start(bf16[128,3456]{1,0:T(8,128)(2,1)S(1)} %pad_maximum_fusion.5.refs_0_), channel_id=1, source_target_pairs={{0,4},{4,0},{8,12},{12,8},{16,20},{20,16},{24,28},{28,24},{1,5},{5... | collective-permute-start | bytes 2654216 | tf_op jit(solution)/shard_map/ppermute | solution.py:19
  134.5 32.8 %collective-permute-start.26 = (bf16[128,3456]{1,0:T(8,128)(2,1)S(1)}, bf16[128,3456]{1,0:T(8,128)(2,1)S(1)}, u32[]{:S(2)}, u32[]{:S(2)}) collective-permute-start(bf16[128,3456]{1,0:T(8,128)(2,1)S(1)} %collective-permute-done.25.refs_2_), channel_id=1, source_target_pairs={{0,4},{4,0},{8,12},{12,8},{16,20},{20,16},{24,28},{28,24},{1,5},{5... | collective-permute-start | bytes 2654216 | tf_op jit(solution)/shard_map/ppermute | solution.py:19
  134.5 32.8 %collective-permute-start.28 = (bf16[128,3456]{1,0:T(8,128)(2,1)}, bf16[128,3456]{1,0:T(8,128)(2,1)S(1)}, u32[]{:S(2)}, u32[]{:S(2)}) collective-permute-start(bf16[128,3456]{1,0:T(8,128)(2,1)} %collective-permute-done.27.refs_4_), channel_id=1, source_target_pairs={{0,4},{4,0},{8,12},{12,8},{16,20},{20,16},{24,28},{28,24},{1,5},{5... | collective-permute-start | bytes 2654216 | tf_op jit(solution)/shard_map/ppermute | solution.py:19
  140.4 26.9 %collective-permute-start.30 = (bf16[128,3456]{1,0:T(8,128)(2,1)}, bf16[128,3456]{1,0:T(8,128)(2,1)S(1)}, u32[]{:S(2)}, u32[]{:S(2)}) collective-permute-start(bf16[128,3456]{1,0:T(8,128)(2,1)} %collective-permute-done.29.refs_6_), channel_id=1, source_target_pairs={{0,4},{4,0},{8,12},{12,8},{16,20},{20,16},{24,28},{28,24},{1,5},{5... | collective-permute-start | bytes 2654216 | tf_op jit(solution)/shard_map/ppermute | solution.py:19
  140.8 25.0 %collective-permute-start.31 = (bf16[256,1024]{1,0:T(8,128)(2,1)S(1)}, bf16[256,1024]{1,0:T(8,128)(2,1)S(1)}, u32[]{:S(2)}, u32[]{:S(2)}) collective-permute-start(bf16[256,1024]{1,0:T(8,128)(2,1)S(1)} %get-tuple-element.68.n_ref), channel_id=1, source_target_pairs={{0,1},{1,2},{2,3},{3,0},{4,5},{5,6},{6,7},{7,4},{8,9},{9,10},{10,1... | collective-permute-start | bytes 1572872 | tf_op jit(solution)/shard_map/ppermute | solution.py:24
  187.8 31.5 %collective-permute-start.40 = (bf16[256,1024]{1,0:T(8,128)(2,1)S(1)}, bf16[256,1024]{1,0:T(8,128)(2,1)S(1)}, u32[]{:S(2)}, u32[]{:S(2)}) collective-permute-start(bf16[256,1024]{1,0:T(8,128)(2,1)S(1)} %get-tuple-element.76), channel_id=1, source_target_pairs={{0,3},{1,0},{2,1},{3,2},{4,7},{5,4},{6,5},{7,6},{8,11},{9,8},{10,9... | collective-permute-start | bytes 1572872 | tf_op jit(solution)/shard_map/ppermute | solution.py:24
  198.0 21.3 %collective-permute-start.41 = (bf16[256,1024]{1,0:T(8,128)(2,1)S(1)}, bf16[256,1024]{1,0:T(8,128)(2,1)S(1)}, u32[]{:S(2)}, u32[]{:S(2)}) collective-permute-start(bf16[256,1024]{1,0:T(8,128)(2,1)S(1)} %get-tuple-element.77), channel_id=1, source_target_pairs={{0,1},{1,2},{2,3},{3,0},{4,5},{5,6},{6,7},{7,4},{8,9},{9,10},{10,1... | collective-permute-start | bytes 1572872 | tf_op jit(solution)/shard_map/ppermute | solution.py:24
  206.7 28.7 %collective-permute-start.42 = (bf16[256,1024]{1,0:T(8,128)(2,1)S(1)}, bf16[256,1024]{1,0:T(8,128)(2,1)S(1)}, u32[]{:S(2)}, u32[]{:S(2)}) collective-permute-start(bf16[256,1024]{1,0:T(8,128)(2,1)S(1)} %get-tuple-element.78), channel_id=1, source_target_pairs={{0,2},{1,3},{2,0},{3,1},{4,6},{5,7},{6,4},{7,5},{8,10},{9,11},{10,... | collective-permute-start | bytes 1572872 | tf_op jit(solution)/shard_map/ppermute | solution.py:24
  248.1 25.7 %collective-permute-start.54 = (bf16[4,4,256,256]{3,2,1,0:T(8,128)(2,1)S(1)}, bf16[4,4,256,256]{3,2,1,0:T(8,128)(2,1)S(1)}, u32[]{:S(2)}, u32[]{:S(2)}) collective-permute-start(bf16[4,4,256,256]{3,2,1,0:T(8,128)(2,1)S(1)} %get-tuple-element.100), channel_id=1, source_target_pairs={{0,4},{4,0},{8,12},{12,8},{16,20},{20,16},{24,28},{28,24},{1,5},{5... | collective-permute-start | bytes 6291464 | tf_op jit(solution)/shard_map/ppermute | solution.py:19
  248.6 24.5 %collective-permute-start.43 = (bf16[4,8,2048]{2,1,0:T(8,128)(2,1)S(1)}, bf16[4,8,2048]{2,1,0:T(8,128)(2,1)S(1)}, u32[]{:S(2)}, u32[]{:S(2)}) collective-permute-start(bf16[4,8,2048]{2,1,0:T(8,128)(2,1)S(1)} %slice_bitcast_fusion.7), channel_id=1, source_target_pairs={{0,16},{4,20},{8,24},{12,28},{16,0},{20,4},{24,8},{28,12},{1,17},{... | collective-permute-start | bytes 393224 | tf_op jit(solution)/shard_map/ppermute | solution.py:19
  258.1 70.3 %collective-permute-start.47 = (bf16[4,4,272,256]{3,2,1,0:T(8,128)(2,1)}, bf16[4,4,272,256]{3,2,1,0:T(8,128)(2,1)}, u32[]{:S(2)}, u32[]{:S(2)}) collective-permute-start(bf16[4,4,272,256]{3,2,1,0:T(8,128)(2,1)} %get-tuple-element.95), channel_id=1, source_target_pairs={{0,4},{4,0},{8,12},{12,8},{16,20},{20,16},{24,28},{28,24},{1,5},{5... | collective-permute-start | bytes 6684680 | tf_op jit(solution)/shard_map/ppermute | solution.py:19
  272.9 102.6 %collective-permute-start.61 = (bf16[4,128,3456]{2,1,0:T(8,128)(2,1)}, bf16[4,128,3456]{2,1,0:T(8,128)(2,1)}, u32[]{:S(2)}, u32[]{:S(2)}) collective-permute-start(bf16[4,128,3456]{2,1,0:T(8,128)(2,1)} %get-tuple-element.110), channel_id=1, source_target_pairs={{0,4},{4,0},{8,12},{12,8},{16,20},{20,16},{24,28},{28,24},{1,5},{5... | collective-permute-start | bytes 10616840 | tf_op jit(solution)/shard_map/ppermute | solution.py:19
  273.2 4.4 %collective-permute-start.44 = (bf16[2,8,2048]{2,1,0:T(8,128)(2,1)S(1)}, bf16[2,8,2048]{2,1,0:T(8,128)(2,1)S(1)}, u32[]{:S(2)}, u32[]{:S(2)}) collective-permute-start(bf16[2,8,2048]{2,1,0:T(8,128)(2,1)S(1)} %slice.205), channel_id=1, source_target_pairs={{0,8},{4,12},{8,0},{12,4},{16,24},{20,28},{24,16},{28,20},{1,9},{5... | collective-permute-start | bytes 196616 | tf_op jit(solution)/shard_map/ppermute | solution.py:19
  275.9 16.1 %collective-permute-start.57 = (bf16[4,256,256]{2,1,0:T(8,128)(2,1)}, bf16[4,256,256]{2,1,0:T(8,128)(2,1)}, u32[]{:S(2)}, u32[]{:S(2)}) collective-permute-start(bf16[4,256,256]{2,1,0:T(8,128)(2,1)} %get-tuple-element.149), channel_id=1, source_target_pairs={{0,24},{4,28},{8,16},{12,20},{16,8},{20,12},{24,0},{28,4},{1,25},{... | collective-permute-start | bytes 1572872 | tf_op jit(solution)/shard_map/ppermute | solution.py:19
  277.6 1.9 collective-permute-start.45
  277.7 24.7 %collective-permute-start.56 = (bf16[4,256,256]{2,1,0:T(8,128)(2,1)}, bf16[4,256,256]{2,1,0:T(8,128)(2,1)}, u32[]{:S(2)}, u32[]{:S(2)}) collective-permute-start(bf16[4,256,256]{2,1,0:T(8,128)(2,1)} %get-tuple-element.150), channel_id=1, source_target_pairs={{0,16},{4,20},{8,24},{12,28},{16,0},{20,4},{24,8},{28,12},{1,17},{... | collective-permute-start | bytes 1572872 | tf_op jit(solution)/shard_map/ppermute | solution.py:19
  279.5 23.1 %collective-permute-start.55 = (bf16[4,256,256]{2,1,0:T(8,128)(2,1)}, bf16[4,256,256]{2,1,0:T(8,128)(2,1)}, u32[]{:S(2)}, u32[]{:S(2)}) collective-permute-start(bf16[4,256,256]{2,1,0:T(8,128)(2,1)} %get-tuple-element.148), channel_id=1, source_target_pairs={{0,8},{4,12},{8,0},{12,4},{16,24},{20,28},{24,16},{28,20},{1,9},{5... | collective-permute-start | bytes 1572872 | tf_op jit(solution)/shard_map/ppermute | solution.py:19
  292.0 36.5 %collective-permute-start.39 = (bf16[256,1024]{1,0:T(8,128)(2,1)}, bf16[256,1024]{1,0:T(8,128)(2,1)S(1)}, u32[]{:S(2)}, u32[]{:S(2)}) collective-permute-start(bf16[256,1024]{1,0:T(8,128)(2,1)} %copy-done.41), channel_id=1, source_target_pairs={{0,2},{1,3},{2,0},{3,1},{4,6},{5,7},{6,4},{7,5},{8,10},{9,11},{10,... | collective-permute-start | bytes 1572872 | tf_op jit(solution)/shard_map/ppermute | solution.py:24
  302.4 29.1 %collective-permute-start.36 = (bf16[256,1024]{1,0:T(8,128)(2,1)}, bf16[256,1024]{1,0:T(8,128)(2,1)S(1)}, u32[]{:S(2)}, u32[]{:S(2)}) collective-permute-start(bf16[256,1024]{1,0:T(8,128)(2,1)} %copy-done.40), channel_id=1, source_target_pairs={{0,1},{1,2},{2,3},{3,0},{4,5},{5,6},{6,7},{7,4},{8,9},{9,10},{10,1... | collective-permute-start | bytes 1572872 | tf_op jit(solution)/shard_map/ppermute | solution.py:24
  302.6 36.6 %collective-permute-start.33 = (bf16[256,1024]{1,0:T(8,128)(2,1)}, bf16[256,1024]{1,0:T(8,128)(2,1)S(1)}, u32[]{:S(2)}, u32[]{:S(2)}) collective-permute-start(bf16[256,1024]{1,0:T(8,128)(2,1)} %copy-done.39), channel_id=1, source_target_pairs={{0,3},{1,0},{2,1},{3,2},{4,7},{5,4},{6,5},{7,6},{8,11},{9,8},{10,9... | collective-permute-start | bytes 1572872 | tf_op jit(solution)/shard_map/ppermute | solution.py:24
  328.5 11.4 %collective-permute-start.46 = (bf16[8,2048]{1,0:T(8,128)(2,1)S(1)}, bf16[8,2048]{1,0:T(8,128)(2,1)S(1)}, u32[]{:S(2)}, u32[]{:S(2)}) collective-permute-start(bf16[8,2048]{1,0:T(8,128)(2,1)S(1)} %fusion.33), channel_id=1, source_target_pairs={{0,3},{1,0},{2,1},{3,2},{4,7},{5,4},{6,5},{7,6},{8,11},{9,8},{10,9... | collective-permute-start | bytes 98312 | tf_op jit(solution)/shard_map/ppermute | solution.py:24
  328.5 13.4 %collective-permute-start.60 = (bf16[256,256]{1,0:T(8,128)(2,1)S(1)}, bf16[256,256]{1,0:T(8,128)(2,1)S(1)}, u32[]{:S(2)}, u32[]{:S(2)}) collective-permute-start(bf16[256,256]{1,0:T(8,128)(2,1)S(1)} %get-tuple-element.160), channel_id=1, source_target_pairs={{0,3},{1,0},{2,1},{3,2},{4,7},{5,4},{6,5},{7,6},{8,11},{9,8},{10,9... | collective-permute-start | bytes 393224 | tf_op jit(solution)/shard_map/ppermute | solution.py:24
  331.4 27.8 %collective-permute-start.50 = (bf16[4,272,256]{2,1,0:T(8,128)(2,1)S(1)}, bf16[4,272,256]{2,1,0:T(8,128)(2,1)S(1)}, u32[]{:S(2)}, u32[]{:S(2)}) collective-permute-start(bf16[4,272,256]{2,1,0:T(8,128)(2,1)S(1)} %get-tuple-element.146), channel_id=1, source_target_pairs={{0,24},{4,28},{8,16},{12,20},{16,8},{20,12},{24,0},{28,4},{1,25},{... | collective-permute-start | bytes 1671176 | tf_op jit(solution)/shard_map/ppermute | solution.py:19
  339.2 20.1 %collective-permute-start.49 = (bf16[4,272,256]{2,1,0:T(8,128)(2,1)S(1)}, bf16[4,272,256]{2,1,0:T(8,128)(2,1)S(1)}, u32[]{:S(2)}, u32[]{:S(2)}) collective-permute-start(bf16[4,272,256]{2,1,0:T(8,128)(2,1)S(1)} %get-tuple-element.147), channel_id=1, source_target_pairs={{0,16},{4,20},{8,24},{12,28},{16,0},{20,4},{24,8},{28,12},{1,17},{... | collective-permute-start | bytes 1671176 | tf_op jit(solution)/shard_map/ppermute | solution.py:19
  339.9 19.4 %collective-permute-start.48 = (bf16[4,272,256]{2,1,0:T(8,128)(2,1)S(1)}, bf16[4,272,256]{2,1,0:T(8,128)(2,1)S(1)}, u32[]{:S(2)}, u32[]{:S(2)}) collective-permute-start(bf16[4,272,256]{2,1,0:T(8,128)(2,1)S(1)} %get-tuple-element.145), channel_id=1, source_target_pairs={{0,8},{4,12},{8,0},{12,4},{16,24},{20,28},{24,16},{28,20},{1,9},{5... | collective-permute-start | bytes 1671176 | tf_op jit(solution)/shard_map/ppermute | solution.py:19
  341.9 10.2 %collective-permute-start.59 = (bf16[256,256]{1,0:T(8,128)(2,1)S(1)}, bf16[256,256]{1,0:T(8,128)(2,1)S(1)}, u32[]{:S(2)}, u32[]{:S(2)}) collective-permute-start(bf16[256,256]{1,0:T(8,128)(2,1)S(1)} %get-tuple-element.161), channel_id=1, source_target_pairs={{0,2},{1,3},{2,0},{3,1},{4,6},{5,7},{6,4},{7,5},{8,10},{9,11},{10,... | collective-permute-start | bytes 393224 | tf_op jit(solution)/shard_map/ppermute | solution.py:24
  352.1 7.1 %collective-permute-start.58 = (bf16[256,256]{1,0:T(8,128)(2,1)S(1)}, bf16[256,256]{1,0:T(8,128)(2,1)S(1)}, u32[]{:S(2)}, u32[]{:S(2)}) collective-permute-start(bf16[256,256]{1,0:T(8,128)(2,1)S(1)} %get-tuple-element.159), channel_id=1, source_target_pairs={{0,1},{1,2},{2,3},{3,0},{4,5},{5,6},{6,7},{7,4},{8,9},{9,10},{10,1... | collective-permute-start | bytes 393224 | tf_op jit(solution)/shard_map/ppermute | solution.py:24
  362.6 18.6 %collective-permute-start.53 = (bf16[272,256]{1,0:T(8,128)(2,1)S(1)}, bf16[272,256]{1,0:T(8,128)(2,1)S(1)}, u32[]{:S(2)}, u32[]{:S(2)}) collective-permute-start(bf16[272,256]{1,0:T(8,128)(2,1)S(1)} %get-tuple-element.157), channel_id=1, source_target_pairs={{0,3},{1,0},{2,1},{3,2},{4,7},{5,4},{6,5},{7,6},{8,11},{9,8},{10,9... | collective-permute-start | bytes 417800 | tf_op jit(solution)/shard_map/ppermute | solution.py:24
  374.4 12.4 %collective-permute-start.52 = (bf16[272,256]{1,0:T(8,128)(2,1)}, bf16[272,256]{1,0:T(8,128)(2,1)}, u32[]{:S(2)}, u32[]{:S(2)}) collective-permute-start(bf16[272,256]{1,0:T(8,128)(2,1)} %get-tuple-element.158), channel_id=1, source_target_pairs={{0,2},{1,3},{2,0},{3,1},{4,6},{5,7},{6,4},{7,5},{8,10},{9,11},{10,... | collective-permute-start | bytes 417800 | tf_op jit(solution)/shard_map/ppermute | solution.py:24
  374.4 12.4 %collective-permute-start.51 = (bf16[272,256]{1,0:T(8,128)(2,1)}, bf16[272,256]{1,0:T(8,128)(2,1)}, u32[]{:S(2)}, u32[]{:S(2)}) collective-permute-start(bf16[272,256]{1,0:T(8,128)(2,1)} %get-tuple-element.156), channel_id=1, source_target_pairs={{0,1},{1,2},{2,3},{3,0},{4,5},{5,6},{6,7},{7,4},{8,9},{9,10},{10,1... | collective-permute-start | bytes 417800 | tf_op jit(solution)/shard_map/ppermute | solution.py:24
  379.1 23.8 %collective-permute-start.64 = (bf16[128,3456]{1,0:T(8,128)(2,1)}, bf16[128,3456]{1,0:T(8,128)(2,1)}, u32[]{:S(2)}, u32[]{:S(2)}) collective-permute-start(bf16[128,3456]{1,0:T(8,128)(2,1)} %get-tuple-element.143), channel_id=1, source_target_pairs={{0,24},{4,28},{8,16},{12,20},{16,8},{20,12},{24,0},{28,4},{1,25},{... | collective-permute-start | bytes 2654216 | tf_op jit(solution)/shard_map/ppermute | solution.py:19
  380.7 39.4 %collective-permute-start.63 = (bf16[128,3456]{1,0:T(8,128)(2,1)}, bf16[128,3456]{1,0:T(8,128)(2,1)}, u32[]{:S(2)}, u32[]{:S(2)}) collective-permute-start(bf16[128,3456]{1,0:T(8,128)(2,1)} %get-tuple-element.144), channel_id=1, source_target_pairs={{0,16},{4,20},{8,24},{12,28},{16,0},{20,4},{24,8},{28,12},{1,17},{... | collective-permute-start | bytes 2654216 | tf_op jit(solution)/shard_map/ppermute | solution.py:19
  381.3 38.8 %collective-permute-start.62 = (bf16[128,3456]{1,0:T(8,128)(2,1)}, bf16[128,3456]{1,0:T(8,128)(2,1)}, u32[]{:S(2)}, u32[]{:S(2)}) collective-permute-start(bf16[128,3456]{1,0:T(8,128)(2,1)} %get-tuple-element.142), channel_id=1, source_target_pairs={{0,8},{4,12},{8,0},{12,4},{16,24},{20,28},{24,16},{28,20},{1,9},{5... | collective-permute-start | bytes 2654216 | tf_op jit(solution)/shard_map/ppermute | solution.py:19
  (64 other events, 637.0 us)

commit v3 on v2

--- a/solution.py
+++ b/solution.py
@@ -10,18 +10,26 @@
 INNER = 8
 BF = jnp.bfloat16
 F32 = jnp.float32
-VMEM_LIMIT = 26 << 20
-
-
-def dp_swap(value, step):
+VMEM_LIMIT = 12 << 20
+
+
+def dp_swap(value, step, tag):
     size = lax.axis_size("dp")
     hop = step * (size // INNER)
-    return lax.ppermute(value, "dp", [(i, i ^ hop) for i in range(size)])
-
-
-def z_shift(value, step):
+    with jax.named_scope(f"{tag}_dp{step}"):
+        return lax.ppermute(value, "dp", [(i, i ^ hop) for i in range(size)])
+
+
+def z_shift(value, step, tag):
     size = lax.axis_size("tensor")
-    return lax.ppermute(value, "tensor", [(i, (i + step) % size) for i in range(size)])
+    with jax.named_scope(f"{tag}_z"):
+        return lax.ppermute(value, "tensor", [(i, (i + step) % size) for i in range(size)])
+
+
+def z_swap(value, step, tag):
+    size = lax.axis_size("tensor")
+    with jax.named_scope(f"{tag}_z{step}"):
+        return lax.ppermute(value, "tensor", [(i, i ^ step) for i in range(size)])
 
 
 def after(value, *events):
@@ -44,9 +52,9 @@
     return jax.ShapeDtypeStruct(dims, dtype)
 
 
-def whole_call(kernel, name, outs, args, scalars=0, hbm=0, scratch=(), flops=0, extra=0):
+def whole_call(kernel, name, outs, args, scalars=0, hbm=0, scratch=(), flops=0, extra=0, alias=None):
     specs = [pl.BlockSpec(memory_space=pltpu.SMEM)] * scalars
-    specs += [pl.BlockSpec(memory_space=pl.ANY)] * hbm
+    specs += [pl.BlockSpec(memory_space=pltpu.HBM)] * hbm
     specs += [pl.BlockSpec(memory_space=pltpu.VMEM)] * (len(args) - scalars - hbm)
     moved = sum(a.size * a.dtype.itemsize for a in args) + sum(
         o.size * jnp.dtype(o.dtype).itemsize for o in outs
@@ -57,19 +65,33 @@
         in_specs=specs,
         out_specs=[pl.BlockSpec(memory_space=pltpu.VMEM)] * len(outs),
         scratch_shapes=list(scratch),
+        input_output_aliases=alias or {},
         compiler_params=pltpu.CompilerParams(vmem_limit_bytes=VMEM_LIMIT),
-        cost_estimate=pl.CostEstimate(flops=flops, bytes_accessed=moved, transcendentals=extra),
+        cost_estimate=pl.CostEstimate(flops=1, bytes_accessed=1, transcendentals=0),
         name=name,
     )(*args)
 
 
-def pair_up(own, other):
+def plane_send(local, tag, kqs, *waits):
+    return [dp_swap(after(local, *waits), 2 * kq, tag) for kq in kqs]
+
+
+def core_pairs(own, tag, *waits):
+    other = [dp_swap(after(piece, *waits) if waits else piece, 1, tag) for piece in own]
     return [piece for pair in zip(own, other) for piece in pair]
 
 
-def plane_gather(local):
-    own = [local] + [dp_swap(local, 2 * kq) for kq in (1, 2, 3)]
-    return pair_up(own, [dp_swap(piece, 1) for piece in own])
+def z_send(local, tag, steps, *waits):
+    local = after(local, *waits) if waits else local
+    return [z_swap(local, step, tag) for step in steps]
+
+
+def z_return(parts, tag, *waits):
+    total = parts[0].astype(F32)
+    for step in range(1, len(parts)):
+        part = after(parts[step], *waits) if waits else parts[step]
+        total = total + z_swap(part, step, tag).astype(F32)
+    return total
 
 
 def place_mixer_kernel(with_small, idx_ref, *refs):
@@ -81,7 +103,7 @@
     for k in range(8):
         at = pl.multiple_of(jnp.bitwise_xor(me, k) * rows, rows)
         for s in range(n_z):
-            col = pl.multiple_of(lax.rem(z + n_z - s, n_z) * 256, 256)
+            col = pl.multiple_of(jnp.bitwise_xor(z, s) * 256, 256)
             for st in range(2):
                 copies.append(
                     pltpu.make_async_copy(
@@ -118,21 +140,13 @@
 
 
 def place_ffn_kernel(idx_ref, *refs):
-    pieces, (gu_ref, down_ref), sems = refs[:8], refs[8:10], refs[10]
+    pieces, out_ref, sems = refs[:8], refs[8], refs[9]
     me = idx_ref[0]
-    rows = gu_ref.shape[0] // 8
-    split = gu_ref.shape[1]
+    rows = out_ref.shape[0] // 8
     copies = []
     for k in range(8):
         at = pl.ds(pl.multiple_of(jnp.bitwise_xor(me, k) * rows, rows), rows)
-        copies.append(
-            pltpu.make_async_copy(pieces[k].at[:, pl.ds(0, split)], gu_ref.at[at], sems.at[k, 0])
-        )
-        copies.append(
-            pltpu.make_async_copy(
-                pieces[k].at[:, pl.ds(split, split // 2)], down_ref.at[at], sems.at[k, 1]
-            )
-        )
+        copies.append(pltpu.make_async_copy(pieces[k], out_ref.at[at], sems.at[k]))
     for copy in copies:
         copy.start()
     for copy in copies:
@@ -144,39 +158,48 @@
     return whole_call(
         place_ffn_kernel,
         "place_ffn",
-        [shape(8 * rows, columns // 3 * 2), shape(8 * rows, columns // 3)],
+        [shape(8 * rows, columns)],
         (index, *pieces),
         scalars=1,
         hbm=8,
-        scratch=[pltpu.SemaphoreType.DMA((8, 2))],
-    )
-
-
-def ffn_kernel(n_ref, d_ref, gu_ref, down_ref, dn_ref, part_ref, hid_ref, dgu_ref):
-    units = down_ref.shape[1]
-    both = mm(n_ref[...], gu_ref[...])
+        scratch=[pltpu.SemaphoreType.DMA((8,))],
+    )[0]
+
+
+def ffn_kernel(step, n_ref, d_ref, w_ref, *refs):
+    dn_ref, part_ref, n_all_ref, d_all_ref, hid_ref, dgu_ref = refs[-6:]
+    tokens = n_ref.shape[0]
+    own = slice(step * tokens, (step + 1) * tokens)
+    units = w_ref.shape[1] // 3
+    gu, down = slice(0, 2 * units), slice(2 * units, 3 * units)
+    n_all_ref[own] = n_ref[...]
+    d_all_ref[own] = d_ref[...]
+    both = mm(n_ref[...], w_ref[:, gu])
     gate, up = both[:, :units], both[:, units:]
     sig = jax.nn.sigmoid(gate)
     silu = gate * sig
     hidden = (silu * up).astype(BF)
-    hid_ref[...] = hidden
-    d_hidden = mm(d_ref[...], down_ref[...])
-    dgu_ref[:, :units] = (d_hidden * up * (sig * (1.0 + gate * (1.0 - sig)))).astype(BF)
-    dgu_ref[:, units:] = (d_hidden * silu).astype(BF)
-    dn_ref[...] = mm_nt(dgu_ref[...], gu_ref[...]).astype(BF)
-    part_ref[...] = mm_nt(hidden, down_ref[...]).astype(BF)
-
-
-def ffn_piece(normed, d_out, w_gu, w_down):
+    hid_ref[own] = hidden
+    d_hidden = mm(d_ref[...], w_ref[:, down])
+    dgu_ref[own, :units] = (d_hidden * up * (sig * (1.0 + gate * (1.0 - sig)))).astype(BF)
+    dgu_ref[own, units:] = (d_hidden * silu).astype(BF)
+    dn_ref[...] = mm_nt(dgu_ref[own], w_ref[:, gu]).astype(BF)
+    part_ref[...] = mm_nt(hidden, w_ref[:, down]).astype(BF)
+
+
+def ffn_piece(step, steps, normed, d_out, weights, kept):
     tokens, width = normed.shape
-    units = w_down.shape[1]
-    return whole_call(
-        ffn_kernel,
+    units = weights.shape[1] // 3
+    every = steps * tokens
+    return whole_call(
+        functools.partial(ffn_kernel, step),
         "ffn_piece",
-        [shape(tokens, width)] * 2 + [shape(tokens, units), shape(tokens, 2 * units)],
-        (normed, d_out, w_gu, w_down),
+        [shape(tokens, width)] * 2
+        + [shape(every, width), shape(every, width), shape(every, units), shape(every, 2 * units)],
+        (normed, d_out, weights, *kept),
         flops=12 * tokens * width * units,
         extra=tokens * units,
+        alias={3 + i: 2 + i for i in range(len(kept))},
     )
 
 
@@ -338,7 +361,7 @@
 def mixer_grad_kernel(with_halo, idx_ref, *refs):
     n_in = 7 if with_halo else 4
     ins, away_ref, home_ref = refs[:n_in], refs[n_in], refs[n_in + 1]
-    me = idx_ref[0]
+    me, my_z = idx_ref[0], idx_ref[1]
     quad, core = me // 2, lax.rem(me, 2)
     n_z, ch = away_ref.shape[1], away_ref.shape[3]
     rows = ins[0].shape[1] // 8
@@ -359,8 +382,9 @@
             grad = grad.astype(BF)
             for z in range(n_z):
                 cols = slice(z * ch, (z + 1) * ch)
-                away_ref[kq, z, st * rows : (st + 1) * rows] = grad[:rows, cols]
-                home_ref[kq, z, st * rows : (st + 1) * rows] = grad[rows:, cols]
+                at_z = jnp.bitwise_xor(my_z, z)
+                away_ref[kq, at_z, st * rows : (st + 1) * rows] = grad[:rows, cols]
+                home_ref[kq, at_z, st * rows : (st + 1) * rows] = grad[rows:, cols]
         if with_halo:
             for ref, at in ((away_ref, away), (home_ref, home)):
                 values = ins[6][:, pl.ds(at, rows)]
@@ -392,7 +416,7 @@
 
     @pl.loop(0, count)
     def _(i):
-        chip = jnp.bitwise_xor(quad, first - i) * 2
+        chip = jnp.bitwise_xor(quad, first + i) * 2
         away = pl.multiple_of((chip + 1 - core) * rows, rows)
         home = pl.multiple_of((chip + core) * rows, rows)
         left = jnp.concatenate([n_ref[:, pl.ds(away, rows)], n_ref[:, pl.ds(home, rows)]], axis=1)
@@ -418,9 +442,9 @@
     )
 
 
-def plane_reduce(halves):
-    arrived = {kq: dp_swap(halves[kq], 2 * kq) for kq in (3, 1, 2)}
-    return halves[0].astype(F32) + arrived[1].astype(F32) + arrived[2].astype(F32) + arrived[3].astype(F32)
+def core_sum(away, home, count, tag):
+    other = dp_swap(away, 1, tag)
+    return [(home[kq].astype(F32) + other[kq].astype(F32)).astype(BF) for kq in range(count)]
 
 
 def body(
@@ -471,27 +495,36 @@
     groups = [[i * outer + o for o in range(outer)] for i in range(INNER)]
     if outer > 1:
         wide = functools.partial(lax.all_gather, axis_name="dp", tiled=True, axis_index_groups=groups)
-        mix_bu, mix_co, ffn_own = wide(mix_bu, axis=1), wide(mix_co, axis=1), wide(ffn_own, axis=0)
-        small = wide(small, axis=1)
+        mix_bu, mix_co, small = wide(mix_bu, axis=1), wide(mix_co, axis=1), wide(small, axis=1)
+        ffn_own = wide(ffn_own, axis=0)
     n_small = small.shape[0]
     small_rows = jnp.pad(small, ((0, 16 - n_small), (0, channels - block)))
     bu_rows, co_rows = (m.reshape(2 * block, channels) for m in (mix_bu, mix_co))
 
-    bu_set = [bu_rows] + [z_shift(bu_rows, s) for s in range(1, n_z)]
-    bu_pieces = plane_gather(jnp.concatenate(bu_set + [small_rows], axis=0))
-    co_set = [co_rows] + [z_shift(co_rows, s) for s in range(1, n_z)]
-    co_pieces = plane_gather(jnp.concatenate(co_set, axis=0))
-    w_b, w_u, small_all = place_mixer(index, bu_pieces, width, n_z, True)
-    w_c, w_o = place_mixer(index, co_pieces, width, n_z, False)
-    w_gu_all, w_down_all = place_ffn(index, plane_gather(ffn_own))
-
-    before = z_shift(layer_in[:, own_len - reach :].reshape(row_count, reach * width), 1)
+    steps = tuple(range(1, n_z))
+    tails = layer_in[:, own_len - reach :].reshape(row_count, reach * width)
+    before = z_shift(tails, 1, "tail")
     every = before[None]
     if outer > 1:
         every = lax.all_gather(before, "dp", axis=0, axis_index_groups=groups)
     every = every[None]
-    for step in (1, 2, 4):
-        every = jnp.concatenate([every, dp_swap(every, step)], axis=0)
+    every = jnp.concatenate([every, dp_swap(every, 1, "tail")], axis=0)
+    bu_set = z_send(bu_rows, "bu", steps)
+    co_set = z_send(co_rows, "co", steps, *bu_set)
+    ffn_near = plane_send(ffn_own, "ffn", (1, 2))
+    d_ffn = jnp.where(valid[:, :, None], cotangent, jnp.zeros_like(cotangent)).reshape(tokens, width)
+
+    gate = (*ffn_near, every)
+    bu_rows = jnp.concatenate([bu_rows] + bu_set + [small_rows], axis=0)
+    bu_set = plane_send(bu_rows, "bu", (1, 2, 3), *gate)
+    dy_set = z_send(d_ffn, "dy", (1, 2), *gate, *co_set)
+    every = jnp.concatenate([every, dp_swap(after(every, *gate), 2, "tail")], axis=0)
+
+    gate = (*bu_set, *dy_set, every)
+    co_rows = jnp.concatenate([co_rows] + co_set, axis=0)
+    co_set = plane_send(co_rows, "co", (1, 2, 3), *gate)
+    dy_set = dy_set + [z_swap(after(dy_set[1], *gate), 1, "dy_on")]
+    every = jnp.concatenate([every, dp_swap(after(every, *gate), 4, "tail")], axis=0)
     slots = INNER * outer * row_count
     rel = jnp.bitwise_xor(me_in, jnp.arange(INNER, dtype=jnp.int32))
     slot_rows = row_order.reshape(INNER, outer * row_count)[rel].reshape(slots)
@@ -501,70 +534,76 @@
     before_mask = jnp.logical_and(before_mask, z == 0).astype(BF)
     crossed = mm(before_mask, every.reshape(slots, reach * width))
     x_halo = jnp.where(z == 0, crossed.astype(BF), before).reshape(row_count * reach, width)
-
-    d_ffn = jnp.where(valid[:, :, None], cotangent, jnp.zeros_like(cotangent)).reshape(tokens, width)
-    d_ffn_set = [d_ffn] + [z_shift(d_ffn, s) for s in range(1, n_z)]
-
     x_own = layer_in.reshape(tokens, width)
+    w_b, w_u, small_all = place_mixer(index, core_pairs([bu_rows] + bu_set, "bu"), width, n_z, True)
     n_one, n_halo, b_own, u_own, b_halo, u_halo, mixed, mixed_halo, conv = mixer_in(
         own_len, x_own, x_halo, small_all, w_b, w_u
     )
+
+    gate = (*co_set, dy_set[2], n_one)
+    ffn_far = plane_send(ffn_own, "ffn", (3,), *gate)
+    w_c, w_o = place_mixer(index, core_pairs([co_rows] + co_set, "co"), width, n_z, False)
     c_own, gated, middle, n_two = mixer_out(x_own, n_one, conv, small_all, w_c, w_o)
-
-    n_two_set = [n_two] + [z_shift(n_two, s) for s in range(1, n_z)]
-    order = [0, 1, 3, 2] if n_z == 4 else list(range(n_z))
-    runs = {s: ffn_piece(n_two_set[s], d_ffn_set[s], w_gu_all, w_down_all) for s in order}
-    d_parts = [runs[0][0]] + [z_shift(runs[s][0], n_z - s) for s in order[1:]]
-
-    n_all = jnp.concatenate([n_two_set[s] for s in order], axis=0)
-    d_all = jnp.concatenate([d_ffn_set[s] for s in order], axis=0)
-    hid_all = jnp.concatenate([runs[s][2] for s in order], axis=0)
-    dgu_all = jnp.concatenate([runs[s][3] for s in order], axis=0)
-    away, home = ffn_grads(index, 3, 4, n_all, d_all, hid_all, dgu_all)
-    other = dp_swap(away, 1)
-    halves = [(home[3 - kq].astype(F32) + other[3 - kq].astype(F32)).astype(BF) for kq in range(4)]
-    ffn_total = plane_reduce(halves)
-
+    ffn_set = [ffn_own] + ffn_near + ffn_far
+    w_ffn = place_ffn(index, core_pairs(ffn_set[:3], "ffn", *gate) + core_pairs(ffn_set[3:], "ffn"))
+    d_ffn_set = [d_ffn] + dy_set
+    n_two_set = [n_two] + z_send(n_two, "n2", (1, 2))
+    n_two_set = n_two_set + z_send(n_two_set[2], "n2_on", (1,))
+    d_parts, out_parts, kept = [], [], ()
+    for s in range(n_z):
+        d_part, out_part, *kept = ffn_piece(s, n_z, n_two_set[s], d_ffn_set[s], w_ffn, kept)
+        d_parts.append(z_swap(d_part, s, "dn") if s else d_part)
+        out_parts.append(out_part)
+
+    away, home = ffn_grads(index, 0, 4, *kept)
+    gf_set = core_sum(away, home, 4, "gf")
+    gf_near = [dp_swap(after(gf_set[kq], d_parts[1]), 2 * kq, "gf") for kq in (1, 2)]
     d_mix, d_b, d_u, d_c, d_b_halo, d_u_halo, grad_mid, d_x_halo, small_grads = mixer_back(
         own_len,
-        d_parts,
+        [after(d_parts[0], *gf_near)] + d_parts[1:],
         (middle, d_ffn, x_own, x_halo, small_all, b_own, u_own, c_own, b_halo, u_halo, mixed, mixed_halo, conv),
         (w_b, w_u, w_c, w_o),
     )
     co_away, co_home = mixer_grads(index, (n_one, d_c, d_mix, gated), n_z, block, False)
     d_bu_halo = jnp.concatenate([d_b_halo, d_u_halo], axis=1)
+    co_halves = core_sum(co_away, co_home, 4, "gco")
     bu_away, bu_home = mixer_grads(
-        index, (n_one, d_b, n_one, d_u, n_halo, d_bu_halo, small_grads), n_z, block, True
-    )
-
-    def mixer_reduce(away, home):
-        other = dp_swap(away, 1)
-        halves = [(home[kq].astype(F32) + other[kq].astype(F32)).astype(BF) for kq in range(4)]
-        plane = plane_reduce(halves).astype(BF)
-        total = lax.dynamic_index_in_dim(plane, z, 0, keepdims=False).astype(F32)
-        for s in range(1, n_z):
-            piece = lax.dynamic_index_in_dim(plane, lax.rem(z + s, n_z), 0, keepdims=False)
-            total = total + z_shift(piece, s).astype(F32)
-        return total
-
-    co_total = mixer_reduce(co_away, co_home)
-    bu_total = mixer_reduce(bu_away, bu_home)
-
-    ffn_sum = runs[0][1].astype(F32)
-    for s in order[1:]:
-        ffn_sum = ffn_sum + z_shift(runs[s][1], n_z - s).astype(F32)
-    layer_out = (middle + ffn_sum).astype(BF).reshape(row_count, own_len, width)
-
+        index, (after(n_one, *co_halves), d_b, n_one, d_u, n_halo, d_bu_halo, small_grads), n_z, block, True
+    )
+    bu_halves = core_sum(bu_away, bu_home, 4, "gbu")
+
+    gco_set = [dp_swap(co_halves[kq], 2 * kq, "gco") for kq in (1, 2, 3)]
+    out_on = z_swap(after(out_parts[3], d_mix), 1, "out_on")
+    out_first = z_swap(after(out_parts[1], d_mix), 1, "out")
     back = d_x_halo.reshape(row_count, reach * width)
     spread = mm_tn(before_mask, back).astype(BF).reshape(INNER, outer * row_count, reach * width)
-    for step in (4, 2, 1):
-        spread = (spread[:step].astype(F32) + dp_swap(spread[step:], step).astype(F32)).astype(BF)
-    returned = spread[0]
+
+    def fold(spread, step, *waits):
+        arrived = dp_swap(after(spread[step:], *waits), step, "back").astype(F32)
+        return (spread[:step].astype(F32) + arrived).astype(BF)
+
+    spread = fold(spread, 4, *co_halves)
+    gate = (*gco_set, out_on, out_first, spread)
+    gbu_set = [dp_swap(after(bu_halves[kq], *gate), 2 * kq, "gbu") for kq in (1, 2, 3)]
+    co_plane = co_halves[0].astype(F32) + sum(piece.astype(F32) for piece in gco_set)
+    co_total = z_return(list(co_plane.astype(BF)), "gco")
+    out_second = (out_parts[2].astype(F32) + out_on.astype(F32)).astype(BF)
+    out_second = z_swap(after(out_second, *gate), 2, "out")
+    layer_out = middle + out_parts[0].astype(F32) + out_first.astype(F32) + out_second.astype(F32)
+    layer_out = layer_out.astype(BF).reshape(row_count, own_len, width)
+    spread = fold(spread, 2, *gate)
+
+    gate = (*gbu_set, co_total, out_second, spread)
+    gf_far = dp_swap(after(gf_set[3], *gate), 6, "gf")
+    ffn_total = gf_set[0].astype(F32) + sum(piece.astype(F32) for piece in (*gf_near, gf_far))
+    bu_plane = bu_halves[0].astype(F32) + sum(piece.astype(F32) for piece in gbu_set)
+    bu_total = z_return(list(bu_plane.astype(BF)), "gbu", *gate)
+    returned = fold(spread, 1, *gate)[0]
     if outer > 1:
         returned = lax.psum_scatter(
             returned, "dp", scatter_dimension=0, tiled=True, axis_index_groups=groups
         )
-    returned = z_shift(jnp.where(z == 0, returned, back), n_z - 1)
+    returned = z_shift(jnp.where(z == 0, returned, back), n_z - 1, "back")
     returned = returned.astype(F32).reshape(row_count, reach, width)
     grad_in = grad_mid.reshape(row_count, own_len, width)
     grad_in = grad_in + jnp.pad(returned, ((0, 0), (own_len - reach, 0), (0, 0)))

time: 435 us -> 398 us (0.915)
  waiting for transfers between devices: 184 us -> 232 us
  local copies, waits for them, and re-layouts: 52.7 us -> 20.3 us
  starting transfers between devices: 90.1 us -> 60.8 us
  other arithmetic: 40.2 us -> 21 us
    ppermute x0 -> x24, waiting for transfers between devices: none -> 121 us  [z_swap(): return lax.ppermute(value, 'tensor', [(i, i ^ step) for i in range(size)])]
    ppermute x26 -> x2, waiting for transfers between devices: 93 us -> 2.95 us  [z_shift(): lax.ppermute(value, 'tensor', [(i, (i + step) % size) for i in range(size)])]
    ppermute x26 -> x2, starting transfers between devices: 60.7 us -> 3.06 us  [z_shift(): lax.ppermute(value, 'tensor', [(i, (i + step) % size) for i in range(size)])]
    unnamed x137 -> x85, local copies, waits for them, and re-layouts: 44.6 us -> 15.5 us
    ppermute x0 -> x24, starting transfers between devices: none -> 27.9 us  [z_swap(): return lax.ppermute(value, 'tensor', [(i, i ^ step) for i in range(size)])]
    ppermute x39, waiting for transfers between devices: 91.1 us -> 109 us  [dp_swap(): return lax.ppermute(value, 'dp', [(i, i ^ hop) for i in range(size)])]
    concatenate x8 -> x4, other arithmetic: 16.6 us -> 3.95 us  [the longest x1 1.28 us: body(): bu_rows = jnp.concatenate([bu_rows] + bu_set + [small_rows], axis=0)]
    convert_element_type x8 -> x9, other arithmetic: 12.3 us -> 8.98 us  [the longest x3 4.84 us: core_sum(): (home[kq].astype(F32) + other[kq].astype(F32)).astype(BF)]
  transfers between devices with their start and end apart: 65 -> 65, of which waited for: 27 -> 32; matrix products, arithmetic and copies ran while one was open for 12% -> 7% of each run, Pallas kernels for 8% -> 6%
where the time goes in v3:
time: 398 us; the launch traced here: 390 us
  waiting for transfers between devices  232 us (58%)
  starting transfers between devices  60.8 us (15%)
  Pallas kernels  52.4 us (13%)
  other arithmetic  21 us (5%)
  local copies, waits for them, and re-layouts  20.3 us (5%)
    ppermute x24, waiting for transfers between devices, z_swap(): return lax.ppermute(value, 'tensor', [(i, i ^ step) for i in range(size)])  121 us
    ppermute x39, waiting for transfers between devices, dp_swap(): return lax.ppermute(value, 'dp', [(i, i ^ hop) for i in range(size)])  109 us
    pallas_call x13, Pallas kernels, whole_call(): pl.pallas_call(kernel, out_shape=outs, in_specs=specs, out_specs=[pl.Bloc...  52.4 us
    ppermute x39, starting transfers between devices, dp_swap(): return lax.ppermute(value, 'dp', [(i, i ^ hop) for i in range(size)])  29.9 us
    ppermute x24, starting transfers between devices, z_swap(): return lax.ppermute(value, 'tensor', [(i, i ^ step) for i in range(size)])  27.9 us
    unnamed x85, local copies, waits for them, and re-layouts  15.5 us
  transfers between devices with their start and end apart: 65, of which 32 were waited for; matrix products, arithmetic and copies ran while one was open for 7% of the time, Pallas kernels for 6%

profile of v3, /device:TPU:0, one launch (start us, length us, event | category | flops | bytes accessed | tf_op | source)
XLA Modules:
  0.0 390.0 jit_solution(10292786762729536081)
XLA Ops:
  1.7 5.1 %collective-permute-start.7 = (bf16[256,256]{1,0:T(8,128)(2,1)S(1)}, bf16[256,256]{1,0:T(8,128)(2,1)}, u32[]{:S(2)}, u32[]{:S(2)}) collective-permute-start(bf16[256,256]{1,0:T(8,128)(2,1)S(1)} %bitcast.126), channel_id=1, source_target_pairs={{0,3},{1,2},{2,1},{3,0},{4,7},{5,6},{6,5},{7,4},{8,11},{9,10},{10,... | collective-permute-start | bytes 393224 | tf_op jit(solution)/shard_map/bu_z3/ppermute | solution.py:32
  9.0 1.6 collective-permute-start.3
  10.6 1.5 collective-permute-start.2
  15.1 2.9 collective-permute-done
  20.7 4.9 %collective-permute-done.5 = bf16[256,256]{1,0:T(8,128)(2,1)S(1)} collective-permute-done((bf16[256,256]{1,0:T(8,128)(2,1)S(1)}, bf16[256,256]{1,0:T(8,128)(2,1)S(1)}, u32[]{:S(2)}, u32[]{:S(2)}) %collective-permute-start.5) | collective-permute-done | bytes 131104 | tf_op jit(solution)/shard_map/bu_z1/ppermute | solution.py:32
  25.6 1.9 collective-permute-start.13
  27.7 2.3 collective-permute-start.11
  30.6 1.6 constant_dynamic-update-slice_fusion.2
  32.2 1.6 constant_dynamic-update-slice_fusion.1
  42.6 18.3 %collective-permute-done.4 = bf16[2,1,8,2048]{3,2,1,0:T(8,128)(2,1)S(1)} collective-permute-done((bf16[2,1,8,2048]{3,2,1,0:T(8,128)(2,1)S(1)}, bf16[2,1,8,2048]{3,2,1,0:T(8,128)(2,1)S(1)}, u32[]{:S(2)}, u32[]{:S(2)}) %collective-permute-start.4) | collective-permute-done | bytes 65568 | tf_op jit(solution)/shard_map/tail_dp2/ppermute | solution.py:20
  62.0 2.8 collective-permute-done.15.d_ref
  67.4 8.5 %collective-permute-done.14.d_ref = bf16[256,1024]{1,0:T(8,128)(2,1)S(1)} collective-permute-done((bf16[256,1024]{1,0:T(8,128)(2,1)S(1)}, bf16[256,1024]{1,0:T(8,128)(2,1)S(1)}, u32[]{:S(2)}, u32[]{:S(2)}) %collective-permute-start.14) | collective-permute-done | bytes 524320 | tf_op jit(solution)/shard_map/dy_z1/ppermute | solution.py:32
  76.8 1.6 collective-permute-start.16
  79.6 1.5 collective-permute-start.26
  81.1 10.8 %collective-permute-done.16 = bf16[4,1,8,2048]{3,2,1,0:T(8,128)(2,1)} collective-permute-done((bf16[4,1,8,2048]{3,2,1,0:T(8,128)(2,1)S(1)}, bf16[4,1,8,2048]{3,2,1,0:T(8,128)(2,1)}, u32[]{:S(2)}, u32[]{:S(2)}) %collective-permute-start.16) | collective-permute-done | bytes 131104 | tf_op jit(solution)/shard_map/tail_dp4/ppermute | solution.py:20
  91.9 3.1 collective-permute-start.24
  99.9 3.3 place_small.1
  103.3 2.4 mixer_in.1
  105.8 1.5 collective-permute-start.32
  110.9 2.9 place_mixer.1
  113.8 1.4 mixer_out.1
  115.2 2.0 collective-permute-start.35
  117.7 11.0 %collective-permute-done.32.refs_6_ = bf16[128,3456]{1,0:T(8,128)(2,1)S(1)} collective-permute-done((bf16[128,3456]{1,0:T(8,128)(2,1)S(1)}, bf16[128,3456]{1,0:T(8,128)(2,1)S(1)}, u32[]{:S(2)}, u32[]{:S(2)}) %collective-permute-start.32) | collective-permute-done | bytes 884768 | tf_op jit(solution)/shard_map/ffn_dp6/ppermute | solution.py:20
  128.7 2.0 collective-permute-start.34
  130.7 10.7 %collective-permute-done.35.n_ref = bf16[256,1024]{1,0:T(8,128)(2,1)S(1)} collective-permute-done((bf16[256,1024]{1,0:T(8,128)(2,1)S(1)}, bf16[256,1024]{1,0:T(8,128)(2,1)S(1)}, u32[]{:S(2)}, u32[]{:S(2)}) %collective-permute-start.35) | collective-permute-done | bytes 524320 | tf_op jit(solution)/shard_map/n2_z2/ppermute | solution.py:32
  141.5 2.3 place_ffn.1.w_ref
  143.8 4.2 %ffn_piece.4 = (bf16[256,1024]{1,0:T(8,128)(2,1)S(1)}, bf16[256,1024]{1,0:T(8,128)(2,1)S(1)}, bf16[1024,1024]{1,0:T(8,128)(2,1)S(1)}, bf16[1024,1024]{1,0:T(8,12...) custom-call(bf16[256,1024]{1,0:T(8,128)(2,1)S(1)} %get-tuple-element.107.n_ref, ...), custom_call_target="tpu_custom_call" | custom-call | flops 1 | bytes 1 | tf_op jit(solution)/shard_map/ffn_piece/pallas_call | solution.py:62
  147.9 4.7 %collective-permute-done.34.n_ref = bf16[256,1024]{1,0:T(8,128)(2,1)S(1)} collective-permute-done((bf16[256,1024]{1,0:T(8,128)(2,1)S(1)}, bf16[256,1024]{1,0:T(8,128)(2,1)S(1)}, u32[]{:S(2)}, u32[]{:S(2)}) %collective-permute-start.34) | collective-permute-done | bytes 524320 | tf_op jit(solution)/shard_map/n2_z1/ppermute | solution.py:32
  152.6 4.2 %ffn_piece.5 = (bf16[256,1024]{1,0:T(8,128)(2,1)S(1)}, bf16[256,1024]{1,0:T(8,128)(2,1)S(1)}, bf16[1024,1024]{1,0:T(8,128)(2,1)S(1)}, bf16[1024,1024]{1,0:T(8,12...) custom-call(bf16[256,1024]{1,0:T(8,128)(2,1)S(1)} %collective-permut, ...), custom_call_target="tpu_custom_call", output_to_operand_aliasing={{2}: (3, {}), {3}: (4, {}), {4}: (5, {}), {5}: (6, {})} | custom-call | flops 1 | bytes 1 | tf_op jit(solution)/shard_map/ffn_piece/pallas_call | solution.py:62
  156.8 4.2 %ffn_piece.6 = (bf16[256,1024]{1,0:T(8,128)(2,1)S(1)}, bf16[256,1024]{1,0:T(8,128)(2,1)S(1)}, bf16[1024,1024]{1,0:T(8,128)(2,1)S(1)}, bf16[1024,1024]{1,0:T(8,12...) custom-call(bf16[256,1024]{1,0:T(8,128)(2,1)S(1)} %collective-permut, ...), custom_call_target="tpu_custom_call", output_to_operand_aliasing={{2}: (3, {}), {3}: (4, {}), {4}: (5, {}), {5}: (6, {})} | custom-call | flops 1 | bytes 1 | tf_op jit(solution)/shard_map/ffn_piece/pallas_call | solution.py:62
  160.9 2.9 collective-permute-done.36.n_ref
  163.8 5.5 %ffn_piece.7 = (bf16[256,1024]{1,0:T(8,128)(2,1)S(1)}, bf16[256,1024]{1,0:T(8,128)(2,1)S(1)}, bf16[1024,1024]{1,0:T(8,128)(2,1)S(1)}, bf16[1024,1024]{1,0:T(8,12...) custom-call(bf16[256,1024]{1,0:T(8,128)(2,1)S(1)} %collective-permut, ...), custom_call_target="tpu_custom_call", output_to_operand_aliasing={{2}: (3, {}), {3}: (4, {}), {4}: (5, {}), {5}: (6, {})} | custom-call | flops 1 | bytes 1 | tf_op jit(solution)/shard_map/ffn_piece/pallas_call | solution.py:62
  170.1 9.1 %ffn_grads.1 = (bf16[4,128,3456]{2,1,0:T(8,128)(2,1)S(1)}, bf16[4,128,3456]{2,1,0:T(8,128)(2,1)S(1)}) custom-call(s32[2]{0:T(128)S(1)} %pad_add_fusion.idx_ref, bf16[1024,1024]{1,0:T(8,128)(2,1)S(1)} %get-tuple-element.127.n_ref, bf16[1024,1024]{1,0:T(8,128)(2,1)S(1)} %get-tuple-element.128.d_ref, bf16[1024,1152]{1,0:T(8,128)(2,1)S(1)} %get-tuple-element.129.hid_ref, ...), custom_call_target="tpu_custom_call" | custom-call | flops 1 | bytes 1 | tf_op jit(solution)/shard_map/ffn_grads/pallas_call | solution.py:62
  179.4 6.1 %collective-permute-done.37 = bf16[4,128,3456]{2,1,0:T(8,128)(2,1)S(1)} collective-permute-done((bf16[4,128,3456]{2,1,0:T(8,128)(2,1)S(1)}, bf16[4,128,3456]{2,1,0:T(8,128)(2,1)S(1)}, u32[]{:S(2)}, u32[]{:S(2)}) %collective-permute-start.37) | collective-permute-done | bytes 3538976 | tf_op jit(solution)/shard_map/gf_dp1/ppermute | solution.py:20
  185.5 2.0 fusion.5
  187.6 6.0 %collective-permute-done.38.refs_1_ = bf16[256,1024]{1,0:T(8,128)(2,1)S(1)} collective-permute-done((bf16[256,1024]{1,0:T(8,128)(2,1)S(1)}, bf16[256,1024]{1,0:T(8,128)(2,1)S(1)}, u32[]{:S(2)}, u32[]{:S(2)}) %collective-permute-start.38) | collective-permute-done | bytes 524320 | tf_op jit(solution)/shard_map/dn_z1/ppermute | solution.py:32
  195.5 2.1 collective-permute-start.42
  197.6 17.1 %collective-permute-done.39 = bf16[128,3456]{1,0:T(8,128)(2,1)S(1)} collective-permute-done((bf16[128,3456]{1,0:T(8,128)(2,1)S(1)}, bf16[128,3456]{1,0:T(8,128)(2,1)S(1)}, u32[]{:S(2)}, u32[]{:S(2)}) %collective-permute-start.39) | collective-permute-done | bytes 884768 | tf_op jit(solution)/shard_map/gf_dp2/ppermute | solution.py:20
  215.1 27.0 %collective-permute-done.41.refs_2_ = bf16[256,1024]{1,0:T(8,128)(2,1)S(1)} collective-permute-done((bf16[256,1024]{1,0:T(8,128)(2,1)S(1)}, bf16[256,1024]{1,0:T(8,128)(2,1)S(1)}, u32[]{:S(2)}, u32[]{:S(2)}) %collective-permute-start.41) | collective-permute-done | bytes 524320 | tf_op jit(solution)/shard_map/dn_z2/ppermute | solution.py:32
  242.0 5.5 %mixer_back.1 = (bf16[256,1024]{1,0:T(8,128)(2,1)S(1)}, bf16[256,1024]{1,0:T(8,128)(2,1)S(1)}, bf16[256,1024]{1,0:T(8,128)(2,1)S(1)}, bf16[256,1024]{1,0:T(8,128...) custom-call(bf16[256,1024]{1,0:T(8,128)(2,1)S(1)} %get-tuple-element, ...), custom_call_target="tpu_custom_call" | custom-call | flops 1 | bytes 1 | tf_op jit(solution)/shard_map/mixer_back/pallas_call | solution.py:62
  248.6 2.5 grads_out.1
  251.1 4.1 %collective-permute-done.45 = bf16[4,4,256,256]{3,2,1,0:T(8,128)(2,1)S(1)} collective-permute-done((bf16[4,4,256,256]{3,2,1,0:T(8,128)(2,1)S(1)}, bf16[4,4,256,256]{3,2,1,0:T(8,128)(2,1)S(1)}, u32[]{:S(2)}, u32[]{:S(2)}) %collective-permute-start.45) | collective-permute-done | bytes 2097184 | tf_op jit(solution)/shard_map/gco_dp1/ppermute | solution.py:20
  255.8 1.7 collective-permute-start.48
  259.3 12.2 %collective-permute-done.48 = bf16[4,256,256]{2,1,0:T(8,128)(2,1)S(1)} collective-permute-done((bf16[4,256,256]{2,1,0:T(8,128)(2,1)S(1)}, bf16[4,256,256]{2,1,0:T(8,128)(2,1)S(1)}, u32[]{:S(2)}, u32[]{:S(2)}) %collective-permute-start.48) | collective-permute-done | bytes 524320 | tf_op jit(solution)/shard_map/gco_dp6/ppermute | solution.py:20
  271.6 10.4 %collective-permute-done.47 = bf16[4,256,256]{2,1,0:T(8,128)(2,1)S(1)} collective-permute-done((bf16[4,256,256]{2,1,0:T(8,128)(2,1)S(1)}, bf16[4,256,256]{2,1,0:T(8,128)(2,1)S(1)}, u32[]{:S(2)}, u32[]{:S(2)}) %collective-permute-start.47) | collective-permute-done | bytes 524320 | tf_op jit(solution)/shard_map/gco_dp4/ppermute | solution.py:20
  283.1 5.2 %grads_in.1 = (bf16[4,4,272,256]{3,2,1,0:T(8,128)(2,1)}, bf16[4,4,272,256]{3,2,1,0:T(8,128)(2,1)S(1)}) custom-call(s32[2]{0:T(128)S(1)} %pad_add_fusion.idx_ref, bf16[256,1024]{1,0:T(8,128)(2,1)S(1)} %get-tuple-element.160.n_ref.refs_0_.refs_2_, bf16[256,1024]{1,0:T(8,128)(2,1)S(1)} %get-tuple-element.161.refs_1_, ...), custom_call_target="tpu_custom_call" | custom-call | flops 1 | bytes 1 | tf_op jit(solution)/shard_map/grads_in/pallas_call | solution.py:62
  288.3 1.3 copy-done.2
  290.1 2.1 collective-permute-start.43
  292.2 12.3 %collective-permute-done.44 = bf16[256,1024]{1,0:T(8,128)(2,1)S(1)} collective-permute-done((bf16[256,1024]{1,0:T(8,128)(2,1)S(1)}, bf16[256,1024]{1,0:T(8,128)(2,1)S(1)}, u32[]{:S(2)}, u32[]{:S(2)}) %collective-permute-start.44) | collective-permute-done | bytes 524320 | tf_op jit(solution)/shard_map/out_on_z1/ppermute | solution.py:32
  305.7 2.2 collective-permute-start.58
  307.9 1.9 collective-permute-done.49
  310.6 10.7 %collective-permute-done.43 = bf16[256,1024]{1,0:T(8,128)(2,1)S(1)} collective-permute-done((bf16[256,1024]{1,0:T(8,128)(2,1)S(1)}, bf16[256,1024]{1,0:T(8,128)(2,1)S(1)}, u32[]{:S(2)}, u32[]{:S(2)}) %collective-permute-start.43) | collective-permute-done | bytes 524320 | tf_op jit(solution)/shard_map/out_z1/ppermute | solution.py:32
  321.3 2.5 collective-permute-done.56
  325.8 2.3 fusion.8
  330.4 1.3 collective-permute-start.55
  331.8 18.4 %collective-permute-done.50 = bf16[256,1024]{1,0:T(8,128)(2,1)S(1)} collective-permute-done((bf16[256,1024]{1,0:T(8,128)(2,1)S(1)}, bf16[256,1024]{1,0:T(8,128)(2,1)S(1)}, u32[]{:S(2)}, u32[]{:S(2)}) %collective-permute-start.50) | collective-permute-done | bytes 524320 | tf_op jit(solution)/shard_map/out_z2/ppermute | solution.py:32
  351.4 3.7 collective-permute-done.54
  355.0 1.6 fusion.1
  356.7 2.2 collective-permute-start.60
  359.6 1.6 collective-permute-start.63
  364.6 6.5 %collective-permute-done.62 = bf16[272,256]{1,0:T(8,128)(2,1)S(1)} collective-permute-done((bf16[272,256]{1,0:T(8,128)(2,1)S(1)}, bf16[272,256]{1,0:T(8,128)(2,1)S(1)}, u32[]{:S(2)}, u32[]{:S(2)}) %collective-permute-start.62) | collective-permute-done | bytes 139296 | tf_op jit(solution)/shard_map/gbu_z2/ppermute | solution.py:32
  374.3 10.0 %collective-permute-done.64 = bf16[128,3456]{1,0:T(8,128)(2,1)S(1)} collective-permute-done((bf16[128,3456]{1,0:T(8,128)(2,1)S(1)}, bf16[128,3456]{1,0:T(8,128)(2,1)S(1)}, u32[]{:S(2)}, u32[]{:S(2)}) %collective-permute-start.64) | collective-permute-done | bytes 884768 | tf_op jit(solution)/shard_map/gf_dp6/ppermute | solution.py:20
  384.3 2.1 convert_add_fusion
  387.7 1.9 copy.61
  (225 shorter events, 57.8 us)
Async XLA Ops:
  1.7 19.0 %collective-permute-start.7 = (bf16[256,256]{1,0:T(8,128)(2,1)S(1)}, bf16[256,256]{1,0:T(8,128)(2,1)}, u32[]{:S(2)}, u32[]{:S(2)}) collective-permute-start(bf16[256,256]{1,0:T(8,128)(2,1)S(1)} %bitcast.126), channel_id=1, source_target_pairs={{0,3},{1,2},{2,1},{3,0},{4,7},{5,6},{6,5},{7,4},{8,11},{9,10},{10,... | collective-permute-start | bytes 393224 | tf_op jit(solution)/shard_map/bu_z3/ppermute | solution.py:32
  6.8 13.9 %collective-permute-start.6 = (bf16[256,256]{1,0:T(8,128)(2,1)S(1)}, bf16[256,256]{1,0:T(8,128)(2,1)}, u32[]{:S(2)}, u32[]{:S(2)}) collective-permute-start(bf16[256,256]{1,0:T(8,128)(2,1)S(1)} %bitcast.127), channel_id=1, source_target_pairs={{0,2},{1,3},{2,0},{3,1},{4,6},{5,7},{6,4},{7,5},{8,10},{9,11},{10,... | collective-permute-start | bytes 393224 | tf_op jit(solution)/shard_map/bu_z2/ppermute | solution.py:32
  9.0 26.0 %collective-permute-start.3 = (bf16[128,3456]{1,0:T(8,128)(2,1)S(1)}, bf16[128,3456]{1,0:T(8,128)(2,1)S(1)}, u32[]{:S(2)}, u32[]{:S(2)}) collective-permute-start(bf16[128,3456]{1,0:T(8,128)(2,1)S(1)} %pad_maximum_fusion.1.refs_0_), channel_id=1, source_target_pairs={{0,16},{4,20},{8,24},{12,28},{16,0},{20,4},{24,8},{28,12},{1,17},{... | collective-permute-start | bytes 2654216 | tf_op jit(solution)/shard_map/ffn_dp4/ppermute | solution.py:20
  10.6 24.4 %collective-permute-start.2 = (bf16[128,3456]{1,0:T(8,128)(2,1)S(1)}, bf16[128,3456]{1,0:T(8,128)(2,1)S(1)}, u32[]{:S(2)}, u32[]{:S(2)}) collective-permute-start(bf16[128,3456]{1,0:T(8,128)(2,1)S(1)} %pad_maximum_fusion.1.refs_0_), channel_id=1, source_target_pairs={{0,8},{4,12},{8,0},{12,4},{16,24},{20,28},{24,16},{28,20},{1,9},{5... | collective-permute-start | bytes 2654216 | tf_op jit(solution)/shard_map/ffn_dp2/ppermute | solution.py:20
  12.2 5.9 %collective-permute-start = (bf16[8,2048]{1,0:T(8,128)(2,1)S(1)}, bf16[8,2048]{1,0:T(8,128)(2,1)S(1)}, u32[]{:S(2)}, u32[]{:S(2)}) collective-permute-start(bf16[8,2048]{1,0:T(8,128)(2,1)S(1)} %bitcast.141), channel_id=1, source_target_pairs={{0,1},{1,2},{2,3},{3,0},{4,5},{5,6},{6,7},{7,4},{8,9},{9,10},{10,1... | collective-permute-start | bytes 98312 | tf_op jit(solution)/shard_map/tail_z/ppermute | solution.py:26
  18.0 1.6 collective-permute-start.1
  19.7 5.9 %collective-permute-start.5 = (bf16[256,256]{1,0:T(8,128)(2,1)S(1)}, bf16[256,256]{1,0:T(8,128)(2,1)S(1)}, u32[]{:S(2)}, u32[]{:S(2)}) collective-permute-start(bf16[256,256]{1,0:T(8,128)(2,1)S(1)} %bitcast.129), channel_id=1, source_target_pairs={{0,1},{1,0},{2,3},{3,2},{4,5},{5,4},{6,7},{7,6},{8,9},{9,8},{10,11... | collective-permute-start | bytes 393224 | tf_op jit(solution)/shard_map/bu_z1/ppermute | solution.py:32
  25.6 12.7 %collective-permute-start.13 = (bf16[256,256]{1,0:T(8,128)(2,1)}, bf16[256,256]{1,0:T(8,128)(2,1)S(1)}, u32[]{:S(2)}, u32[]{:S(2)}) collective-permute-start(bf16[256,256]{1,0:T(8,128)(2,1)} %bitcast.131), channel_id=1, source_target_pairs={{0,3},{1,2},{2,1},{3,0},{4,7},{5,6},{6,5},{7,4},{8,11},{9,10},{10,... | collective-permute-start | bytes 393224 | tf_op jit(solution)/shard_map/co_z3/ppermute | solution.py:32
  27.4 12.2 %collective-permute-start.12 = (bf16[256,256]{1,0:T(8,128)(2,1)}, bf16[256,256]{1,0:T(8,128)(2,1)S(1)}, u32[]{:S(2)}, u32[]{:S(2)}) collective-permute-start(bf16[256,256]{1,0:T(8,128)(2,1)} %bitcast.132), channel_id=1, source_target_pairs={{0,2},{1,3},{2,0},{3,1},{4,6},{5,7},{6,4},{7,5},{8,10},{9,11},{10,... | collective-permute-start | bytes 393224 | tf_op jit(solution)/shard_map/co_z2/ppermute | solution.py:32
  27.7 11.9 %collective-permute-start.11 = (bf16[256,256]{1,0:T(8,128)(2,1)}, bf16[256,256]{1,0:T(8,128)(2,1)S(1)}, u32[]{:S(2)}, u32[]{:S(2)}) collective-permute-start(bf16[256,256]{1,0:T(8,128)(2,1)} %bitcast.133), channel_id=1, source_target_pairs={{0,1},{1,0},{2,3},{3,2},{4,5},{5,4},{6,7},{7,6},{8,9},{9,8},{10,11... | collective-permute-start | bytes 393224 | tf_op jit(solution)/shard_map/co_z1/ppermute | solution.py:32
  35.1 30.6 %collective-permute-start.10 = (bf16[1040,256]{1,0:T(8,128)(2,1)}, bf16[1040,256]{1,0:T(8,128)(2,1)}, u32[]{:S(2)}, u32[]{:S(2)}) collective-permute-start(bf16[1040,256]{1,0:T(8,128)(2,1)} %constant_dynamic-update-slice_fusion.refs_0_), channel_id=1, source_target_pairs={{0,24},{4,28},{8,16},{12,20},{16,8},{20,12},{24,0},{28,4},{1,25},{... | collective-permute-start | bytes 1597448 | tf_op jit(solution)/shard_map/bu_dp6/ppermute | solution.py:20
  36.0 30.1 %collective-permute-start.9 = (bf16[1040,256]{1,0:T(8,128)(2,1)}, bf16[1040,256]{1,0:T(8,128)(2,1)}, u32[]{:S(2)}, u32[]{:S(2)}) collective-permute-start(bf16[1040,256]{1,0:T(8,128)(2,1)} %constant_dynamic-update-slice_fusion.refs_0_), channel_id=1, source_target_pairs={{0,16},{4,20},{8,24},{12,28},{16,0},{20,4},{24,8},{28,12},{1,17},{... | collective-permute-start | bytes 1597448 | tf_op jit(solution)/shard_map/bu_dp4/ppermute | solution.py:20
  39.6 25.2 %collective-permute-start.15 = (bf16[256,1024]{1,0:T(8,128)(2,1)S(1)}, bf16[256,1024]{1,0:T(8,128)(2,1)S(1)}, u32[]{:S(2)}, u32[]{:S(2)}) collective-permute-start(bf16[256,1024]{1,0:T(8,128)(2,1)S(1)} %bitcast.120), channel_id=1, source_target_pairs={{0,2},{1,3},{2,0},{3,1},{4,6},{5,7},{6,4},{7,5},{8,10},{9,11},{10,... | collective-permute-start | bytes 1572872 | tf_op jit(solution)/shard_map/dy_z2/ppermute | solution.py:32
  40.6 25.6 %collective-permute-start.8 = (bf16[1040,256]{1,0:T(8,128)(2,1)}, bf16[1040,256]{1,0:T(8,128)(2,1)}, u32[]{:S(2)}, u32[]{:S(2)}) collective-permute-start(bf16[1040,256]{1,0:T(8,128)(2,1)} %constant_dynamic-update-slice_fusion.refs_0_), channel_id=1, source_target_pairs={{0,8},{4,12},{8,0},{12,4},{16,24},{20,28},{24,16},{28,20},{1,9},{5... | collective-permute-start | bytes 1597448 | tf_op jit(solution)/shard_map/bu_dp2/ppermute | solution.py:20
  41.5 19.4 %collective-permute-start.4 = (bf16[2,1,8,2048]{3,2,1,0:T(8,128)(2,1)S(1)}, bf16[2,1,8,2048]{3,2,1,0:T(8,128)(2,1)S(1)}, u32[]{:S(2)}, u32[]{:S(2)}) collective-permute-start(bf16[2,1,8,2048]{3,2,1,0:T(8,128)(2,1)S(1)} %pad_maximum_fusion.7), channel_id=1, source_target_pairs={{0,8},{4,12},{8,0},{12,4},{16,24},{20,28},{24,16},{28,20},{1,9},{5... | collective-permute-start | bytes 196616 | tf_op jit(solution)/shard_map/tail_dp2/ppermute | solution.py:20
  60.9 15.0 %collective-permute-start.14 = (bf16[256,1024]{1,0:T(8,128)(2,1)S(1)}, bf16[256,1024]{1,0:T(8,128)(2,1)S(1)}, u32[]{:S(2)}, u32[]{:S(2)}) collective-permute-start(bf16[256,1024]{1,0:T(8,128)(2,1)S(1)} %bitcast.121), channel_id=1, source_target_pairs={{0,1},{1,0},{2,3},{3,2},{4,5},{5,4},{6,7},{7,6},{8,9},{9,8},{10,11... | collective-permute-start | bytes 1572872 | tf_op jit(solution)/shard_map/dy_z1/ppermute | solution.py:32
  65.6 13.9 %collective-permute-start.17 = (bf16[1040,256]{1,0:T(8,128)(2,1)}, bf16[1040,256]{1,0:T(8,128)(2,1)}, u32[]{:S(2)}, u32[]{:S(2)}) collective-permute-start(bf16[1040,256]{1,0:T(8,128)(2,1)} %constant_dynamic-update-slice_fusion.refs_0_), channel_id=1, source_target_pairs={{0,4},{4,0},{8,12},{12,8},{16,20},{20,16},{24,28},{28,24},{1,5},{5... | collective-permute-start | bytes 1597448 | tf_op jit(solution)/shard_map/bu_dp1/ppermute | solution.py:20
  65.6 29.3 %collective-permute-start.20 = (bf16[1040,256]{1,0:T(8,128)(2,1)}, bf16[1040,256]{1,0:T(8,128)(2,1)}, u32[]{:S(2)}, u32[]{:S(2)}) collective-permute-start(bf16[1040,256]{1,0:T(8,128)(2,1)} %collective-permute-done.10.refs_6_), channel_id=1, source_target_pairs={{0,4},{4,0},{8,12},{12,8},{16,20},{20,16},{24,28},{28,24},{1,5},{5... | collective-permute-start | bytes 1597448 | tf_op jit(solution)/shard_map/bu_dp1/ppermute | solution.py:20
  66.1 30.2 %collective-permute-start.19 = (bf16[1040,256]{1,0:T(8,128)(2,1)}, bf16[1040,256]{1,0:T(8,128)(2,1)}, u32[]{:S(2)}, u32[]{:S(2)}) collective-permute-start(bf16[1040,256]{1,0:T(8,128)(2,1)} %collective-permute-done.9.refs_4_), channel_id=1, source_target_pairs={{0,4},{4,0},{8,12},{12,8},{16,20},{20,16},{24,28},{28,24},{1,5},{5... | collective-permute-start | bytes 1597448 | tf_op jit(solution)/shard_map/bu_dp1/ppermute | solution.py:20
  66.2 31.5 %collective-permute-start.18 = (bf16[1040,256]{1,0:T(8,128)(2,1)}, bf16[1040,256]{1,0:T(8,128)(2,1)}, u32[]{:S(2)}, u32[]{:S(2)}) collective-permute-start(bf16[1040,256]{1,0:T(8,128)(2,1)} %collective-permute-done.8.refs_2_), channel_id=1, source_target_pairs={{0,4},{4,0},{8,12},{12,8},{16,20},{20,16},{24,28},{28,24},{1,5},{5... | collective-permute-start | bytes 1597448 | tf_op jit(solution)/shard_map/bu_dp1/ppermute | solution.py:20
  76.8 15.1 %collective-permute-start.16 = (bf16[4,1,8,2048]{3,2,1,0:T(8,128)(2,1)S(1)}, bf16[4,1,8,2048]{3,2,1,0:T(8,128)(2,1)}, u32[]{:S(2)}, u32[]{:S(2)}) collective-permute-start(bf16[4,1,8,2048]{3,2,1,0:T(8,128)(2,1)S(1)} %pad_maximum_fusion.4), channel_id=1, source_target_pairs={{0,16},{4,20},{8,24},{12,28},{16,0},{20,4},{24,8},{28,12},{1,17},{... | collective-permute-start | bytes 393224 | tf_op jit(solution)/shard_map/tail_dp4/ppermute | solution.py:20
  79.6 26.1 %collective-permute-start.26 = (bf16[1024,256]{1,0:T(8,128)(2,1)S(1)}, bf16[1024,256]{1,0:T(8,128)(2,1)}, u32[]{:S(2)}, u32[]{:S(2)}) collective-permute-start(bf16[1024,256]{1,0:T(8,128)(2,1)S(1)} %pad_maximum_fusion.2.refs_0_), channel_id=1, source_target_pairs={{0,24},{4,28},{8,16},{12,20},{16,8},{20,12},{24,0},{28,4},{1,25},{... | collective-permute-start | bytes 1572872 | tf_op jit(solution)/shard_map/co_dp6/ppermute | solution.py:20
  91.9 13.8 %collective-permute-start.24 = (bf16[1024,256]{1,0:T(8,128)(2,1)S(1)}, bf16[1024,256]{1,0:T(8,128)(2,1)}, u32[]{:S(2)}, u32[]{:S(2)}) collective-permute-start(bf16[1024,256]{1,0:T(8,128)(2,1)S(1)} %pad_maximum_fusion.2.refs_0_), channel_id=1, source_target_pairs={{0,16},{4,20},{8,24},{12,28},{16,0},{20,4},{24,8},{28,12},{1,17},{... | collective-permute-start | bytes 1572872 | tf_op jit(solution)/shard_map/co_dp4/ppermute | solution.py:20
  95.0 10.7 %collective-permute-start.22 = (bf16[1024,256]{1,0:T(8,128)(2,1)S(1)}, bf16[1024,256]{1,0:T(8,128)(2,1)}, u32[]{:S(2)}, u32[]{:S(2)}) collective-permute-start(bf16[1024,256]{1,0:T(8,128)(2,1)S(1)} %pad_maximum_fusion.2.refs_0_), channel_id=1, source_target_pairs={{0,8},{4,12},{8,0},{12,4},{16,24},{20,28},{24,16},{28,20},{1,9},{5... | collective-permute-start | bytes 1572872 | tf_op jit(solution)/shard_map/co_dp2/ppermute | solution.py:20
  96.3 9.5 %collective-permute-start.28 = (bf16[256,1024]{1,0:T(8,128)(2,1)}, bf16[256,1024]{1,0:T(8,128)(2,1)}, u32[]{:S(2)}, u32[]{:S(2)}) collective-permute-start(bf16[256,1024]{1,0:T(8,128)(2,1)} %copy-done.10), channel_id=1, source_target_pairs={{0,1},{1,0},{2,3},{3,2},{4,5},{5,4},{6,7},{7,6},{8,9},{9,8},{10,11... | collective-permute-start | bytes 1572872 | tf_op jit(solution)/shard_map/dy_on_z1/ppermute | solution.py:32
  97.7 10.1 %collective-permute-start.21 = (bf16[1024,256]{1,0:T(8,128)(2,1)S(1)}, bf16[1024,256]{1,0:T(8,128)(2,1)}, u32[]{:S(2)}, u32[]{:S(2)}) collective-permute-start(bf16[1024,256]{1,0:T(8,128)(2,1)S(1)} %pad_maximum_fusion.2.refs_0_), channel_id=1, source_target_pairs={{0,4},{4,0},{8,12},{12,8},{16,20},{20,16},{24,28},{28,24},{1,5},{5... | collective-permute-start | bytes 1572872 | tf_op jit(solution)/shard_map/co_dp1/ppermute | solution.py:20
  105.8 22.9 %collective-permute-start.32 = (bf16[128,3456]{1,0:T(8,128)(2,1)S(1)}, bf16[128,3456]{1,0:T(8,128)(2,1)S(1)}, u32[]{:S(2)}, u32[]{:S(2)}) collective-permute-start(bf16[128,3456]{1,0:T(8,128)(2,1)S(1)} %pad_maximum_fusion.1.refs_0_), channel_id=1, source_target_pairs={{0,24},{4,28},{8,16},{12,20},{16,8},{20,12},{24,0},{28,4},{1,25},{... | collective-permute-start | bytes 2654216 | tf_op jit(solution)/shard_map/ffn_dp6/ppermute | solution.py:20
  107.3 2.1 collective-permute-start.27
  107.3 2.9 collective-permute-start.25
  107.8 3.1 collective-permute-start.23
  107.8 20.9 %collective-permute-start.29 = (bf16[128,3456]{1,0:T(8,128)(2,1)S(1)}, bf16[128,3456]{1,0:T(8,128)(2,1)S(1)}, u32[]{:S(2)}, u32[]{:S(2)}) collective-permute-start(bf16[128,3456]{1,0:T(8,128)(2,1)S(1)} %pad_maximum_fusion.1.refs_0_), channel_id=1, source_target_pairs={{0,4},{4,0},{8,12},{12,8},{16,20},{20,16},{24,28},{28,24},{1,5},{5... | collective-permute-start | bytes 2654216 | tf_op jit(solution)/shard_map/ffn_dp1/ppermute | solution.py:20
  115.2 26.3 %collective-permute-start.35 = (bf16[256,1024]{1,0:T(8,128)(2,1)S(1)}, bf16[256,1024]{1,0:T(8,128)(2,1)S(1)}, u32[]{:S(2)}, u32[]{:S(2)}) collective-permute-start(bf16[256,1024]{1,0:T(8,128)(2,1)S(1)} %get-tuple-element.107.n_ref), channel_id=1, source_target_pairs={{0,2},{1,3},{2,0},{3,1},{4,6},{5,7},{6,4},{7,5},{8,10},{9,11},{10,... | collective-permute-start | bytes 1572872 | tf_op jit(solution)/shard_map/n2_z2/ppermute | solution.py:32
  117.2 24.3 %collective-permute-start.30 = (bf16[128,3456]{1,0:T(8,128)(2,1)S(1)}, bf16[128,3456]{1,0:T(8,128)(2,1)S(1)}, u32[]{:S(2)}, u32[]{:S(2)}) collective-permute-start(bf16[128,3456]{1,0:T(8,128)(2,1)S(1)} %copy-done.8), channel_id=1, source_target_pairs={{0,4},{4,0},{8,12},{12,8},{16,20},{20,16},{24,28},{28,24},{1,5},{5... | collective-permute-start | bytes 2654216 | tf_op jit(solution)/shard_map/ffn_dp1/ppermute | solution.py:20
  117.3 24.2 %collective-permute-start.31 = (bf16[128,3456]{1,0:T(8,128)(2,1)S(1)}, bf16[128,3456]{1,0:T(8,128)(2,1)S(1)}, u32[]{:S(2)}, u32[]{:S(2)}) collective-permute-start(bf16[128,3456]{1,0:T(8,128)(2,1)S(1)} %copy-done.6), channel_id=1, source_target_pairs={{0,4},{4,0},{8,12},{12,8},{16,20},{20,16},{24,28},{28,24},{1,5},{5... | collective-permute-start | bytes 2654216 | tf_op jit(solution)/shard_map/ffn_dp1/ppermute | solution.py:20
  128.7 12.8 %collective-permute-start.33 = (bf16[128,3456]{1,0:T(8,128)(2,1)S(1)}, bf16[128,3456]{1,0:T(8,128)(2,1)S(1)}, u32[]{:S(2)}, u32[]{:S(2)}) collective-permute-start(bf16[128,3456]{1,0:T(8,128)(2,1)S(1)} %collective-permute-done.32.refs_6_), channel_id=1, source_target_pairs={{0,4},{4,0},{8,12},{12,8},{16,20},{20,16},{24,28},{28,24},{1,5},{5... | collective-permute-start | bytes 2654216 | tf_op jit(solution)/shard_map/ffn_dp1/ppermute | solution.py:20
  128.7 23.9 %collective-permute-start.34 = (bf16[256,1024]{1,0:T(8,128)(2,1)S(1)}, bf16[256,1024]{1,0:T(8,128)(2,1)S(1)}, u32[]{:S(2)}, u32[]{:S(2)}) collective-permute-start(bf16[256,1024]{1,0:T(8,128)(2,1)S(1)} %get-tuple-element.107.n_ref), channel_id=1, source_target_pairs={{0,1},{1,0},{2,3},{3,2},{4,5},{5,4},{6,7},{7,6},{8,9},{9,8},{10,11... | collective-permute-start | bytes 1572872 | tf_op jit(solution)/shard_map/n2_z1/ppermute | solution.py:32
  141.4 22.4 %collective-permute-start.36 = (bf16[256,1024]{1,0:T(8,128)(2,1)S(1)}, bf16[256,1024]{1,0:T(8,128)(2,1)S(1)}, u32[]{:S(2)}, u32[]{:S(2)}) collective-permute-start(bf16[256,1024]{1,0:T(8,128)(2,1)S(1)} %collective-permute-done.35.n_ref), channel_id=1, source_target_pairs={{0,1},{1,0},{2,3},{3,2},{4,5},{5,4},{6,7},{7,6},{8,9},{9,8},{10,11... | collective-permute-start | bytes 1572872 | tf_op jit(solution)/shard_map/n2_on_z1/ppermute | solution.py:32
  179.2 6.3 %collective-permute-start.37 = (bf16[4,128,3456]{2,1,0:T(8,128)(2,1)S(1)}, bf16[4,128,3456]{2,1,0:T(8,128)(2,1)S(1)}, u32[]{:S(2)}, u32[]{:S(2)}) collective-permute-start(bf16[4,128,3456]{2,1,0:T(8,128)(2,1)S(1)} %get-tuple-element.132), channel_id=1, source_target_pairs={{0,4},{4,0},{8,12},{12,8},{16,20},{20,16},{24,28},{28,24},{1,5},{5... | collective-permute-start | bytes 10616840 | tf_op jit(solution)/shard_map/gf_dp1/ppermute | solution.py:20
  179.3 14.3 %collective-permute-start.38 = (bf16[256,1024]{1,0:T(8,128)(2,1)S(1)}, bf16[256,1024]{1,0:T(8,128)(2,1)S(1)}, u32[]{:S(2)}, u32[]{:S(2)}) collective-permute-start(bf16[256,1024]{1,0:T(8,128)(2,1)S(1)} %get-tuple-element.133), channel_id=1, source_target_pairs={{0,1},{1,0},{2,3},{3,2},{4,5},{5,4},{6,7},{7,6},{8,9},{9,8},{10,11... | collective-permute-start | bytes 1572872 | tf_op jit(solution)/shard_map/dn_z1/ppermute | solution.py:32
  193.6 21.1 %collective-permute-start.39 = (bf16[128,3456]{1,0:T(8,128)(2,1)S(1)}, bf16[128,3456]{1,0:T(8,128)(2,1)S(1)}, u32[]{:S(2)}, u32[]{:S(2)}) collective-permute-start(bf16[128,3456]{1,0:T(8,128)(2,1)S(1)} %get-tuple-element.134), channel_id=1, source_target_pairs={{0,8},{4,12},{8,0},{12,4},{16,24},{20,28},{24,16},{28,20},{1,9},{5... | collective-permute-start | bytes 2654216 | tf_op jit(solution)/shard_map/gf_dp2/ppermute | solution.py:20
  194.2 20.8 %collective-permute-start.40 = (bf16[128,3456]{1,0:T(8,128)(2,1)S(1)}, bf16[128,3456]{1,0:T(8,128)(2,1)S(1)}, u32[]{:S(2)}, u32[]{:S(2)}) collective-permute-start(bf16[128,3456]{1,0:T(8,128)(2,1)S(1)} %get-tuple-element.135), channel_id=1, source_target_pairs={{0,16},{4,20},{8,24},{12,28},{16,0},{20,4},{24,8},{28,12},{1,17},{... | collective-permute-start | bytes 2654216 | tf_op jit(solution)/shard_map/gf_dp4/ppermute | solution.py:20
  195.5 19.6 %collective-permute-start.42 = (bf16[256,1024]{1,0:T(8,128)(2,1)S(1)}, bf16[256,1024]{1,0:T(8,128)(2,1)S(1)}, u32[]{:S(2)}, u32[]{:S(2)}) collective-permute-start(bf16[256,1024]{1,0:T(8,128)(2,1)S(1)} %get-tuple-element.138), channel_id=1, source_target_pairs={{0,3},{1,2},{2,1},{3,0},{4,7},{5,6},{6,5},{7,4},{8,11},{9,10},{10,... | collective-permute-start | bytes 1572872 | tf_op jit(solution)/shard_map/dn_z3/ppermute | solution.py:32
  197.6 44.5 %collective-permute-start.41 = (bf16[256,1024]{1,0:T(8,128)(2,1)S(1)}, bf16[256,1024]{1,0:T(8,128)(2,1)S(1)}, u32[]{:S(2)}, u32[]{:S(2)}) collective-permute-start(bf16[256,1024]{1,0:T(8,128)(2,1)S(1)} %get-tuple-element.137), channel_id=1, source_target_pairs={{0,2},{1,3},{2,0},{3,1},{4,6},{5,7},{6,4},{7,5},{8,10},{9,11},{10,... | collective-permute-start | bytes 1572872 | tf_op jit(solution)/shard_map/dn_z2/ppermute | solution.py:32
  251.0 4.2 %collective-permute-start.45 = (bf16[4,4,256,256]{3,2,1,0:T(8,128)(2,1)S(1)}, bf16[4,4,256,256]{3,2,1,0:T(8,128)(2,1)S(1)}, u32[]{:S(2)}, u32[]{:S(2)}) collective-permute-start(bf16[4,4,256,256]{3,2,1,0:T(8,128)(2,1)S(1)} %get-tuple-element.154), channel_id=1, source_target_pairs={{0,4},{4,0},{8,12},{12,8},{16,20},{20,16},{24,28},{28,24},{1,5},{5... | collective-permute-start | bytes 6291464 | tf_op jit(solution)/shard_map/gco_dp1/ppermute | solution.py:20
  255.8 15.8 %collective-permute-start.48 = (bf16[4,256,256]{2,1,0:T(8,128)(2,1)S(1)}, bf16[4,256,256]{2,1,0:T(8,128)(2,1)S(1)}, u32[]{:S(2)}, u32[]{:S(2)}) collective-permute-start(bf16[4,256,256]{2,1,0:T(8,128)(2,1)S(1)} %get-tuple-element.216), channel_id=1, source_target_pairs={{0,24},{4,28},{8,16},{12,20},{16,8},{20,12},{24,0},{28,4},{1,25},{... | collective-permute-start | bytes 1572872 | tf_op jit(solution)/shard_map/gco_dp6/ppermute | solution.py:20
  257.4 24.5 %collective-permute-start.47 = (bf16[4,256,256]{2,1,0:T(8,128)(2,1)S(1)}, bf16[4,256,256]{2,1,0:T(8,128)(2,1)S(1)}, u32[]{:S(2)}, u32[]{:S(2)}) collective-permute-start(bf16[4,256,256]{2,1,0:T(8,128)(2,1)S(1)} %get-tuple-element.217), channel_id=1, source_target_pairs={{0,16},{4,20},{8,24},{12,28},{16,0},{20,4},{24,8},{28,12},{1,17},{... | collective-permute-start | bytes 1572872 | tf_op jit(solution)/shard_map/gco_dp4/ppermute | solution.py:20
  258.3 23.7 %collective-permute-start.46 = (bf16[4,256,256]{2,1,0:T(8,128)(2,1)S(1)}, bf16[4,256,256]{2,1,0:T(8,128)(2,1)S(1)}, u32[]{:S(2)}, u32[]{:S(2)}) collective-permute-start(bf16[4,256,256]{2,1,0:T(8,128)(2,1)S(1)} %get-tuple-element.218), channel_id=1, source_target_pairs={{0,8},{4,12},{8,0},{12,4},{16,24},{20,28},{24,16},{28,20},{1,9},{5... | collective-permute-start | bytes 1572872 | tf_op jit(solution)/shard_map/gco_dp2/ppermute | solution.py:20
  289.6 36.2 %collective-permute-start.52 = (bf16[4,4,272,256]{3,2,1,0:T(8,128)(2,1)}, bf16[4,4,272,256]{3,2,1,0:T(8,128)(2,1)}, u32[]{:S(2)}, u32[]{:S(2)}) collective-permute-start(bf16[4,4,272,256]{3,2,1,0:T(8,128)(2,1)} %get-tuple-element.168), channel_id=1, source_target_pairs={{0,4},{4,0},{8,12},{12,8},{16,20},{20,16},{24,28},{28,24},{1,5},{5... | collective-permute-start | bytes 6684680 | tf_op jit(solution)/shard_map/gbu_dp1/ppermute | solution.py:20
  289.7 14.9 %collective-permute-start.44 = (bf16[256,1024]{1,0:T(8,128)(2,1)S(1)}, bf16[256,1024]{1,0:T(8,128)(2,1)S(1)}, u32[]{:S(2)}, u32[]{:S(2)}) collective-permute-start(bf16[256,1024]{1,0:T(8,128)(2,1)S(1)} %copy-done.17), channel_id=1, source_target_pairs={{0,1},{1,0},{2,3},{3,2},{4,5},{5,4},{6,7},{7,6},{8,9},{9,8},{10,11... | collective-permute-start | bytes 1572872 | tf_op jit(solution)/shard_map/out_on_z1/ppermute | solution.py:32
  290.1 31.2 %collective-permute-start.43 = (bf16[256,1024]{1,0:T(8,128)(2,1)S(1)}, bf16[256,1024]{1,0:T(8,128)(2,1)S(1)}, u32[]{:S(2)}, u32[]{:S(2)}) collective-permute-start(bf16[256,1024]{1,0:T(8,128)(2,1)S(1)} %copy-done.15), channel_id=1, source_target_pairs={{0,1},{1,0},{2,3},{3,2},{4,5},{5,4},{6,7},{7,6},{8,9},{9,8},{10,11... | collective-permute-start | bytes 1572872 | tf_op jit(solution)/shard_map/out_z1/ppermute | solution.py:32
  304.8 5.0 %collective-permute-start.49 = (bf16[4,8,2048]{2,1,0:T(8,128)(2,1)S(1)}, bf16[4,8,2048]{2,1,0:T(8,128)(2,1)S(1)}, u32[]{:S(2)}, u32[]{:S(2)}) collective-permute-start(bf16[4,8,2048]{2,1,0:T(8,128)(2,1)S(1)} %slice_bitcast_fusion.15), channel_id=1, source_target_pairs={{0,16},{4,20},{8,24},{12,28},{16,0},{20,4},{24,8},{28,12},{1,17},{... | collective-permute-start | bytes 393224 | tf_op jit(solution)/shard_map/back_dp4/ppermute | solution.py:20
  305.6 18.1 %collective-permute-start.56 = (bf16[256,256]{1,0:T(8,128)(2,1)S(1)}, bf16[256,256]{1,0:T(8,128)(2,1)S(1)}, u32[]{:S(2)}, u32[]{:S(2)}) collective-permute-start(bf16[256,256]{1,0:T(8,128)(2,1)S(1)} %get-tuple-element.227), channel_id=1, source_target_pairs={{0,1},{1,0},{2,3},{3,2},{4,5},{5,4},{6,7},{7,6},{8,9},{9,8},{10,11... | collective-permute-start | bytes 393224 | tf_op jit(solution)/shard_map/gco_z1/ppermute | solution.py:32
  305.7 18.0 %collective-permute-start.58 = (bf16[256,256]{1,0:T(8,128)(2,1)S(1)}, bf16[256,256]{1,0:T(8,128)(2,1)S(1)}, u32[]{:S(2)}, u32[]{:S(2)}) collective-permute-start(bf16[256,256]{1,0:T(8,128)(2,1)S(1)} %get-tuple-element.228), channel_id=1, source_target_pairs={{0,3},{1,2},{2,1},{3,0},{4,7},{5,6},{6,5},{7,4},{8,11},{9,10},{10,... | collective-permute-start | bytes 393224 | tf_op jit(solution)/shard_map/gco_z3/ppermute | solution.py:32
  309.8 14.0 %collective-permute-start.57 = (bf16[256,256]{1,0:T(8,128)(2,1)S(1)}, bf16[256,256]{1,0:T(8,128)(2,1)S(1)}, u32[]{:S(2)}, u32[]{:S(2)}) collective-permute-start(bf16[256,256]{1,0:T(8,128)(2,1)S(1)} %get-tuple-element.229), channel_id=1, source_target_pairs={{0,2},{1,3},{2,0},{3,1},{4,6},{5,7},{6,4},{7,5},{8,10},{9,11},{10,... | collective-permute-start | bytes 393224 | tf_op jit(solution)/shard_map/gco_z2/ppermute | solution.py:32
  321.3 10.4 %collective-permute-start.51 = (bf16[2,8,2048]{2,1,0:T(8,128)(2,1)S(1)}, bf16[2,8,2048]{2,1,0:T(8,128)(2,1)S(1)}, u32[]{:S(2)}, u32[]{:S(2)}) collective-permute-start(bf16[2,8,2048]{2,1,0:T(8,128)(2,1)S(1)} %slice.211), channel_id=1, source_target_pairs={{0,8},{4,12},{8,0},{12,4},{16,24},{20,28},{24,16},{28,20},{1,9},{5... | collective-permute-start | bytes 196616 | tf_op jit(solution)/shard_map/back_dp2/ppermute | solution.py:20
  324.6 25.6 %collective-permute-start.50 = (bf16[256,1024]{1,0:T(8,128)(2,1)S(1)}, bf16[256,1024]{1,0:T(8,128)(2,1)S(1)}, u32[]{:S(2)}, u32[]{:S(2)}) collective-permute-start(bf16[256,1024]{1,0:T(8,128)(2,1)S(1)} %add_convert_fusion.15), channel_id=1, source_target_pairs={{0,2},{1,3},{2,0},{3,1},{4,6},{5,7},{6,4},{7,5},{8,10},{9,11},{10,... | collective-permute-start | bytes 1572872 | tf_op jit(solution)/shard_map/out_z2/ppermute | solution.py:32
  328.2 23.2 %collective-permute-start.53 = (bf16[4,272,256]{2,1,0:T(8,128)(2,1)S(1)}, bf16[4,272,256]{2,1,0:T(8,128)(2,1)S(1)}, u32[]{:S(2)}, u32[]{:S(2)}) collective-permute-start(bf16[4,272,256]{2,1,0:T(8,128)(2,1)S(1)} %get-tuple-element.169), channel_id=1, source_target_pairs={{0,8},{4,12},{8,0},{12,4},{16,24},{20,28},{24,16},{28,20},{1,9},{5... | collective-permute-start | bytes 1671176 | tf_op jit(solution)/shard_map/gbu_dp2/ppermute | solution.py:20
  329.2 25.8 %collective-permute-start.54 = (bf16[4,272,256]{2,1,0:T(8,128)(2,1)S(1)}, bf16[4,272,256]{2,1,0:T(8,128)(2,1)S(1)}, u32[]{:S(2)}, u32[]{:S(2)}) collective-permute-start(bf16[4,272,256]{2,1,0:T(8,128)(2,1)S(1)} %get-tuple-element.170), channel_id=1, source_target_pairs={{0,16},{4,20},{8,24},{12,28},{16,0},{20,4},{24,8},{28,12},{1,17},{... | collective-permute-start | bytes 1671176 | tf_op jit(solution)/shard_map/gbu_dp4/ppermute | solution.py:20
  330.4 24.6 %collective-permute-start.55 = (bf16[4,272,256]{2,1,0:T(8,128)(2,1)S(1)}, bf16[4,272,256]{2,1,0:T(8,128)(2,1)S(1)}, u32[]{:S(2)}, u32[]{:S(2)}) collective-permute-start(bf16[4,272,256]{2,1,0:T(8,128)(2,1)S(1)} %get-tuple-element.171), channel_id=1, source_target_pairs={{0,24},{4,28},{8,16},{12,20},{16,8},{20,12},{24,0},{28,4},{1,25},{... | collective-permute-start | bytes 1671176 | tf_op jit(solution)/shard_map/gbu_dp6/ppermute | solution.py:20
  356.7 7.0 %collective-permute-start.60 = (bf16[8,2048]{1,0:T(8,128)(2,1)S(1)}, bf16[8,2048]{1,0:T(8,128)(2,1)S(1)}, u32[]{:S(2)}, u32[]{:S(2)}) collective-permute-start(bf16[8,2048]{1,0:T(8,128)(2,1)S(1)} %fusion.26), channel_id=1, source_target_pairs={{0,3},{1,0},{2,1},{3,2},{4,7},{5,4},{6,5},{7,6},{8,11},{9,8},{10,9... | collective-permute-start | bytes 98312 | tf_op jit(solution)/shard_map/back_z/ppermute | solution.py:26
  358.9 12.1 %collective-permute-start.62 = (bf16[272,256]{1,0:T(8,128)(2,1)S(1)}, bf16[272,256]{1,0:T(8,128)(2,1)S(1)}, u32[]{:S(2)}, u32[]{:S(2)}) collective-permute-start(bf16[272,256]{1,0:T(8,128)(2,1)S(1)} %get-tuple-element.174), channel_id=1, source_target_pairs={{0,2},{1,3},{2,0},{3,1},{4,6},{5,7},{6,4},{7,5},{8,10},{9,11},{10,... | collective-permute-start | bytes 417800 | tf_op jit(solution)/shard_map/gbu_z2/ppermute | solution.py:32
  359.6 11.5 %collective-permute-start.63 = (bf16[272,256]{1,0:T(8,128)(2,1)S(1)}, bf16[272,256]{1,0:T(8,128)(2,1)S(1)}, u32[]{:S(2)}, u32[]{:S(2)}) collective-permute-start(bf16[272,256]{1,0:T(8,128)(2,1)S(1)} %get-tuple-element.175), channel_id=1, source_target_pairs={{0,3},{1,2},{2,1},{3,0},{4,7},{5,6},{6,5},{7,4},{8,11},{9,10},{10,... | collective-permute-start | bytes 417800 | tf_op jit(solution)/shard_map/gbu_z3/ppermute | solution.py:32
  361.2 11.1 %collective-permute-start.61 = (bf16[272,256]{1,0:T(8,128)(2,1)S(1)}, bf16[272,256]{1,0:T(8,128)(2,1)S(1)}, u32[]{:S(2)}, u32[]{:S(2)}) collective-permute-start(bf16[272,256]{1,0:T(8,128)(2,1)S(1)} %get-tuple-element.173), channel_id=1, source_target_pairs={{0,1},{1,0},{2,3},{3,2},{4,5},{5,4},{6,7},{7,6},{8,9},{9,8},{10,11... | collective-permute-start | bytes 417800 | tf_op jit(solution)/shard_map/gbu_z1/ppermute | solution.py:32
  362.5 21.8 %collective-permute-start.64 = (bf16[128,3456]{1,0:T(8,128)(2,1)S(1)}, bf16[128,3456]{1,0:T(8,128)(2,1)S(1)}, u32[]{:S(2)}, u32[]{:S(2)}) collective-permute-start(bf16[128,3456]{1,0:T(8,128)(2,1)S(1)} %copy-done.25), channel_id=1, source_target_pairs={{0,24},{4,28},{8,16},{12,20},{16,8},{20,12},{24,0},{28,4},{1,25},{... | collective-permute-start | bytes 2654216 | tf_op jit(solution)/shard_map/gf_dp6/ppermute | solution.py:20
  (38 other events, 534.6 us)
